TPU v7x, 256 devices: a whole 4x4x8 slice. The times are simulated.
256 devices in a mesh: half: 2 (over core), cls: 128 (over x, y, z).
Axes of the slice: x: 4, y: 4, z: 8, core: 2. Of those that a mesh axis runs over, the one named last changes fastest.
Arguments:
- particles: bfloat16 [2, 8192, 128, 128], P('half', 'cls'), may hold values from -6 to 6
- assign: int32 [2, 8192], P('half', 'cls'), may hold values from 0 to 127, as said below
- rotation: int32 [2, 8192], P('half', 'cls'), may hold values from 0 to 35
- group: int32 [2, 8192], P('half', 'cls'), may hold values from 0 to 255
- ctf: float32 [256, 64], replicated, may hold values from -1 to 1
Outputs:
- class_avg: bfloat16 [2, 128, 128, 128], P('half', 'cls')
- residual: bfloat16 [2, 8192, 128, 128], P('half', 'cls')
- scores: bfloat16 [2, 8192, 36], P('half', 'cls')
- leverage: bfloat16 [2, 8192], P('half', 'cls')
Inputs may be any that keep to these rules, and one draw needn't show every extreme that they name: `assign`: among the 64 particles of one device no class appears more than 2 times, and one class appears exactly 2 times among every device's particles.
All inputs are finite; a program needn't handle non-finite values.
Results may differ from a plain program's by a relative error of at most 0.0065.
Values may be sent and summed in bfloat16 or wider, within the bound.
No kernel may reach another device: no remote copies, remote signals or barrier semaphores. Data moves between devices by JAX's collectives and lax.ppermute only.
A program may use at most 128 MiB of HBM per device.

v0:
```python
import math

import jax
import jax.numpy as jnp
from jax import lax
from jax.sharding import PartitionSpec as P

NROT = 36


wiener_tau = 1.0


def partner_2(value, axis, stride):
    mask = 2**stride
    pairs = [(source, source ^ mask) for source in range(lax.axis_size(axis))]
    return lax.ppermute(value, axis, pairs)


def rotation_table(angles):
    turns = jnp.arange(NROT, dtype=jnp.int32)[:, None, None]
    source = jnp.arange(angles, dtype=jnp.int32)[None, :, None]
    target = jnp.arange(angles, dtype=jnp.int32)[None, None, :]
    offset = turns * angles // NROT
    fraction = (turns * angles % NROT).astype(jnp.float32) / NROT
    primary = (source == (target - offset) % angles).astype(jnp.float32)
    neighbor = (source == (target - offset - 1) % angles).astype(jnp.float32)
    return ((1.0 - fraction) * primary + fraction * neighbor).astype(jnp.bfloat16)


def cycle_weights(ctf_table, group_ids, live):
    weights = ctf_table[group_ids] * live[:, None]
    return (weights, jnp.concatenate([weights, weights], axis=1))


def rotation_scores(images, predicted, table):
    cross = jnp.einsum("sra,srb->sab", images, predicted, preferred_element_type=jnp.float32)
    raw = jnp.einsum(
        "sab,tab->st", cross, table.astype(jnp.float32), precision=lax.Precision.HIGHEST
    )
    pixels = images.shape[1] * images.shape[2]
    first = jnp.sqrt(jnp.mean(jnp.square(images.astype(jnp.float32)), axis=(1, 2)) + 1e-05)
    second = jnp.sqrt(jnp.mean(jnp.square(predicted.astype(jnp.float32)), axis=(1, 2)) + 1e-05)
    return raw / (math.sqrt(pixels) * first * second)[:, None]


def body(particles, assign, rotation, group, ctf):
    images = particles[0]
    classes = assign[0]
    turns = rotation[0]
    groups = group[0]
    count, rows, angles = images.shape
    owners = lax.axis_size("cls")
    table = rotation_table(angles)
    capacity = max(2, 2 * count // owners)
    marks = (classes[:, None] == jnp.arange(owners, dtype=jnp.int32)[None, :]).astype(jnp.int32)
    before = jnp.cumsum(marks, axis=0) - marks
    places = classes * capacity + jnp.sum(before * marks, axis=1)
    outgoing = jnp.zeros((owners * capacity, rows, angles), jnp.bfloat16).at[places].set(images)
    codes = jnp.zeros((owners * capacity,), jnp.int32).at[places].set(groups * NROT + turns + 1)
    arrived, arrived_codes = (
        lax.all_to_all(
            outgoing.reshape(owners, capacity, rows, angles),
            "cls",
            split_axis=0,
            concat_axis=0,
            tiled=True,
        ),
        lax.all_to_all(
            codes.reshape(owners, capacity), "cls", split_axis=0, concat_axis=0, tiled=True
        ),
    )
    slot_images = arrived.reshape(owners * capacity, rows, angles)
    slot_codes = arrived_codes.reshape(owners * capacity)
    live = (slot_codes > 0).astype(jnp.float32)
    lowered = jnp.maximum(slot_codes - 1, 0)
    weights, stacked = cycle_weights(ctf, lowered // NROT, live)
    aligned = jnp.einsum(
        "srb,sba->sra", slot_images, table[lowered % NROT], preferred_element_type=jnp.float32
    )
    class_sum = jnp.sum(stacked[:, :, None] * aligned, axis=0)
    weight_sum = jnp.sum(weights * weights, axis=0)
    denom = jnp.concatenate([weight_sum, weight_sum])[:, None] + wiener_tau
    average = (class_sum / denom).astype(jnp.bfloat16)
    partner = partner_2(average, "half", 0)
    predicted = (stacked[:, :, None] * partner.astype(jnp.float32)).astype(jnp.bfloat16)
    residual = (aligned - predicted).astype(jnp.bfloat16)
    scores = rotation_scores(slot_images, predicted, table).astype(jnp.bfloat16)
    leverage = jnp.mean(weights * weights / (weight_sum[None, :] + wiener_tau), axis=1).astype(
        jnp.bfloat16
    )
    back_resid, back_scores, back_lever = (
        lax.all_to_all(
            residual.reshape(owners, capacity, rows, angles),
            "cls",
            split_axis=0,
            concat_axis=0,
            tiled=True,
        ),
        lax.all_to_all(
            scores.reshape(owners, capacity, NROT), "cls", split_axis=0, concat_axis=0, tiled=True
        ),
        lax.all_to_all(
            leverage.reshape(owners, capacity), "cls", split_axis=0, concat_axis=0, tiled=True
        ),
    )
    residual = back_resid.reshape(owners * capacity, rows, angles)[places]
    scores = back_scores.reshape(owners * capacity, NROT)[places]
    leverage = back_lever.reshape(owners * capacity)[places]
    return (average[None, None], residual[None], scores[None], leverage[None])


def solution(mesh):
    in_specs = (
        P("half", "cls", None, None),
        P("half", "cls"),
        P("half", "cls"),
        P("half", "cls"),
        P(),
    )
    out_specs = (
        P("half", "cls", None, None),
        P("half", "cls", None, None),
        P("half", "cls", None),
        P("half", "cls"),
    )
    return jax.shard_map(body, mesh=mesh, in_specs=in_specs, out_specs=out_specs, check_vma=False)
```

profile of v0, /device:TPU:1, one launch (start us, length us, event | category | flops | bytes accessed | tf_op | source)
XLA Modules:
  0.0 559.5 jit_solution(8362141544646513996)
XLA Ops:
  0.6 0.9 fusion.25
  1.6 0.8 select_reduce_fusion
  3.8 0.8 scatter_custom_fusion
  4.6 0.8 all_to_all.19
  5.3 16.3 %all-to-all-start = ((s32[128,1,2]{2,1,0:T(1,128)}), s32[128,1,2]{2,1,0:T(1,128)S(1)}, u32[]{:S(2)}, u32[]{:S(2)}) async-start(s32[128,1,2]{2,1,0:T(1,128)} %bitcast.5), calls=%async_computation | async-start | bytes 131072 | tf_op jit(solution)/shard_map/all_to_all | solution.py:69
  21.7 5.3 broadcast_in_dim.8
  27.0 8.6 %scatter_fusion = bf16[256,128,128]{2,1,0:T(8,128)(2,1)} fusion(bf16[256,128,128]{2,1,0:T(8,128)(2,1)} %broadcast_in_dim.8, s32[64]{0:T(128)S(1)} %fusion.33, bf16[64,128,128]{2,1,0:T(8,128)(2,1)S(1)} %bitcast.41), kind=kCustom, calls=%fused_computation.6 | custom fusion | bytes 6291712 | tf_op jit(solution)/shard_map/scatter | solution.py:59
  35.6 14.0 %all-to-all-start.1 = ((bf16[128,2,128,128]{3,2,1,0:T(8,128)(2,1)}), bf16[128,2,128,128]{3,2,1,0:T(8,128)(2,1)}, u32[]{:S(2)}, u32[]{:S(2)}) async-start(bf16[128,2,128,128]{3,2,1,0:T(8,128)(2,1)} %bitcast.39), calls=%async_computation.1 | async-start | bytes 16777216 | tf_op jit(solution)/shard_map/all_to_all | solution.py:62
  52.3 0.7 gather_fusion
  53.3 0.8 convert_element_type.96
  54.1 8.4 %gather_fusion.1 = bf16[256,128,128]{2,1,0:T(8,128)(2,1)} fusion(bf16[36,128,128]{2,1,0:T(8,128)(2,1)S(1)} %add_convert_fusion, s32[1024]{0:T(1024)S(1)} %pad_clamp_fusion.1), kind=kCustom, calls=%fused_computation.1 | custom fusion | bytes 16778240 | tf_op jit(solution)/shard_map/gather | solution.py:79
  62.6 170.4 %all-to-all-done.1 = bf16[128,2,128,128]{3,2,1,0:T(8,128)(2,1)} async-done(((bf16[128,2,128,128]{3,2,1,0:T(8,128)(2,1)}), bf16[128,2,128,128]{3,2,1,0:T(8,128)(2,1)}, u32[]{:S(2)}, u32[]{:S(2)}) %all-to-all-start.1) | async-done | bytes 8388640 | tf_op jit(solution)/shard_map/all_to_all | solution.py:62
  233.0 8.8 %all-to-all-start.4 = ((bf16[128,1,2]{2,1,0:T(2,128)(2,1)}), bf16[128,1,2]{2,1,0:T(2,128)(2,1)S(1)}, u32[]{:S(2)}, u32[]{:S(2)}) async-start(bf16[128,1,2]{2,1,0:T(2,128)(2,1)} %convert_element_type.96), calls=%async_computation.4 | async-start | bytes 131072 | tf_op jit(solution)/shard_map/all_to_all | solution.py:103
  241.8 14.6 %multiply_reduce_fusion.1 = (f32[128,128]{1,0:T(8,128)S(1)}, f32[256,128,128]{2,1,0:T(8,128)}) fusion(f32[256,128]{1,0:T(8,128)S(1)} %pad_maximum_fusion, bf16[256,128,128]{2,1,0:T(8,128)(2,1)} %bitcast.9, bf16[256,128,128]{2,1,0:T(8,128)(2,1)} %gather_fusion.1), kind=kOutput, calls=%fused_computation.15 | convolution fusion | flops 1082114048 | bytes 33751040 | tf_op jit(solution)/shard_map/srb,sba->sra/dot_general | solution.py:78
  256.5 2.6 collective-permute-start
  259.1 5.3 multiply_reduce_fusion
  264.6 15.4 %fusion.4 = f32[256,128,128]{2,1,0:T(8,128)} fusion(bf16[256,128,128]{2,1,0:T(8,128)(2,1)} %bitcast.9, f32[128,128]{1,0:T(8,128)S(1)} %convert_element_type.87, f32[256,128]{1,0:T(8,128)S(1)} %pad_maximum_fusion), kind=kOutput, calls=%fused_computation.16 | convolution fusion | flops 1082130432 | bytes 25362432 | tf_op jit(solution)/shard_map/sra,srb->sab/dot_general | solution.py:37
  280.0 31.4 %fusion.1 = (f32[256]{0:T(256)S(1)}, bf16[256,128,128]{2,1,0:T(8,128)(2,1)}) fusion(f32[128,128]{1,0:T(8,128)S(1)} %convert_element_type.87, f32[256,128]{1,0:T(8,128)S(1)} %pad_maximum_fusion, f32[256,128,128]{2,1,0:T(8,128)S(1)} %copy-done), kind=kLoop, calls=%fused_computation.10 | loop fusion | flops 29359872 | bytes 25363456 | tf_op jit(solution)/shard_map/reduce_sum | solution.py:43
  311.3 24.7 %fusion.18 = bf16[256,36]{0,1:T(8,128)(2,1)S(1)} fusion(bf16[36,128,128]{2,1,0:T(8,128)(2,1)S(1)} %add_convert_fusion, f32[256,128,128]{2,1,0:T(8,128)} %fusion.4, f32[256]{0:T(256)S(1)} %sqrt_multiply_fusion.1), kind=kOutput, calls=%fused_computation.25 | convolution fusion | flops 1811957760 | bytes 17976320 | tf_op jit(solution)/shard_map/sab,tab->st/dot_general | solution.py:38
  336.2 23.9 %all_to_all.30 = bf16[128,2,36]{2,1,0:T(2,128)(2,1)S(1)} all-to-all(bf16[128,2,36]{2,1,0:T(2,128)(2,1)S(1)} %bitcast.44), channel_id=1, replica_groups=mesh['half'=2,'cls'=128] {'cls'}, dimensions={0} | all-to-all | bytes 36864 | tf_op jit(solution)/shard_map/all_to_all | solution.py:100
  360.1 7.5 %all-to-all-start.2 = ((bf16[128,2,128,128]{3,2,1,0:T(8,128)(2,1)}), bf16[128,2,128,128]{3,2,1,0:T(8,128)(2,1)}, u32[]{:S(2)}, u32[]{:S(2)}) async-start(bf16[128,2,128,128]{3,2,1,0:T(8,128)(2,1)} %bitcast.40), calls=%async_computation.2 | async-start | bytes 16777216 | tf_op jit(solution)/shard_map/all_to_all | solution.py:93
  367.9 1.3 gather_fusion.4
  371.3 182.3 %all-to-all-done.2 = bf16[128,2,128,128]{3,2,1,0:T(8,128)(2,1)} async-done(((bf16[128,2,128,128]{3,2,1,0:T(8,128)(2,1)}), bf16[128,2,128,128]{3,2,1,0:T(8,128)(2,1)}, u32[]{:S(2)}, u32[]{:S(2)}) %all-to-all-start.2) | async-done | bytes 8388640 | tf_op jit(solution)/shard_map/all_to_all | solution.py:93
  553.6 5.5 gather_fusion.2
  (45 shorter events, 7.3 us)
Async XLA Ops:
  0.6 26.4 %copy-start.1 = (bf16[1,64,128,128]{3,2,1,0:T(8,128)(2,1)S(1)}, bf16[1,64,128,128]{3,2,1,0:T(8,128)(2,1)}, u32[]{:S(2)}) copy-start(bf16[1,64,128,128]{3,2,1,0:T(8,128)(2,1)} %param.5) | copy-start | bytes 6291460
  5.3 30.3 %all-to-all-start = ((s32[128,1,2]{2,1,0:T(1,128)}), s32[128,1,2]{2,1,0:T(1,128)S(1)}, u32[]{:S(2)}, u32[]{:S(2)}) async-start(s32[128,1,2]{2,1,0:T(1,128)} %bitcast.5), calls=%async_computation | async-start | bytes 131072 | tf_op jit(solution)/shard_map/all_to_all | solution.py:69
  35.6 14.0 %copy-start.2 = (f32[256,64]{0,1:T(8,128)S(1)}, f32[256,64]{0,1:T(8,128)}, u32[]{:S(2)}) copy-start(f32[256,64]{0,1:T(8,128)} %param.9) | copy-start | bytes 196612
  35.6 197.4 %all-to-all-start.1 = ((bf16[128,2,128,128]{3,2,1,0:T(8,128)(2,1)}), bf16[128,2,128,128]{3,2,1,0:T(8,128)(2,1)}, u32[]{:S(2)}, u32[]{:S(2)}) async-start(bf16[128,2,128,128]{3,2,1,0:T(8,128)(2,1)} %bitcast.39), calls=%async_computation.1 | async-start | bytes 16777216 | tf_op jit(solution)/shard_map/all_to_all | solution.py:62
  233.0 103.1 %all-to-all-start.4 = ((bf16[128,1,2]{2,1,0:T(2,128)(2,1)}), bf16[128,1,2]{2,1,0:T(2,128)(2,1)S(1)}, u32[]{:S(2)}, u32[]{:S(2)}) async-start(bf16[128,1,2]{2,1,0:T(2,128)(2,1)} %convert_element_type.96), calls=%async_computation.4 | async-start | bytes 131072 | tf_op jit(solution)/shard_map/all_to_all | solution.py:103
  256.5 8.1 %collective-permute-start = (bf16[128,128]{1,0:T(8,128)(2,1)S(1)}, bf16[128,128]{1,0:T(8,128)(2,1)S(1)}, u32[]{:S(2)}, u32[]{:S(2)}) collective-permute-start(bf16[128,128]{1,0:T(8,128)(2,1)S(1)} %divide_convert_fusion), channel_id=1, source_target_pairs={{0,128},{128,0},{1,129},{129,1},{2,130},{130,2},{3,131},{131,3},{4... | collective-permute-start | bytes 98312 | tf_op jit(solution)/shard_map/ppermute | solution.py:17
  264.6 15.4 %copy-start = (f32[256,128,128]{2,1,0:T(8,128)S(1)}, f32[256,128,128]{2,1,0:T(8,128)}, u32[]{:S(2)}) copy-start(f32[256,128,128]{2,1,0:T(8,128)} %get-tuple-element.35) | copy-start | bytes 50331652
  360.1 193.5 %all-to-all-start.2 = ((bf16[128,2,128,128]{3,2,1,0:T(8,128)(2,1)}), bf16[128,2,128,128]{3,2,1,0:T(8,128)(2,1)}, u32[]{:S(2)}, u32[]{:S(2)}) async-start(bf16[128,2,128,128]{3,2,1,0:T(8,128)(2,1)} %bitcast.40), calls=%async_computation.2 | async-start | bytes 16777216 | tf_op jit(solution)/shard_map/all_to_all | solution.py:93
where the time goes:
time: 570 us; the launch traced here: 560 us
  waiting for transfers between devices  353 us (62%)
  matrix products  54.6 us (10%)
  starting transfers between devices  49.1 us (9%)
  other arithmetic  43.3 us (8%)
  local copies, waits for them, and re-layouts  34.6 us (6%)
  blocking collectives  23.9 us (4%)
    all_to_all x1, waiting for transfers between devices, body(): lax.all_to_all(residual.reshape(owners, capacity, rows, angles), 'cls', s...  182 us
    all_to_all x1, waiting for transfers between devices, body(): lax.all_to_all(outgoing.reshape(owners, capacity, rows, angles), 'cls', s...  170 us
    reduce_sum x1, other arithmetic, rotation_scores(): jnp.mean(jnp.square(predicted.astype(jnp.float32)), axis=(1, 2)) + 1e-05  31.4 us
    dot_general x1, matrix products, rotation_scores(): jnp.einsum('sab,tab->st', cross, table.astype(jnp.float32), precision=lax...  24.7 us
    all_to_all x1, blocking collectives, body(): lax.all_to_all(scores.reshape(owners, capacity, NROT), 'cls', split_axis=...  23.9 us
    all_to_all x1, starting transfers between devices, body(): lax.all_to_all(codes.reshape(owners, capacity), 'cls', split_axis=0, conc...  16.3 us
    dot_general x1, matrix products, rotation_scores(): jnp.einsum('sra,srb->sab', images, predicted, preferred_element_type=jnp....  15.4 us
    dot_general x1, matrix products, body(): jnp.einsum('srb,sba->sra', slot_images, table[lowered % NROT], preferred_...  14.6 us
  transfers between devices with their start and end apart: 5, of which 2 were waited for; matrix products, arithmetic and copies ran while one was open for 22% of the time, Pallas kernels for 0%

commit v1 on v0

v1 whole, which is shorter than its diff:
```python
import math

import jax
import jax.numpy as jnp
import numpy as np
from jax import lax
from jax.experimental import pallas as pl
from jax.experimental.pallas import tpu as pltpu
from jax.sharding import PartitionSpec as P

NROT = 36
TAU = 1.0
PLANE = 16
DEPTH = 8
CLASSES = PLANE * DEPTH
ROWS = 128
LANES = 128
BAND = DEPTH * ROWS + 16
SLAB = ROWS + 16
HIGH = lax.Precision.HIGHEST
F32 = jnp.float32
BF16 = jnp.bfloat16


def rotation_steps():
    turns = np.arange(NROT)
    offset = turns * LANES // NROT
    fraction = ((turns * LANES) % NROT).astype(np.float32) / np.float32(NROT)
    keep = (np.float32(1.0) - fraction).astype(BF16).astype(np.float32)
    carry = fraction.astype(BF16).astype(np.float32)
    return offset.astype(np.int32), np.stack([keep, carry])


def lag_matrix():
    offset, parts = rotation_steps()
    out = np.zeros((LANES, LANES), np.float32)
    for r in range(NROT):
        out[offset[r] % LANES, r] += parts[0, r]
        out[(offset[r] + 1) % LANES, r] += parts[1, r]
    return out


def weights_by_shell(group_row, ctf):
    groups = ctf.shape[0]
    count = group_row.shape[1]
    pick = (lax.broadcasted_iota(jnp.int32, (groups, count), 0) == group_row).astype(F32)
    return lax.dot_general(ctf, pick, (((0,), (0,)), ((), ())), precision=HIGH, preferred_element_type=F32)


def split_pair(value):
    high = value.astype(BF16).astype(F32)
    return high, value - high


def align(image, turn, offset_ref, part_ref):
    first = pltpu.roll(image, offset_ref[turn], 1)
    second = pltpu.roll(first, 1, 1)
    return part_ref[0, turn] * first + part_ref[1, turn] * second


def sums_kernel(
    assign_ref, turn_ref, offset_ref, part_ref, images_ref, assign_row, group_row, ctf_ref, out_ref, spread, dens, slots
):
    plane = pl.program_id(0)
    count = images_ref.shape[0]
    shells = ROWS // 2

    @pl.when(plane == 0)
    def _():
        by_shell = weights_by_shell(group_row[...], ctf_ref[...])
        for i in range(count):
            spread[i] = jnp.broadcast_to(by_shell[:, i : i + 1], (shells, LANES))
        member = (lax.broadcasted_iota(jnp.int32, (CLASSES, count), 0) == assign_row[...]).astype(F32)
        square = jnp.transpose(by_shell * by_shell)
        den = lax.dot_general(member, square, (((1,), (0,)), ((), ())), precision=HIGH, preferred_element_type=F32)
        dens[...] = jnp.concatenate(split_pair(den), axis=1)

        def clear(c, _):
            slots[0, c] = -1
            slots[1, c] = -1
            return 0

        lax.fori_loop(0, CLASSES, clear, 0)

        def place(i, _):
            c = assign_ref[i]
            held = slots[0, c]
            slots[1, c] = jnp.where(held >= 0, i, -1)
            slots[0, c] = jnp.where(held >= 0, held, i)
            return 0

        lax.fori_loop(0, count, place, 0)

    def weighted(i):
        image = images_ref[i].astype(F32)
        turned = align(image, turn_ref[i], offset_ref, part_ref)
        w = spread[i]
        return jnp.concatenate([w * turned[:shells], w * turned[shells:]], axis=0)

    def one(z, _):
        c = plane * DEPTH + z
        a = slots[0, c]
        b = slots[1, c]
        at = pl.multiple_of(z * ROWS, ROWS)

        @pl.when(a < 0)
        def _():
            out_ref[0, pl.ds(at, ROWS), :] = jnp.zeros((ROWS, LANES), BF16)

        @pl.when((a >= 0) & (b < 0))
        def _():
            out_ref[0, pl.ds(at, ROWS), :] = weighted(a).astype(BF16)

        @pl.when(b >= 0)
        def _():
            out_ref[0, pl.ds(at, ROWS), :] = (weighted(a) + weighted(b)).astype(BF16)

        return 0

    lax.fori_loop(0, DEPTH, one, 0)
    tile = dens[pl.ds(pl.multiple_of(plane * DEPTH, DEPTH), DEPTH), :]
    out_ref[0, DEPTH * ROWS :, :] = jnp.concatenate([tile, jnp.zeros_like(tile)], axis=0).astype(BF16)


def class_sums(images, classes, turns, groups, ctf):
    count = images.shape[0]
    offset, parts = rotation_steps()
    return pl.pallas_call(
        sums_kernel,
        out_shape=jax.ShapeDtypeStruct((PLANE, BAND, LANES), BF16),
        grid_spec=pltpu.PrefetchScalarGridSpec(
            num_scalar_prefetch=4,
            grid=(PLANE,),
            in_specs=[
                pl.BlockSpec((count, ROWS, LANES), lambda p, *_: (0, 0, 0)),
                pl.BlockSpec((1, count), lambda p, *_: (0, 0)),
                pl.BlockSpec((1, count), lambda p, *_: (0, 0)),
                pl.BlockSpec(ctf.shape, lambda p, *_: (0, 0)),
            ],
            out_specs=pl.BlockSpec((1, BAND, LANES), lambda p, *_: (p, 0, 0)),
            scratch_shapes=[
                pltpu.VMEM((count, ROWS // 2, LANES), F32),
                pltpu.VMEM((CLASSES, LANES), F32),
                pltpu.SMEM((2, CLASSES), jnp.int32),
            ],
        ),
        compiler_params=pltpu.CompilerParams(dimension_semantics=("arbitrary",), vmem_limit_bytes=40 << 20),
        name="class_sums",
    )(classes, turns, jnp.asarray(offset), jnp.asarray(parts), images, classes[None], groups[None], ctf)


def repack_pair(pair):
    total = pair[:, : LANES // 2] + pair[:, LANES // 2 :]
    return jnp.concatenate(split_pair(total), axis=1)


def plane_kernel(band_ref, tail_ref, out_ref):
    z = pl.program_id(0)
    out_ref[0, :ROWS, :] = jnp.sum(band_ref[...].astype(F32), axis=0).astype(BF16)
    tail = repack_pair(jnp.sum(tail_ref[...].astype(F32), axis=0))
    here = lax.broadcasted_iota(jnp.int32, tail.shape, 0) == z
    row = jnp.sum(jnp.where(here, tail, 0.0), axis=0, keepdims=True)
    out_ref[0, ROWS:, :] = jnp.broadcast_to(row, (16, LANES)).astype(BF16)


def plane_sum(bands):
    return pl.pallas_call(
        plane_kernel,
        out_shape=jax.ShapeDtypeStruct((DEPTH, SLAB, LANES), BF16),
        grid=(DEPTH,),
        in_specs=[
            pl.BlockSpec((PLANE, ROWS, LANES), lambda z: (0, z, 0)),
            pl.BlockSpec((PLANE, 16, LANES), lambda z: (0, DEPTH * ROWS // 16, 0)),
        ],
        out_specs=pl.BlockSpec((1, SLAB, LANES), lambda z: (z, 0, 0)),
        compiler_params=pltpu.CompilerParams(dimension_semantics=("arbitrary",), vmem_limit_bytes=24 << 20),
        name="plane_sum",
    )(bands, bands)


def average_kernel(slab_ref, avg_ref, den_ref):
    total = jnp.sum(slab_ref[...].astype(F32), axis=0)
    pair = repack_pair(total[ROWS:])
    den_ref[...] = pair.astype(BF16)
    den = pair[:1, : LANES // 2] + pair[:1, LANES // 2 :]
    column = jnp.transpose(jnp.broadcast_to(jnp.concatenate([den, den], axis=1), (ROWS, LANES)))
    avg_ref[...] = (total[:ROWS] / (column + TAU)).astype(BF16)


def class_average(slabs):
    return pl.pallas_call(
        average_kernel,
        out_shape=(jax.ShapeDtypeStruct((ROWS, LANES), BF16), jax.ShapeDtypeStruct((16, LANES), BF16)),
        compiler_params=pltpu.CompilerParams(vmem_limit_bytes=24 << 20),
        name="class_average",
    )(slabs)


def copies_kernel(avg_ref, den_ref, out_ref):
    out_ref[0, :ROWS, :] = avg_ref[...]
    out_ref[0, ROWS:, :] = den_ref[...]


def depth_copies(avg, den):
    return pl.pallas_call(
        copies_kernel,
        out_shape=jax.ShapeDtypeStruct((DEPTH, SLAB, LANES), BF16),
        grid=(DEPTH,),
        in_specs=[pl.BlockSpec((ROWS, LANES), lambda z: (0, 0)), pl.BlockSpec((16, LANES), lambda z: (0, 0))],
        out_specs=pl.BlockSpec((1, SLAB, LANES), lambda z: (z, 0, 0)),
        compiler_params=pltpu.CompilerParams(dimension_semantics=("arbitrary",)),
        name="depth_copies",
    )(avg, den)


def band_kernel(slab_ref, out_ref):
    rows = []
    for z in range(DEPTH):
        out_ref[0, z * ROWS : (z + 1) * ROWS, :] = slab_ref[z, :ROWS, :]
        rows.append(slab_ref[z, ROWS:, :].astype(F32)[:1])
    tile = jnp.concatenate(rows, axis=0)
    out_ref[0, DEPTH * ROWS :, :] = jnp.concatenate([tile, jnp.zeros_like(tile)], axis=0).astype(BF16)


def plane_copies(slabs):
    return pl.pallas_call(
        band_kernel,
        out_shape=jax.ShapeDtypeStruct((PLANE, BAND, LANES), BF16),
        grid=(PLANE,),
        in_specs=[pl.BlockSpec((DEPTH, SLAB, LANES), lambda p: (0, 0, 0))],
        out_specs=pl.BlockSpec((1, BAND, LANES), lambda p: (p, 0, 0)),
        compiler_params=pltpu.CompilerParams(dimension_semantics=("arbitrary",), vmem_limit_bytes=24 << 20),
        name="plane_copies",
    )(slabs)


BATCH = 8


def outputs_kernel(
    assign_ref, turn_ref, offset_ref, part_ref,
    images_ref, bands_ref, group_row, ctf_ref, lag_ref,
    resid_ref, score_ref, lever_ref,
    spread, dens, lags, powers, energies,
):
    step = pl.program_id(0)
    shells = ROWS // 2
    count = spread.shape[0]

    @pl.when(step == 0)
    def _():
        by_shell = weights_by_shell(group_row[...], ctf_ref[...])
        for i in range(count):
            spread[i] = jnp.broadcast_to(by_shell[:, i : i + 1], (shells, LANES))

    def one(j, _):
        i = step * BATCH + j
        c = assign_ref[i]
        plane = c // DEPTH
        z = c % DEPTH
        image = images_ref[j]
        wide = image.astype(F32)
        turned = align(wide, turn_ref[i], offset_ref, part_ref)
        avg = bands_ref[plane, pl.ds(pl.multiple_of(z * ROWS, ROWS), ROWS), :].astype(F32)
        w = spread[i]
        predicted = jnp.concatenate([w * avg[:shells], w * avg[shells:]], axis=0).astype(BF16)
        back = predicted.astype(F32)
        resid_ref[j] = (turned - back).astype(BF16)
        cross = lax.dot_general(image, predicted, (((0,), (0,)), ((), ())), preferred_element_type=F32)
        lag = cross[:8]
        for r in range(8, LANES, 8):
            lag = lag + pltpu.roll(cross[r : r + 8], LANES - r, 1)
        lags[pl.ds(pl.multiple_of(i * 8, 8), 8), :] = lag
        powers[pl.ds(i, 1), :] = jnp.sum(wide * wide, axis=0, keepdims=True)
        energies[pl.ds(i, 1), :] = jnp.sum(back * back, axis=0, keepdims=True)
        tile = bands_ref[plane, DEPTH * ROWS :, :].astype(F32)
        here = lax.broadcasted_iota(jnp.int32, tile.shape, 0) == z
        dens[pl.ds(i, 1), :] = jnp.sum(jnp.where(here, tile, 0.0), axis=0, keepdims=True)
        return 0

    lax.fori_loop(0, BATCH, one, 0)

    @pl.when(step == pl.num_programs(0) - 1)
    def _():
        lag = lags[pl.ds(0, count, stride=8), :]
        for r in range(1, 8):
            lag = lag + pltpu.roll(lags[pl.ds(r, count, stride=8), :], LANES - r, 1)
        raw = lax.dot_general(
            lag, lag_ref[...], (((1,), (0,)), ((), ())), precision=HIGH, preferred_element_type=F32
        )
        pixels = ROWS * LANES
        first = jnp.sqrt(jnp.sum(powers[...], axis=1, keepdims=True) / pixels + 1e-05)
        second = jnp.sqrt(jnp.sum(energies[...], axis=1, keepdims=True) / pixels + 1e-05)
        score_ref[...] = (raw / (math.sqrt(pixels) * first * second))[:, :NROT].astype(BF16)
        by_shell = weights_by_shell(group_row[...], ctf_ref[...])
        pair = dens[...]
        den = jnp.transpose(pair[:, :shells] + pair[:, shells:])
        lever_ref[...] = (jnp.sum(by_shell * by_shell / (den + TAU), axis=0, keepdims=True) / shells).astype(BF16)


def particle_outputs(images, bands, classes, turns, groups, ctf):
    count = images.shape[0]
    offset, parts = rotation_steps()
    return pl.pallas_call(
        outputs_kernel,
        out_shape=(
            jax.ShapeDtypeStruct(images.shape, BF16),
            jax.ShapeDtypeStruct((count, NROT), BF16),
            jax.ShapeDtypeStruct((1, count), BF16),
        ),
        grid_spec=pltpu.PrefetchScalarGridSpec(
            num_scalar_prefetch=4,
            grid=(count // BATCH,),
            in_specs=[
                pl.BlockSpec((BATCH, ROWS, LANES), lambda s, *_: (s, 0, 0)),
                pl.BlockSpec((PLANE, BAND, LANES), lambda s, *_: (0, 0, 0), pipeline_mode=pl.Buffered(1)),
                pl.BlockSpec((1, count), lambda s, *_: (0, 0)),
                pl.BlockSpec(ctf.shape, lambda s, *_: (0, 0)),
                pl.BlockSpec((LANES, LANES), lambda s, *_: (0, 0)),
            ],
            out_specs=[
                pl.BlockSpec((BATCH, ROWS, LANES), lambda s, *_: (s, 0, 0)),
                pl.BlockSpec((count, NROT), lambda s, *_: (0, 0)),
                pl.BlockSpec((1, count), lambda s, *_: (0, 0)),
            ],
            scratch_shapes=[
                pltpu.VMEM((count, ROWS // 2, LANES), F32),
                pltpu.VMEM((count, LANES), F32),
                pltpu.VMEM((count * 8, LANES), F32),
                pltpu.VMEM((count, LANES), F32),
                pltpu.VMEM((count, LANES), F32),
            ],
        ),
        compiler_params=pltpu.CompilerParams(dimension_semantics=("arbitrary",), vmem_limit_bytes=40 << 20),
        name="particle_outputs",
    )(
        classes, turns, jnp.asarray(offset), jnp.asarray(parts),
        images, bands, groups[None], ctf, jnp.asarray(lag_matrix()),
    )


def exchange(value, groups):
    return lax.all_to_all(value, "cls", split_axis=0, concat_axis=0, tiled=True, axis_index_groups=groups)


def chip_groups():
    ids = np.arange(CLASSES).reshape(PLANE, DEPTH)
    return ids.T.tolist(), ids.tolist()


def body(particles, assign, rotation, group, ctf):
    images = particles[0]
    classes = assign[0]
    turns = rotation[0]
    groups = group[0]
    across, along = chip_groups()
    bands = exchange(class_sums(images, classes, turns, groups, ctf), across)
    slabs = exchange(plane_sum(bands), along)
    average, weight_sum = class_average(slabs)
    partner = lax.ppermute(average, "half", [(0, 1), (1, 0)])
    slabs = exchange(depth_copies(partner, weight_sum), along)
    bands = exchange(plane_copies(slabs), across)
    residual, scores, leverage = particle_outputs(images, bands, classes, turns, groups, ctf)
    return (average[None, None], residual[None], scores[None], leverage)


def solution(mesh):
    in_specs = (
        P("half", "cls", None, None),
        P("half", "cls"),
        P("half", "cls"),
        P("half", "cls"),
        P(),
    )
    out_specs = (
        P("half", "cls", None, None),
        P("half", "cls", None, None),
        P("half", "cls", None),
        P("half", "cls"),
    )
    return jax.shard_map(body, mesh=mesh, in_specs=in_specs, out_specs=out_specs, check_vma=False)
```

time: 570 us -> 201 us (0.35); the launches traced: 560 us -> 201 us
  waiting for transfers between devices: 353 us -> 1.07 us
  blocking collectives: 23.9 us -> 145 us
  matrix products: 54.6 us -> 0 us
  starting transfers between devices: 49.1 us -> 3.86 us
  other arithmetic: 43.3 us -> 0 us
  Pallas kernels: 0 us -> 42.1 us
  local copies, waits for them, and re-layouts: 34.6 us -> 7.75 us
    all_to_all x4 -> x0, waiting for transfers between devices: 353 us -> none  [the longest x1 182 us: body(): lax.all_to_all(residual.reshape(owners, capacity, rows, angles), 'cls', s...]
    all_to_all x1 -> x4, blocking collectives: 23.9 us -> 145 us  [exchange(): lax.all_to_all(value, 'cls', split_axis=0, concat_axis=0, tiled=True, axi...]
    dot_general x3 -> x0, matrix products: 54.6 us -> none  [the longest x1 24.7 us: rotation_scores(): jnp.einsum('sab,tab->st', cross, table.astype(jnp.float32), precision=lax...]
    all_to_all x4 -> x0, starting transfers between devices: 46.6 us -> none  [the longest x1 16.3 us: body(): lax.all_to_all(codes.reshape(owners, capacity), 'cls', split_axis=0, conc...]
    pallas_call x0 -> x6, Pallas kernels: none -> 42.1 us  [the longest x1 19.4 us: particle_outputs(): pl.pallas_call(outputs_kernel, out_shape=(jax.ShapeDtypeStruct(images.sha...]
    reduce_sum x5 -> x0, other arithmetic: 37.8 us -> none  [the longest x1 31.4 us: rotation_scores(): jnp.mean(jnp.square(predicted.astype(jnp.float32)), axis=(1, 2)) + 1e-05]
    gather x5 -> x0, local copies, waits for them, and re-layouts: 16.5 us -> none  [the longest x1 8.35 us: body(): table[lowered % NROT]]
    scatter x2 -> x0, local copies, waits for them, and re-layouts: 9.38 us -> none  [the longest x1 8.61 us: body(): jnp.zeros((owners * capacity, rows, angles), jnp.bfloat16).at[places]]
  transfers between devices with their start and end apart: 5 -> 1, of which waited for: 2 -> 1; matrix products, arithmetic and copies ran while one was open for 22% -> 0% of each run, Pallas kernels for 0% -> 0%
where the time goes in v1:
time: 201 us
  blocking collectives  145 us (72%)
  Pallas kernels  42.1 us (21%)
  local copies, waits for them, and re-layouts  7.75 us (4%)
  starting transfers between devices  3.86 us (2%)
    all_to_all x4, blocking collectives, exchange(): lax.all_to_all(value, 'cls', split_axis=0, concat_axis=0, tiled=True, axi...  145 us
    pallas_call x1, Pallas kernels, particle_outputs(): pl.pallas_call(outputs_kernel, out_shape=(jax.ShapeDtypeStruct(images.sha...  19.4 us
    pallas_call x1, Pallas kernels, class_sums(): pl.pallas_call(sums_kernel, out_shape=jax.ShapeDtypeStruct((PLANE, BAND,...  15.5 us
    unnamed x32, local copies, waits for them, and re-layouts  7.75 us
  transfers between devices with their start and end apart: 1, of which 1 were waited for; matrix products, arithmetic and copies ran while one was open for 0% of the time, Pallas kernels for 0%

profile of v1, /device:TPU:1, one launch (start us, length us, event | category | flops | bytes accessed | tf_op | source)
XLA Modules:
  0.0 200.6 jit_solution(12024859018281284994)
XLA Ops:
  0.6 0.9 copy.14.ctf_ref
  1.6 1.6 copy-done
  3.2 0.7 copy-done.3
  3.8 0.7 copy-done.6
  4.5 0.7 copy-done.8
  5.2 0.7 copy-done.10
  5.8 0.7 copy-done.12
  6.5 15.5 %class_sums.1 = bf16[16,1040,128]{2,1,0:T(8,128)(2,1)S(1)} custom-call(s32[64]{0:T(128)S(1)} %bitcast.9, s32[64]{0:T(128)S(1)} %bitcast.11, s32[36]{0:T(128)S(1)} %copy-done.12, f32[2,36]{1,0:T(2,128)S(1)} %copy-done.6, bf16[64,128,128]{2,1,0:T(8,128)(2,1)S(1)} %bitcast.6, s32[1,64]{1,0:T(1,128)S(1)} %copy-done.3, s32[1,64]{1,0:T(1,128)S(1)} %copy-done.10, ...), custom_call_target="tpu_custom_call" | custom-call | tf_op jit(solution)/shard_map/class_sums/pallas_call | solution.py:128
  22.0 58.4 %all_to_all.20.band_ref.tail_ref = bf16[16,1040,128]{2,1,0:T(8,128)(2,1)S(1)} all-to-all(bf16[16,1040,128]{2,1,0:T(8,128)(2,1)S(1)} %class_sums.1), channel_id=1, replica_groups={{0,8,16,24,32,40,48,56,64,72,80,88,96,104,112,120},{1,9,17,25,33,41,49,..., dimensions={0} | all-to-all | bytes 8519680 | tf_op jit(solution)/shard_map/all_to_all | solution.py:343
  80.4 2.4 %plane_sum.1 = bf16[8,144,128]{2,1,0:T(8,128)(2,1)S(1)} custom-call(bf16[16,1040,128]{2,1,0:T(8,128)(2,1)S(1)} %all_to_all.20.band_ref.tail_ref, bf16[16,1040,128]{2,1,0:T(8,128)(2,1)S(1)} %all_to_all.20.band_ref.tail_ref), custom_call_target="tpu_custom_call" | custom-call | tf_op jit(solution)/shard_map/plane_sum/pallas_call | solution.py:167
  82.8 17.4 %all_to_all.21.slab_ref = bf16[8,144,128]{2,1,0:T(8,128)(2,1)S(1)} all-to-all(bf16[8,144,128]{2,1,0:T(8,128)(2,1)S(1)} %plane_sum.1), channel_id=1, replica_groups={{0,1,2,3,4,5,6,7},{8,9,10,11,12,13,14,15},{16,17,18,19,20,21,22,23},{24..., dimensions={0} | all-to-all | bytes 589824 | tf_op jit(solution)/shard_map/all_to_all | solution.py:343
  100.2 1.0 class_average.1
  101.3 0.6 copy-done.5
  101.8 3.9 %collective-permute-start = (bf16[128,128]{1,0:T(8,128)(2,1)}, bf16[128,128]{1,0:T(8,128)(2,1)S(1)}, u32[]{:S(2)}, u32[]{:S(2)}) collective-permute-start(bf16[128,128]{1,0:T(8,128)(2,1)} %get-tuple-element.9), channel_id=1, source_target_pairs={{0,128},{128,0},{1,129},{129,1},{2,130},{130,2},{3,131},{131,3},{4... | collective-permute-start | bytes 98312 | tf_op jit(solution)/shard_map/ppermute | solution.py:360
  105.7 1.1 collective-permute-done.avg_ref
  106.8 0.6 copy-done.14
  107.4 3.2 %depth_copies.1 = bf16[8,144,128]{2,1,0:T(8,128)(2,1)} custom-call(bf16[128,128]{1,0:T(8,128)(2,1)} %copy-done.14, bf16[16,128]{1,0:T(8,128)(2,1)} %copy-done.5), custom_call_target="tpu_custom_call" | custom-call | tf_op jit(solution)/shard_map/depth_copies/pallas_call | solution.py:205
  110.6 16.0 %all_to_all.22.slab_ref = bf16[8,144,128]{2,1,0:T(8,128)(2,1)S(1)} all-to-all(bf16[8,144,128]{2,1,0:T(8,128)(2,1)} %depth_copies.1), channel_id=1, replica_groups={{0,1,2,3,4,5,6,7},{8,9,10,11,12,13,14,15},{16,17,18,19,20,21,22,23},{24..., dimensions={0} | all-to-all | bytes 589824 | tf_op jit(solution)/shard_map/all_to_all | solution.py:343
  126.6 0.5 plane_copies.1
  127.2 0.0 copy-start.2
  127.2 0.0 copy-start.7
  127.2 53.2 %all_to_all.23.bands_ref = bf16[16,1040,128]{2,1,0:T(8,128)(2,1)S(1)} all-to-all(bf16[16,1040,128]{2,1,0:T(8,128)(2,1)S(1)} %plane_copies.1), channel_id=1, replica_groups={{0,8,16,24,32,40,48,56,64,72,80,88,96,104,112,120},{1,9,17,25,33,41,49,..., dimensions={0} | all-to-all | bytes 8519680 | tf_op jit(solution)/shard_map/all_to_all | solution.py:343
  180.5 19.4 %particle_outputs.1 = (bf16[64,128,128]{2,1,0:T(8,128)(2,1)}, bf16[64,36]{1,0:T(8,128)(2,1)S(1)}, bf16[1,64]{1,0:T(2,128)(2,1)}) custom-call(s32[64]{0:T(128)S(1)} %bitcast.10, s32[64]{0:T(128)S(1)} %bitcast.12, s32[36]{0:T(128)S(1)} %copy-done.13, f32[2,36]{1,0:T(2,128)S(1)} %copy-done.7, bf16[64,128,128]{2,1,0:T(8,128)(2,1)S(1)} %bitcast.7, ...), custom_call_target="tpu_custom_call" | custom-call | tf_op jit(solution)/shard_map/particle_outputs/pallas_call | solution.py:304
  199.9 0.7 copy.16
  (20 shorter events, 0.1 us)
Async XLA Ops:
  1.6 1.6 copy-start
  3.2 0.7 copy-start.3
  3.8 0.7 copy-start.6
  4.5 0.7 copy-start.8
  5.2 0.7 copy-start.10
  5.8 0.7 copy-start.12
  101.3 0.6 copy-start.5
  101.8 4.9 %collective-permute-start = (bf16[128,128]{1,0:T(8,128)(2,1)}, bf16[128,128]{1,0:T(8,128)(2,1)S(1)}, u32[]{:S(2)}, u32[]{:S(2)}) collective-permute-start(bf16[128,128]{1,0:T(8,128)(2,1)} %get-tuple-element.9), channel_id=1, source_target_pairs={{0,128},{128,0},{1,129},{129,1},{2,130},{130,2},{3,131},{131,3},{4... | collective-permute-start | bytes 98312 | tf_op jit(solution)/shard_map/ppermute | solution.py:360
  106.8 0.6 copy-start.14
  127.1 53.3 %copy-start.1 = (bf16[1,64,128,128]{3,2,1,0:T(8,128)(2,1)S(1)}, bf16[1,64,128,128]{3,2,1,0:T(8,128)(2,1)}, u32[]{:S(2)}) copy-start(bf16[1,64,128,128]{3,2,1,0:T(8,128)(2,1)} %param.10) | copy-start | bytes 6291460
  127.2 53.3 %copy-start.2 = (f32[128,128]{1,0:T(8,128)S(1)}, f32[128,128]{1,0:T(8,128)}, u32[]{:S(2)}) copy-start(f32[128,128]{1,0:T(8,128)} %constant.8.clone.lag_ref) | copy-start | bytes 196612
  127.2 53.3 %copy-start.4 = (s32[1,64]{1,0:T(1,128)S(1)}, s32[1,64]{1,0:T(1,128)}, u32[]{:S(2)}) copy-start(s32[1,64]{1,0:T(1,128)} %assign_row.1) | copy-start | bytes 772
  127.2 53.3 %copy-start.7 = (f32[2,36]{1,0:T(2,128)S(1)}, f32[2,36]{1,0:T(2,128)}, u32[]{:S(2)}) copy-start(f32[2,36]{1,0:T(2,128)} %constant.7.clone.part_ref) | copy-start | bytes 868
  127.2 53.3 %copy-start.9 = (s32[1,64]{1,0:T(1,128)S(1)}, s32[1,64]{1,0:T(1,128)}, u32[]{:S(2)}) copy-start(s32[1,64]{1,0:T(1,128)} %param.12) | copy-start | bytes 772
  127.2 53.3 %copy-start.11 = (s32[1,64]{1,0:T(1,128)S(1)}, s32[1,64]{1,0:T(1,128)}, u32[]{:S(2)}) copy-start(s32[1,64]{1,0:T(1,128)} %group_row.3) | copy-start | bytes 772
  127.2 53.3 %copy-start.13 = (s32[36]{0:T(128)S(1)}, s32[36]{0:T(128)}, u32[]{:S(2)}) copy-start(s32[36]{0:T(128)} %constant.6.clone.offset_ref) | copy-start | bytes 436

commit v2 on v0

v2 whole, which is shorter than its diff:
```python
import math

import jax
import jax.numpy as jnp
import numpy as np
from jax import lax
from jax.experimental import pallas as pl
from jax.experimental.pallas import tpu as pltpu
from jax.sharding import PartitionSpec as P

NROT = 36
TAU = 1.0
PLANE = 16
DEPTH = 8
CLASSES = PLANE * DEPTH
LANES = 128
HALF = 64
TAIL = 16
BATCH = 8
HIGH = lax.Precision.HIGHEST
F32 = jnp.float32
BF16 = jnp.bfloat16

HBM = pl.BlockSpec(memory_space=pltpu.HBM)
VMEM = pl.BlockSpec(memory_space=pltpu.VMEM)
SMEM = pl.BlockSpec(memory_space=pltpu.SMEM)


def rotation_steps():
    turns = np.arange(NROT)
    offset = turns * LANES // NROT
    fraction = ((turns * LANES) % NROT).astype(np.float32) / np.float32(NROT)
    keep = (np.float32(1.0) - fraction).astype(BF16).astype(np.float32)
    carry = fraction.astype(BF16).astype(np.float32)
    return offset, keep, carry


def lag_matrix():
    offset, keep, carry = rotation_steps()
    out = np.zeros((LANES, LANES), np.float32)
    for r in range(NROT):
        out[offset[r] % LANES, r] += keep[r]
        out[(offset[r] + 1) % LANES, r] += carry[r]
    return out


def fill_steps(offsets, parts):
    offset, keep, carry = rotation_steps()
    for r in range(NROT):
        offsets[r] = jnp.int32(int(offset[r]))
        parts[0, r] = jnp.float32(float(keep[r]))
        parts[1, r] = jnp.float32(float(carry[r]))


def contract(left, right, dims):
    return lax.dot_general(left, right, (dims, ((), ())), precision=HIGH, preferred_element_type=F32)


def weights_by_shell(group_row, table):
    groups, count = table.shape[1], group_row.shape[1]
    pick = (lax.broadcasted_iota(jnp.int32, (groups, count), 0) == group_row).astype(F32)
    return contract(table, pick, ((1,), (0,)))


def split_pair(value):
    high = value.astype(BF16).astype(F32)
    return jnp.concatenate([high, value - high], axis=1)


def join_pair(pair):
    return pair[:, : LANES // 2] + pair[:, LANES // 2 :]


def align(image, turn, offsets, parts):
    first = pltpu.roll(image, offsets[turn], 1)
    second = pltpu.roll(first, 1, 1)
    return parts[0, turn] * first + parts[1, turn] * second


def keep_columns(by_shell, columns):
    for b in range(columns.shape[0]):
        columns[b, :, :BATCH] = by_shell[:, b * BATCH : (b + 1) * BATCH]


def begin(assign, rotation, group, table, images, chunk, places, sems):
    classes, turns, assign_row, group_row, local, rows = places
    copies = [
        pltpu.make_async_copy(images.at[:, pl.ds(chunk * HALF, HALF), :], rows, sems.at[0]),
        pltpu.make_async_copy(group, group_row, sems.at[1]),
        pltpu.make_async_copy(table, local, sems.at[2]),
        pltpu.make_async_copy(assign, assign_row, sems.at[3]),
        pltpu.make_async_copy(assign, classes, sems.at[4]),
        pltpu.make_async_copy(rotation, turns, sems.at[5]),
    ]
    for copy in copies:
        copy.start()
    return copies


def place_shapes(count, groups):
    return [
        pltpu.SMEM((1, count), jnp.int32),
        pltpu.SMEM((1, count), jnp.int32),
        pltpu.VMEM((1, count), jnp.int32),
        pltpu.VMEM((1, count), jnp.int32),
        pltpu.VMEM((HALF, groups), F32),
        pltpu.VMEM((count, HALF, LANES), BF16),
        pltpu.SMEM((NROT,), jnp.int32),
        pltpu.SMEM((2, NROT), F32),
        pltpu.VMEM((count // BATCH, HALF, LANES), F32),
        pltpu.SemaphoreType.DMA((6,)),
    ]


def sums_kernel(chunk, assign, rotation, group, table, images, out, *scratch):
    places, (offsets, parts, columns, sems) = scratch[:6], scratch[6:10]
    classes, turns, assign_row, group_row, local, rows = places
    count = rows.shape[0]
    copies = begin(assign, rotation, group, table, images, chunk, places, sems)
    fill_steps(offsets, parts)
    for plane in range(PLANE):
        out[plane, : DEPTH * HALF, :] = jnp.zeros((DEPTH * HALF, LANES), BF16)
    for copy in copies:
        copy.wait()
    by_shell = weights_by_shell(group_row[...], local[...])
    keep_columns(by_shell, columns)
    if chunk == 0:
        member = (lax.broadcasted_iota(jnp.int32, (CLASSES, count), 0) == assign_row[...]).astype(F32)
        pair = split_pair(contract(member, jnp.transpose(by_shell * by_shell), ((1,), (0,))))
        for plane in range(PLANE):
            tile = pair[plane * DEPTH : (plane + 1) * DEPTH]
            out[plane, DEPTH * HALF :, :] = jnp.concatenate([tile, jnp.zeros_like(tile)], axis=0).astype(BF16)

    def batch(b, _):
        weights = columns[b]
        for j in range(BATCH):
            i = b * BATCH + j
            c = classes[0, i]
            turned = align(rows[i].astype(F32), turns[0, i], offsets, parts)
            at = pl.ds(pl.multiple_of((c % DEPTH) * HALF, HALF), HALF)
            held = out[c // DEPTH, at, :].astype(F32)
            out[c // DEPTH, at, :] = (held + weights[:, j : j + 1] * turned).astype(BF16)
        return 0

    lax.fori_loop(0, count // BATCH, batch, 0)


def class_sums(chunk, assign, rotation, group, table, images):
    count = images.shape[0]
    band = DEPTH * HALF + (TAIL if chunk == 0 else 0)
    return pl.pallas_call(
        lambda *refs: sums_kernel(chunk, *refs),
        out_shape=jax.ShapeDtypeStruct((PLANE, band, LANES), BF16),
        in_specs=[HBM] * 5,
        out_specs=VMEM,
        scratch_shapes=place_shapes(count, table.shape[1]),
        compiler_params=pltpu.CompilerParams(vmem_limit_bytes=24 << 20),
        cost_estimate=pl.CostEstimate(flops=10**9, transcendentals=0, bytes_accessed=16 << 20),
        name="class_sums_%d" % chunk,
    )(assign, rotation, group, table, images)


def plane_kernel(tailed, here, bands, *outs):
    if tailed:
        tail = jnp.sum(bands[:, DEPTH * HALF :, :].astype(F32), axis=0)
        tail = split_pair(join_pair(tail))
    for j in range(DEPTH):
        z = (here[0] + j) % DEPTH
        at = pl.ds(pl.multiple_of(z * HALF, HALF), HALF)
        total = bands[0, at, :].astype(F32)
        for p in range(1, PLANE):
            total = total + bands[p, at, :].astype(F32)
        outs[j][:HALF, :] = total.astype(BF16)
        if tailed:
            pick = lax.broadcasted_iota(jnp.int32, tail.shape, 0) == z
            row = jnp.sum(jnp.where(pick, tail, 0.0), axis=0, keepdims=True)
            outs[j][HALF:, :] = jnp.broadcast_to(row, (TAIL, LANES)).astype(BF16)


def plane_sums(tailed, here, bands):
    slab = HALF + (TAIL if tailed else 0)
    return pl.pallas_call(
        lambda *refs: plane_kernel(tailed, *refs),
        out_shape=[jax.ShapeDtypeStruct((slab, LANES), BF16)] * DEPTH,
        in_specs=[SMEM, VMEM],
        out_specs=[VMEM] * DEPTH,
        compiler_params=pltpu.CompilerParams(vmem_limit_bytes=24 << 20),
        cost_estimate=pl.CostEstimate(flops=10**7, transcendentals=0, bytes_accessed=4 << 20),
        name="plane_sums",
    )(here, bands)


def average_rows(total, den):
    column = jnp.transpose(jnp.broadcast_to(jnp.concatenate([den, den], axis=1), (LANES, LANES)))[:HALF]
    return (total / (column + TAU)).astype(BF16)


def first_average_kernel(*refs):
    slabs, (avg, tail) = refs[:DEPTH], refs[DEPTH:]
    total = sum(s[...].astype(F32) for s in slabs)
    den = join_pair(total[HALF:])
    tail[...] = split_pair(den).astype(BF16)
    avg[...] = average_rows(total[:HALF], den[:1])


def first_average(slabs):
    return pl.pallas_call(
        first_average_kernel,
        out_shape=(jax.ShapeDtypeStruct((HALF, LANES), BF16), jax.ShapeDtypeStruct((TAIL, LANES), BF16)),
        in_specs=[VMEM] * DEPTH,
        out_specs=(VMEM, VMEM),
        name="first_average",
    )(*slabs)


def second_average_kernel(*refs):
    slabs, (tail, other, avg, packed) = refs[:DEPTH], refs[DEPTH:]
    total = sum(s[...].astype(F32) for s in slabs)
    rows = average_rows(total, join_pair(tail[...].astype(F32))[:1])
    avg[...] = rows
    packed[:HALF, :] = rows
    packed[HALF:, :] = other[...]


def second_average(slabs, tail, other):
    return pl.pallas_call(
        second_average_kernel,
        out_shape=(
            jax.ShapeDtypeStruct((HALF, LANES), BF16),
            jax.ShapeDtypeStruct((HALF + TAIL, LANES), BF16),
        ),
        in_specs=[VMEM] * (DEPTH + 2),
        out_specs=(VMEM, VMEM),
        name="second_average",
    )(*slabs, tail, other)


def copies_kernel(tailed, here, *refs):
    slabs, out = refs[:DEPTH], refs[DEPTH]
    if tailed:
        rank = lax.broadcasted_iota(jnp.int32, (TAIL, LANES), 0)
        tail = jnp.zeros((TAIL, LANES), F32)
    for j in range(DEPTH):
        z = (here[0] + DEPTH - j) % DEPTH
        at = pl.ds(pl.multiple_of(z * HALF, HALF), HALF)
        value = slabs[j][:HALF, :]
        for p in range(PLANE):
            out[p, at, :] = value
        if tailed:
            tail = jnp.where(rank == z, slabs[j][HALF:, :].astype(F32), tail)
    if tailed:
        for p in range(PLANE):
            out[p, DEPTH * HALF :, :] = tail.astype(BF16)


def plane_copies(tailed, here, slabs):
    band = DEPTH * HALF + (TAIL if tailed else 0)
    return pl.pallas_call(
        lambda *refs: copies_kernel(tailed, *refs),
        out_shape=jax.ShapeDtypeStruct((PLANE, band, LANES), BF16),
        in_specs=[SMEM] + [VMEM] * DEPTH,
        out_specs=VMEM,
        compiler_params=pltpu.CompilerParams(vmem_limit_bytes=24 << 20),
        name="plane_copies",
    )(here, *slabs)


def outputs_kernel(chunk, *refs):
    assign, rotation, group, table, images, bands = refs[:6]
    if chunk == 0:
        resid, lags, powers, energies = refs[6:10]
        scratch = refs[10:]
    else:
        lags_before, powers_before, energies_before, lag_ref, _, resid, score, lever = refs[6:14]
        scratch = refs[14:]
        dens, lags, powers, energies = scratch[12:16]
    places, (offsets, parts, columns, sems) = scratch[:6], scratch[6:10]
    held, out_sems = scratch[10:12]
    classes, turns, assign_row, group_row, local, rows = places
    count = rows.shape[0]
    copies = begin(assign, rotation, group, table, images, chunk, places, sems)
    fill_steps(offsets, parts)
    for copy in copies:
        copy.wait()
    by_shell = weights_by_shell(group_row[...], local[...])
    keep_columns(by_shell, columns)

    def leave(b):
        at = pl.ds(pl.multiple_of(b * BATCH, BATCH), BATCH)
        return pltpu.make_async_copy(held.at[at], resid.at[at, pl.ds(chunk * HALF, HALF), :], out_sems.at[b])

    def batch(b, _):
        weights = columns[b]
        for j in range(BATCH):
            i = b * BATCH + j
            c = classes[0, i]
            plane, z = c // DEPTH, c % DEPTH
            image = rows[i]
            wide = image.astype(F32)
            turned = align(wide, turns[0, i], offsets, parts)
            avg = bands[plane, pl.ds(pl.multiple_of(z * HALF, HALF), HALF), :].astype(F32)
            predicted = (weights[:, j : j + 1] * avg).astype(BF16)
            back = predicted.astype(F32)
            held[i] = (turned - back).astype(BF16)
            cross = lax.dot_general(image, predicted, (((0,), (0,)), ((), ())), preferred_element_type=F32)
            lag = cross[:8]
            for r in range(8, LANES, 8):
                lag = lag + pltpu.roll(cross[r : r + 8], LANES - r, 1)
            lags[pl.ds(pl.multiple_of(i * 8, 8), 8), :] = lag
            powers[pl.ds(i, 1), :] = jnp.sum(wide * wide, axis=0, keepdims=True)
            energies[pl.ds(i, 1), :] = jnp.sum(back * back, axis=0, keepdims=True)
            if chunk == 1:
                tile = bands[plane, DEPTH * HALF :, :].astype(F32)
                pick = lax.broadcasted_iota(jnp.int32, tile.shape, 0) == z
                dens[pl.ds(i, 1), :] = jnp.sum(jnp.where(pick, tile, 0.0), axis=0, keepdims=True)
        leave(b).start()
        return 0

    lax.fori_loop(0, count // BATCH, batch, 0)
    if chunk == 1:
        shift = jnp.zeros((count, LANES), F32)
        for r in range(8):
            at = pl.ds(r, count, stride=8)
            part = lags[at, :] + lags_before[at, :]
            shift = shift + (pltpu.roll(part, LANES - r, 1) if r else part)
        raw = contract(lag_ref[...], shift, ((0,), (1,)))
        pixels = 2 * HALF * LANES
        power = jnp.sum(jnp.transpose(powers[...] + powers_before[...]), axis=0, keepdims=True)
        energy = jnp.sum(jnp.transpose(energies[...] + energies_before[...]), axis=0, keepdims=True)
        first = jnp.sqrt(power / pixels + 1e-05)
        second = jnp.sqrt(energy / pixels + 1e-05)
        score[...] = (raw / (math.sqrt(pixels) * first * second))[:NROT].astype(BF16)
        den = jnp.transpose(join_pair(dens[...]))
        lever[...] = (jnp.sum(by_shell * by_shell / (den + TAU), axis=0, keepdims=True) / HALF).astype(BF16)

    def finish(b, _):
        leave(b).wait()
        return 0

    lax.fori_loop(0, count // BATCH, finish, 0)


def output_scratch(count, groups):
    return place_shapes(count, groups) + [
        pltpu.VMEM((count, HALF, LANES), BF16),
        pltpu.SemaphoreType.DMA((count // BATCH,)),
    ]


def first_outputs(assign, rotation, group, table, images, bands):
    count = images.shape[0]
    return pl.pallas_call(
        lambda *refs: outputs_kernel(0, *refs),
        out_shape=(
            jax.ShapeDtypeStruct(images.shape, BF16),
            jax.ShapeDtypeStruct((count * 8, LANES), F32),
            jax.ShapeDtypeStruct((count, LANES), F32),
            jax.ShapeDtypeStruct((count, LANES), F32),
        ),
        in_specs=[HBM] * 5 + [VMEM],
        out_specs=(HBM, VMEM, VMEM, VMEM),
        scratch_shapes=output_scratch(count, table.shape[1]),
        compiler_params=pltpu.CompilerParams(vmem_limit_bytes=24 << 20),
        cost_estimate=pl.CostEstimate(flops=10**9, transcendentals=0, bytes_accessed=32 << 20),
        name="outputs_0",
    )(assign, rotation, group, table, images, bands)


def second_outputs(assign, rotation, group, table, images, bands, before):
    resid, lags, powers, energies = before
    count = images.shape[0]
    rows = pltpu.VMEM((count, LANES), F32)
    return pl.pallas_call(
        lambda *refs: outputs_kernel(1, *refs),
        out_shape=(
            jax.ShapeDtypeStruct(images.shape, BF16),
            jax.ShapeDtypeStruct((NROT, count), BF16),
            jax.ShapeDtypeStruct((1, count), BF16),
        ),
        in_specs=[HBM] * 5 + [VMEM] * 5 + [HBM],
        out_specs=(HBM, VMEM, VMEM),
        scratch_shapes=output_scratch(count, table.shape[1]) + [rows, pltpu.VMEM((count * 8, LANES), F32), rows, rows],
        input_output_aliases={10: 0},
        compiler_params=pltpu.CompilerParams(vmem_limit_bytes=24 << 20),
        cost_estimate=pl.CostEstimate(flops=10**9, transcendentals=0, bytes_accessed=32 << 20),
        name="outputs_1",
    )(assign, rotation, group, table, images, bands, lags, powers, energies, jnp.asarray(lag_matrix()), resid)


def across(value):
    groups = np.arange(CLASSES).reshape(PLANE, DEPTH).T.tolist()
    return lax.all_to_all(value, "cls", split_axis=0, concat_axis=0, tiled=True, axis_index_groups=groups)


def upward(chip, steps):
    return chip // DEPTH * DEPTH + (chip + steps) % DEPTH


def gather_depth(pieces):
    return [pieces[0]] + [
        lax.ppermute(pieces[j], "cls", [(i, upward(i, j)) for i in range(CLASSES)]) for j in range(1, DEPTH)
    ]


def spread_depth(value):
    return [
        lax.ppermute(
            value,
            ("half", "cls"),
            [(h * CLASSES + i, (1 - h) * CLASSES + upward(i, j)) for h in range(2) for i in range(CLASSES)],
        )
        for j in range(DEPTH)
    ]


def body(particles, assign, rotation, group, ctf):
    common = (assign, rotation, group, ctf.T, particles[0])
    here = (lax.axis_index("cls") % DEPTH).astype(jnp.int32).reshape(1)
    bands_a = across(class_sums(0, *common))
    bands_b = across(class_sums(1, *common))
    avg_a, tail = first_average(gather_depth(plane_sums(True, here, bands_a)))
    other = lax.ppermute(tail, "half", [(0, 1), (1, 0)])
    bands_a = across(plane_copies(False, here, spread_depth(avg_a)))
    avg_b, packed = second_average(gather_depth(plane_sums(False, here, bands_b)), tail, other)
    bands_b = across(plane_copies(True, here, spread_depth(packed)))
    residual, scores, leverage = second_outputs(*common, bands_b, first_outputs(*common, bands_a))
    average = jnp.concatenate([avg_a, avg_b], axis=0)
    return (average[None, None], residual[None], scores.T[None], leverage)


def solution(mesh):
    in_specs = (
        P("half", "cls", None, None),
        P("half", "cls"),
        P("half", "cls"),
        P("half", "cls"),
        P(),
    )
    out_specs = (
        P("half", "cls", None, None),
        P("half", "cls", None, None),
        P("half", "cls", None),
        P("half", "cls"),
    )
    return jax.shard_map(body, mesh=mesh, in_specs=in_specs, out_specs=out_specs, check_vma=False)
```

time: 570 us -> 195 us (0.34); the launches traced: 560 us -> 194 us
  waiting for transfers between devices: 353 us -> 49.2 us
  matrix products: 54.6 us -> 0 us
  other arithmetic: 43.3 us -> 0.62 us
  Pallas kernels: 0 us -> 42.2 us
  starting transfers between devices: 49.1 us -> 89.1 us
  blocking collectives: 23.9 us -> 0 us
  local copies, waits for them, and re-layouts: 34.6 us -> 12.1 us
    all_to_all x4, waiting for transfers between devices: 353 us -> 40.1 us  [across(): lax.all_to_all(value, 'cls', split_axis=0, concat_axis=0, tiled=True, axi...]
    ppermute x1 -> x31, starting transfers between devices: 2.55 us -> 63 us  [the longest x16 31.6 us: spread_depth(): lax.ppermute(value, ('half', 'cls'), [(h * CLASSES + i, (1 - h) * CLASSES...]
    dot_general x3 -> x0, matrix products: 54.6 us -> none  [the longest x1 24.7 us: rotation_scores(): jnp.einsum('sab,tab->st', cross, table.astype(jnp.float32), precision=lax...]
    pallas_call x0 -> x10, Pallas kernels: none -> 42.2 us  [the longest x1 13 us: second_outputs(): pl.pallas_call(lambda *refs: outputs_kernel(1, *refs), out_shape=(jax.Sha...]
    reduce_sum x5 -> x0, other arithmetic: 37.8 us -> none  [the longest x1 31.4 us: rotation_scores(): jnp.mean(jnp.square(predicted.astype(jnp.float32)), axis=(1, 2)) + 1e-05]
    all_to_all x1 -> x0, blocking collectives: 23.9 us -> none  [body(): lax.all_to_all(scores.reshape(owners, capacity, NROT), 'cls', split_axis=...]
    all_to_all x4, starting transfers between devices: 46.6 us -> 26.1 us  [across(): lax.all_to_all(value, 'cls', split_axis=0, concat_axis=0, tiled=True, axi...]
    gather x5 -> x0, local copies, waits for them, and re-layouts: 16.5 us -> none  [the longest x1 8.35 us: body(): table[lowered % NROT]]
  transfers between devices with their start and end apart: 5 -> 35, of which waited for: 2 -> 9; matrix products, arithmetic and copies ran while one was open for 22% -> 0% of each run, Pallas kernels for 0% -> 13%
where the time goes in v2:
time: 195 us; the launch traced here: 194 us
  starting transfers between devices  89.1 us (46%)
  waiting for transfers between devices  49.2 us (25%)
  Pallas kernels  42.2 us (22%)
  local copies, waits for them, and re-layouts  12.1 us (6%)
    all_to_all x4, waiting for transfers between devices, across(): lax.all_to_all(value, 'cls', split_axis=0, concat_axis=0, tiled=True, axi...  40.1 us
    ppermute x16, starting transfers between devices, spread_depth(): lax.ppermute(value, ('half', 'cls'), [(h * CLASSES + i, (1 - h) * CLASSES...  31.6 us
    ppermute x14, starting transfers between devices, gather_depth(): lax.ppermute(pieces[j], 'cls', [(i, upward(i, j)) for i in range(CLASSES)])  28.9 us
    all_to_all x4, starting transfers between devices, across(): lax.all_to_all(value, 'cls', split_axis=0, concat_axis=0, tiled=True, axi...  26.1 us
    pallas_call x1, Pallas kernels, second_outputs(): pl.pallas_call(lambda *refs: outputs_kernel(1, *refs), out_shape=(jax.Sha...  13 us
    pallas_call x1, Pallas kernels, first_outputs(): pl.pallas_call(lambda *refs: outputs_kernel(0, *refs), out_shape=(jax.Sha...  12.4 us
    unnamed x70, local copies, waits for them, and re-layouts  12.1 us
    pallas_call x2, Pallas kernels, class_sums(): pl.pallas_call(lambda *refs: sums_kernel(chunk, *refs), out_shape=jax.Sha...  8.85 us
  transfers between devices with their start and end apart: 35, of which 9 were waited for; matrix products, arithmetic and copies ran while one was open for 0% of the time, Pallas kernels for 13%

profile of v2, /device:TPU:1, one launch (start us, length us, event | category | flops | bytes accessed | tf_op | source)
XLA Modules:
  0.0 194.5 jit_solution(9231105083174928551)
XLA Ops:
  5.0 4.5 %class_sums_0.1 = bf16[16,528,128]{2,1,0:T(8,128)(2,1)S(1)} custom-call(s32[1,64]{1,0:T(1,128)S(1)} %copy-done.11, s32[1,64]{1,0:T(1,128)S(1)} %copy-done.13, s32[1,64]{1,0:T(1,128)S(1)} %copy-done.15, f32[64,256]{1,0:T(8,128)S(1)} %bitcast.13, bf16[64,128,128]{2,1,0:T(8,128)(2,1)S(1)} %bitcast.9), custom_call_target="tpu_custom_call" | custom-call | flops 1000000000 | bytes 16777216 | tf_op jit(solution)/shard_map/class_sums_0/pallas_call | solution.py:151
  11.0 7.8 %all-to-all-start = ((bf16[16,528,128]{2,1,0:T(8,128)(2,1)}), bf16[16,528,128]{2,1,0:T(8,128)(2,1)}, u32[]{:S(2)}, u32[]{:S(2)}) async-start(bf16[16,528,128]{2,1,0:T(8,128)(2,1)} %copy-done.2), calls=%async_computation | async-start | bytes 4325376 | tf_op jit(solution)/shard_map/all_to_all | solution.py:392
  18.8 4.3 %class_sums_1.1 = bf16[16,512,128]{2,1,0:T(8,128)(2,1)S(1)} custom-call(s32[1,64]{1,0:T(1,128)S(1)} %copy-done.12, s32[1,64]{1,0:T(1,128)S(1)} %copy-done.14, s32[1,64]{1,0:T(1,128)S(1)} %copy-done.16, f32[64,256]{1,0:T(8,128)S(1)} %bitcast.14, bf16[64,128,128]{2,1,0:T(8,128)(2,1)S(1)} %bitcast.10), custom_call_target="tpu_custom_call" | custom-call | flops 1000000000 | bytes 16777216 | tf_op jit(solution)/shard_map/class_sums_1/pallas_call | solution.py:151
  24.5 23.2 %all-to-all-done.refs_1_ = bf16[16,528,128]{2,1,0:T(8,128)(2,1)} async-done(((bf16[16,528,128]{2,1,0:T(8,128)(2,1)}), bf16[16,528,128]{2,1,0:T(8,128)(2,1)}, u32[]{:S(2)}, u32[]{:S(2)}) %all-to-all-start) | async-done | bytes 2162720 | tf_op jit(solution)/shard_map/all_to_all | solution.py:392
  47.7 4.4 %all-to-all-start.1 = ((bf16[16,512,128]{2,1,0:T(8,128)(2,1)}), bf16[16,512,128]{2,1,0:T(8,128)(2,1)}, u32[]{:S(2)}, u32[]{:S(2)}) async-start(bf16[16,512,128]{2,1,0:T(8,128)(2,1)} %copy-done.4), calls=%async_computation.1 | async-start | bytes 4194304 | tf_op jit(solution)/shard_map/all_to_all | solution.py:392
  56.3 3.0 %collective-permute-start.1 = (bf16[80,128]{1,0:T(8,128)(2,1)S(1)}, bf16[80,128]{1,0:T(8,128)(2,1)S(1)}, u32[]{:S(2)}, u32[]{:S(2)}) collective-permute-start(bf16[80,128]{1,0:T(8,128)(2,1)S(1)} %get-tuple-element.33), channel_id=1, source_target_pairs={{0,2},{1,3},{2,4},{3,5},{4,6},{5,7},{6,0},{7,1},{8,10},{9,11},{10,... | collective-permute-start | bytes 61448 | tf_op jit(solution)/shard_map/ppermute | solution.py:401
  59.3 3.8 %collective-permute-start.2 = (bf16[80,128]{1,0:T(8,128)(2,1)S(1)}, bf16[80,128]{1,0:T(8,128)(2,1)S(1)}, u32[]{:S(2)}, u32[]{:S(2)}) collective-permute-start(bf16[80,128]{1,0:T(8,128)(2,1)S(1)} %get-tuple-element.34), channel_id=1, source_target_pairs={{0,3},{1,4},{2,5},{3,6},{4,7},{5,0},{6,1},{7,2},{8,11},{9,12},{10,... | collective-permute-start | bytes 61448 | tf_op jit(solution)/shard_map/ppermute | solution.py:401
  63.5 4.5 %collective-permute-start.4 = (bf16[80,128]{1,0:T(8,128)(2,1)S(1)}, bf16[80,128]{1,0:T(8,128)(2,1)S(1)}, u32[]{:S(2)}, u32[]{:S(2)}) collective-permute-start(bf16[80,128]{1,0:T(8,128)(2,1)S(1)} %get-tuple-element.36), channel_id=1, source_target_pairs={{0,5},{1,6},{2,7},{3,0},{4,1},{5,2},{6,3},{7,4},{8,13},{9,14},{10,... | collective-permute-start | bytes 61448 | tf_op jit(solution)/shard_map/ppermute | solution.py:401
  75.7 5.8 %collective-permute-start.23 = (bf16[64,128]{1,0:T(8,128)(2,1)}, bf16[64,128]{1,0:T(8,128)(2,1)S(1)}, u32[]{:S(2)}, u32[]{:S(2)}) collective-permute-start(bf16[64,128]{1,0:T(8,128)(2,1)} %get-tuple-element.39), channel_id=1, source_target_pairs={{0,128},{1,129},{2,130},{3,131},{4,132},{5,133},{6,134},{7,135},{8... | collective-permute-start | bytes 49160 | tf_op jit(solution)/shard_map/ppermute | solution.py:407
  82.7 3.2 %collective-permute-start.26 = (bf16[64,128]{1,0:T(8,128)(2,1)}, bf16[64,128]{1,0:T(8,128)(2,1)S(1)}, u32[]{:S(2)}, u32[]{:S(2)}) collective-permute-start(bf16[64,128]{1,0:T(8,128)(2,1)} %get-tuple-element.39), channel_id=1, source_target_pairs={{0,131},{1,132},{2,133},{3,134},{4,135},{5,128},{6,129},{7,130},{8... | collective-permute-start | bytes 49160 | tf_op jit(solution)/shard_map/ppermute | solution.py:407
  87.7 3.9 %collective-permute-start.28 = (bf16[64,128]{1,0:T(8,128)(2,1)}, bf16[64,128]{1,0:T(8,128)(2,1)S(1)}, u32[]{:S(2)}, u32[]{:S(2)}) collective-permute-start(bf16[64,128]{1,0:T(8,128)(2,1)} %get-tuple-element.39), channel_id=1, source_target_pairs={{0,133},{1,134},{2,135},{3,128},{4,129},{5,130},{6,131},{7,132},{8... | collective-permute-start | bytes 49160 | tf_op jit(solution)/shard_map/ppermute | solution.py:407
  93.3 2.8 %collective-permute-done.29.refs_7_ = bf16[64,128]{1,0:T(8,128)(2,1)S(1)} collective-permute-done((bf16[64,128]{1,0:T(8,128)(2,1)}, bf16[64,128]{1,0:T(8,128)(2,1)S(1)}, u32[]{:S(2)}, u32[]{:S(2)}) %collective-permute-start.29) | collective-permute-done | bytes 16416 | tf_op jit(solution)/shard_map/ppermute | solution.py:407
  97.9 6.9 %all-to-all-start.3 = ((bf16[16,512,128]{2,1,0:T(8,128)(2,1)}), bf16[16,512,128]{2,1,0:T(8,128)(2,1)}, u32[]{:S(2)}, u32[]{:S(2)}) async-start(bf16[16,512,128]{2,1,0:T(8,128)(2,1)} %copy-done.5), calls=%async_computation.3 | async-start | bytes 4194304 | tf_op jit(solution)/shard_map/all_to_all | solution.py:392
  108.0 2.8 %collective-permute-start.8 = (bf16[64,128]{1,0:T(8,128)(2,1)S(1)}, bf16[64,128]{1,0:T(8,128)(2,1)S(1)}, u32[]{:S(2)}, u32[]{:S(2)}) collective-permute-start(bf16[64,128]{1,0:T(8,128)(2,1)S(1)} %get-tuple-element.42), channel_id=1, source_target_pairs={{0,2},{1,3},{2,4},{3,5},{4,6},{5,7},{6,0},{7,1},{8,10},{9,11},{10,... | collective-permute-start | bytes 49160 | tf_op jit(solution)/shard_map/ppermute | solution.py:401
  111.9 2.8 %collective-permute-start.10 = (bf16[64,128]{1,0:T(8,128)(2,1)S(1)}, bf16[64,128]{1,0:T(8,128)(2,1)S(1)}, u32[]{:S(2)}, u32[]{:S(2)}) collective-permute-start(bf16[64,128]{1,0:T(8,128)(2,1)S(1)} %get-tuple-element.44), channel_id=1, source_target_pairs={{0,4},{1,5},{2,6},{3,7},{4,0},{5,1},{6,2},{7,3},{8,12},{9,13},{10,... | collective-permute-start | bytes 49160 | tf_op jit(solution)/shard_map/ppermute | solution.py:401
  119.8 2.5 %collective-permute-start.14 = (bf16[16,128]{1,0:T(8,128)(2,1)S(1)}, bf16[16,128]{1,0:T(8,128)(2,1)S(1)}, u32[]{:S(2)}, u32[]{:S(2)}) collective-permute-start(bf16[16,128]{1,0:T(8,128)(2,1)S(1)} %copy-done.33), channel_id=1, source_target_pairs={{0,128},{128,0},{1,129},{129,1},{2,130},{130,2},{3,131},{131,3},{4... | collective-permute-start | bytes 12296 | tf_op jit(solution)/shard_map/ppermute | solution.py:422
  127.0 2.8 %collective-permute-start.17 = (bf16[80,128]{1,0:T(8,128)(2,1)}, bf16[80,128]{1,0:T(8,128)(2,1)S(1)}, u32[]{:S(2)}, u32[]{:S(2)}) collective-permute-start(bf16[80,128]{1,0:T(8,128)(2,1)} %get-tuple-element.50), channel_id=1, source_target_pairs={{0,130},{1,131},{2,132},{3,133},{4,134},{5,135},{6,128},{7,129},{8... | collective-permute-start | bytes 61448 | tf_op jit(solution)/shard_map/ppermute | solution.py:407
  131.6 3.0 %collective-permute-start.19 = (bf16[80,128]{1,0:T(8,128)(2,1)}, bf16[80,128]{1,0:T(8,128)(2,1)S(1)}, u32[]{:S(2)}, u32[]{:S(2)}) collective-permute-start(bf16[80,128]{1,0:T(8,128)(2,1)} %get-tuple-element.50), channel_id=1, source_target_pairs={{0,132},{1,133},{2,134},{3,135},{4,128},{5,129},{6,130},{7,131},{8... | collective-permute-start | bytes 61448 | tf_op jit(solution)/shard_map/ppermute | solution.py:407
  134.5 2.9 %collective-permute-start.20 = (bf16[80,128]{1,0:T(8,128)(2,1)}, bf16[80,128]{1,0:T(8,128)(2,1)S(1)}, u32[]{:S(2)}, u32[]{:S(2)}) collective-permute-start(bf16[80,128]{1,0:T(8,128)(2,1)} %get-tuple-element.50), channel_id=1, source_target_pairs={{0,133},{1,134},{2,135},{3,128},{4,129},{5,130},{6,131},{7,132},{8... | collective-permute-start | bytes 61448 | tf_op jit(solution)/shard_map/ppermute | solution.py:407
  140.1 2.5 %collective-permute-done.21.refs_7_ = bf16[80,128]{1,0:T(8,128)(2,1)S(1)} collective-permute-done((bf16[80,128]{1,0:T(8,128)(2,1)}, bf16[80,128]{1,0:T(8,128)(2,1)S(1)}, u32[]{:S(2)}, u32[]{:S(2)}) %collective-permute-start.21) | collective-permute-done | bytes 20512 | tf_op jit(solution)/shard_map/ppermute | solution.py:407
  144.2 7.1 %all-to-all-start.2 = ((bf16[16,528,128]{2,1,0:T(8,128)(2,1)}), bf16[16,528,128]{2,1,0:T(8,128)(2,1)}, u32[]{:S(2)}, u32[]{:S(2)}) async-start(bf16[16,528,128]{2,1,0:T(8,128)(2,1)} %copy-done.3), calls=%async_computation.2 | async-start | bytes 4325376 | tf_op jit(solution)/shard_map/all_to_all | solution.py:392
  152.0 12.4 %outputs_0.1 = (bf16[64,128,128]{2,1,0:T(8,128)(2,1)}, f32[512,128]{1,0:T(8,128)S(1)}, f32[64,128]{1,0:T(8,128)S(1)}, f32[64,128]{1,0:T(8,128)S(1)}) custom-call(s32[1,64]{1,0:T(1,128)S(1)} %copy-done.12, s32[1,64]{1,0:T(1,128)S(1)} %copy-done.14, s32[1,64]{1,0:T(1,128)S(1)} %copy-done.16, f32[64,256]{1,0:T(8,128)S(1)} %bitcast.15, ...), custom_call_target="tpu_custom_call" | custom-call | flops 1000000000 | bytes 33554432 | tf_op jit(solution)/shard_map/outputs_0/pallas_call | solution.py:352
  164.4 16.9 %all-to-all-done.2.refs_5_ = bf16[16,528,128]{2,1,0:T(8,128)(2,1)} async-done(((bf16[16,528,128]{2,1,0:T(8,128)(2,1)}), bf16[16,528,128]{2,1,0:T(8,128)(2,1)}, u32[]{:S(2)}, u32[]{:S(2)}) %all-to-all-start.2) | async-done | bytes 2162720 | tf_op jit(solution)/shard_map/all_to_all | solution.py:392
  181.3 13.0 %outputs_1.1 = (bf16[64,128,128]{2,1,0:T(8,128)(2,1)}, bf16[36,64]{1,0:T(8,128)(2,1)}, bf16[1,64]{1,0:T(2,128)(2,1)}) custom-call(s32[1,64]{1,0:T(1,128)S(1)} %copy-done.12, s32[1,64]{1,0:T(1,128)S(1)} %copy-done.14, s32[1,64]{1,0:T(1,128)S(1)} %copy-done.16, f32[64,256]{1,0:T(8,128)S(1)} %bitcast.16, ...), custom_call_target="tpu_custom_call", output_to_operand_aliasing={{0}: (10, {})} | custom-call | flops 1000000000 | bytes 33554432 | tf_op jit(solution)/shard_map/outputs_1/pallas_call | solution.py:373
  (127 shorter events, 46.8 us)
Async XLA Ops:
  11.0 36.7 %all-to-all-start = ((bf16[16,528,128]{2,1,0:T(8,128)(2,1)}), bf16[16,528,128]{2,1,0:T(8,128)(2,1)}, u32[]{:S(2)}, u32[]{:S(2)}) async-start(bf16[16,528,128]{2,1,0:T(8,128)(2,1)} %copy-done.2), calls=%async_computation | async-start | bytes 4325376 | tf_op jit(solution)/shard_map/all_to_all | solution.py:392
  47.7 50.3 %all-to-all-start.1 = ((bf16[16,512,128]{2,1,0:T(8,128)(2,1)}), bf16[16,512,128]{2,1,0:T(8,128)(2,1)}, u32[]{:S(2)}, u32[]{:S(2)}) async-start(bf16[16,512,128]{2,1,0:T(8,128)(2,1)} %copy-done.4), calls=%async_computation.1 | async-start | bytes 4194304 | tf_op jit(solution)/shard_map/all_to_all | solution.py:392
  54.7 13.3 %collective-permute-start = (bf16[80,128]{1,0:T(8,128)(2,1)S(1)}, bf16[80,128]{1,0:T(8,128)(2,1)S(1)}, u32[]{:S(2)}, u32[]{:S(2)}) collective-permute-start(bf16[80,128]{1,0:T(8,128)(2,1)S(1)} %get-tuple-element.32), channel_id=1, source_target_pairs={{0,1},{1,2},{2,3},{3,4},{4,5},{5,6},{6,7},{7,0},{8,9},{9,10},{10,1... | collective-permute-start | bytes 61448 | tf_op jit(solution)/shard_map/ppermute | solution.py:401
  56.3 14.1 %collective-permute-start.1 = (bf16[80,128]{1,0:T(8,128)(2,1)S(1)}, bf16[80,128]{1,0:T(8,128)(2,1)S(1)}, u32[]{:S(2)}, u32[]{:S(2)}) collective-permute-start(bf16[80,128]{1,0:T(8,128)(2,1)S(1)} %get-tuple-element.33), channel_id=1, source_target_pairs={{0,2},{1,3},{2,4},{3,5},{4,6},{5,7},{6,0},{7,1},{8,10},{9,11},{10,... | collective-permute-start | bytes 61448 | tf_op jit(solution)/shard_map/ppermute | solution.py:401
  59.3 11.8 %collective-permute-start.2 = (bf16[80,128]{1,0:T(8,128)(2,1)S(1)}, bf16[80,128]{1,0:T(8,128)(2,1)S(1)}, u32[]{:S(2)}, u32[]{:S(2)}) collective-permute-start(bf16[80,128]{1,0:T(8,128)(2,1)S(1)} %get-tuple-element.34), channel_id=1, source_target_pairs={{0,3},{1,4},{2,5},{3,6},{4,7},{5,0},{6,1},{7,2},{8,11},{9,12},{10,... | collective-permute-start | bytes 61448 | tf_op jit(solution)/shard_map/ppermute | solution.py:401
  63.1 8.0 %collective-permute-start.3 = (bf16[80,128]{1,0:T(8,128)(2,1)S(1)}, bf16[80,128]{1,0:T(8,128)(2,1)S(1)}, u32[]{:S(2)}, u32[]{:S(2)}) collective-permute-start(bf16[80,128]{1,0:T(8,128)(2,1)S(1)} %get-tuple-element.35), channel_id=1, source_target_pairs={{0,4},{1,5},{2,6},{3,7},{4,0},{5,1},{6,2},{7,3},{8,12},{9,13},{10,... | collective-permute-start | bytes 61448 | tf_op jit(solution)/shard_map/ppermute | solution.py:401
  63.5 7.6 %collective-permute-start.4 = (bf16[80,128]{1,0:T(8,128)(2,1)S(1)}, bf16[80,128]{1,0:T(8,128)(2,1)S(1)}, u32[]{:S(2)}, u32[]{:S(2)}) collective-permute-start(bf16[80,128]{1,0:T(8,128)(2,1)S(1)} %get-tuple-element.36), channel_id=1, source_target_pairs={{0,5},{1,6},{2,7},{3,0},{4,1},{5,2},{6,3},{7,4},{8,13},{9,14},{10,... | collective-permute-start | bytes 61448 | tf_op jit(solution)/shard_map/ppermute | solution.py:401
  75.7 12.0 %collective-permute-start.23 = (bf16[64,128]{1,0:T(8,128)(2,1)}, bf16[64,128]{1,0:T(8,128)(2,1)S(1)}, u32[]{:S(2)}, u32[]{:S(2)}) collective-permute-start(bf16[64,128]{1,0:T(8,128)(2,1)} %get-tuple-element.39), channel_id=1, source_target_pairs={{0,128},{1,129},{2,130},{3,131},{4,132},{5,133},{6,134},{7,135},{8... | collective-permute-start | bytes 49160 | tf_op jit(solution)/shard_map/ppermute | solution.py:407
  81.5 10.1 %collective-permute-start.24 = (bf16[64,128]{1,0:T(8,128)(2,1)}, bf16[64,128]{1,0:T(8,128)(2,1)S(1)}, u32[]{:S(2)}, u32[]{:S(2)}) collective-permute-start(bf16[64,128]{1,0:T(8,128)(2,1)} %get-tuple-element.39), channel_id=1, source_target_pairs={{0,129},{1,130},{2,131},{3,132},{4,133},{5,134},{6,135},{7,128},{8... | collective-permute-start | bytes 49160 | tf_op jit(solution)/shard_map/ppermute | solution.py:407
  81.5 11.2 %collective-permute-start.25 = (bf16[64,128]{1,0:T(8,128)(2,1)}, bf16[64,128]{1,0:T(8,128)(2,1)S(1)}, u32[]{:S(2)}, u32[]{:S(2)}) collective-permute-start(bf16[64,128]{1,0:T(8,128)(2,1)} %get-tuple-element.39), channel_id=1, source_target_pairs={{0,130},{1,131},{2,132},{3,133},{4,134},{5,135},{6,128},{7,129},{8... | collective-permute-start | bytes 49160 | tf_op jit(solution)/shard_map/ppermute | solution.py:407
  82.7 10.0 %collective-permute-start.26 = (bf16[64,128]{1,0:T(8,128)(2,1)}, bf16[64,128]{1,0:T(8,128)(2,1)S(1)}, u32[]{:S(2)}, u32[]{:S(2)}) collective-permute-start(bf16[64,128]{1,0:T(8,128)(2,1)} %get-tuple-element.39), channel_id=1, source_target_pairs={{0,131},{1,132},{2,133},{3,134},{4,135},{5,128},{6,129},{7,130},{8... | collective-permute-start | bytes 49160 | tf_op jit(solution)/shard_map/ppermute | solution.py:407
  85.9 7.4 %collective-permute-start.27 = (bf16[64,128]{1,0:T(8,128)(2,1)}, bf16[64,128]{1,0:T(8,128)(2,1)S(1)}, u32[]{:S(2)}, u32[]{:S(2)}) collective-permute-start(bf16[64,128]{1,0:T(8,128)(2,1)} %get-tuple-element.39), channel_id=1, source_target_pairs={{0,132},{1,133},{2,134},{3,135},{4,128},{5,129},{6,130},{7,131},{8... | collective-permute-start | bytes 49160 | tf_op jit(solution)/shard_map/ppermute | solution.py:407
  97.9 46.3 %all-to-all-start.3 = ((bf16[16,512,128]{2,1,0:T(8,128)(2,1)}), bf16[16,512,128]{2,1,0:T(8,128)(2,1)}, u32[]{:S(2)}, u32[]{:S(2)}) async-start(bf16[16,512,128]{2,1,0:T(8,128)(2,1)} %copy-done.5), calls=%async_computation.3 | async-start | bytes 4194304 | tf_op jit(solution)/shard_map/all_to_all | solution.py:392
  107.3 9.5 %collective-permute-start.7 = (bf16[64,128]{1,0:T(8,128)(2,1)S(1)}, bf16[64,128]{1,0:T(8,128)(2,1)S(1)}, u32[]{:S(2)}, u32[]{:S(2)}) collective-permute-start(bf16[64,128]{1,0:T(8,128)(2,1)S(1)} %get-tuple-element.41), channel_id=1, source_target_pairs={{0,1},{1,2},{2,3},{3,4},{4,5},{5,6},{6,7},{7,0},{8,9},{9,10},{10,1... | collective-permute-start | bytes 49160 | tf_op jit(solution)/shard_map/ppermute | solution.py:401
  108.0 10.6 %collective-permute-start.8 = (bf16[64,128]{1,0:T(8,128)(2,1)S(1)}, bf16[64,128]{1,0:T(8,128)(2,1)S(1)}, u32[]{:S(2)}, u32[]{:S(2)}) collective-permute-start(bf16[64,128]{1,0:T(8,128)(2,1)S(1)} %get-tuple-element.42), channel_id=1, source_target_pairs={{0,2},{1,3},{2,4},{3,5},{4,6},{5,7},{6,0},{7,1},{8,10},{9,11},{10,... | collective-permute-start | bytes 49160 | tf_op jit(solution)/shard_map/ppermute | solution.py:401
  110.8 9.0 %collective-permute-start.9 = (bf16[64,128]{1,0:T(8,128)(2,1)S(1)}, bf16[64,128]{1,0:T(8,128)(2,1)S(1)}, u32[]{:S(2)}, u32[]{:S(2)}) collective-permute-start(bf16[64,128]{1,0:T(8,128)(2,1)S(1)} %get-tuple-element.43), channel_id=1, source_target_pairs={{0,3},{1,4},{2,5},{3,6},{4,7},{5,0},{6,1},{7,2},{8,11},{9,12},{10,... | collective-permute-start | bytes 49160 | tf_op jit(solution)/shard_map/ppermute | solution.py:401
  111.9 10.4 %collective-permute-start.10 = (bf16[64,128]{1,0:T(8,128)(2,1)S(1)}, bf16[64,128]{1,0:T(8,128)(2,1)S(1)}, u32[]{:S(2)}, u32[]{:S(2)}) collective-permute-start(bf16[64,128]{1,0:T(8,128)(2,1)S(1)} %get-tuple-element.44), channel_id=1, source_target_pairs={{0,4},{1,5},{2,6},{3,7},{4,0},{5,1},{6,2},{7,3},{8,12},{9,13},{10,... | collective-permute-start | bytes 49160 | tf_op jit(solution)/shard_map/ppermute | solution.py:401
  114.7 7.6 %collective-permute-start.11 = (bf16[64,128]{1,0:T(8,128)(2,1)S(1)}, bf16[64,128]{1,0:T(8,128)(2,1)S(1)}, u32[]{:S(2)}, u32[]{:S(2)}) collective-permute-start(bf16[64,128]{1,0:T(8,128)(2,1)S(1)} %get-tuple-element.45), channel_id=1, source_target_pairs={{0,5},{1,6},{2,7},{3,0},{4,1},{5,2},{6,3},{7,4},{8,13},{9,14},{10,... | collective-permute-start | bytes 49160 | tf_op jit(solution)/shard_map/ppermute | solution.py:401
  125.4 9.2 %collective-permute-start.15 = (bf16[80,128]{1,0:T(8,128)(2,1)}, bf16[80,128]{1,0:T(8,128)(2,1)S(1)}, u32[]{:S(2)}, u32[]{:S(2)}) collective-permute-start(bf16[80,128]{1,0:T(8,128)(2,1)} %get-tuple-element.50), channel_id=1, source_target_pairs={{0,128},{1,129},{2,130},{3,131},{4,132},{5,133},{6,134},{7,135},{8... | collective-permute-start | bytes 61448 | tf_op jit(solution)/shard_map/ppermute | solution.py:407
  126.5 10.9 %collective-permute-start.16 = (bf16[80,128]{1,0:T(8,128)(2,1)}, bf16[80,128]{1,0:T(8,128)(2,1)S(1)}, u32[]{:S(2)}, u32[]{:S(2)}) collective-permute-start(bf16[80,128]{1,0:T(8,128)(2,1)} %get-tuple-element.50), channel_id=1, source_target_pairs={{0,129},{1,130},{2,131},{3,132},{4,133},{5,134},{6,135},{7,128},{8... | collective-permute-start | bytes 61448 | tf_op jit(solution)/shard_map/ppermute | solution.py:407
  127.0 11.7 %collective-permute-start.17 = (bf16[80,128]{1,0:T(8,128)(2,1)}, bf16[80,128]{1,0:T(8,128)(2,1)S(1)}, u32[]{:S(2)}, u32[]{:S(2)}) collective-permute-start(bf16[80,128]{1,0:T(8,128)(2,1)} %get-tuple-element.50), channel_id=1, source_target_pairs={{0,130},{1,131},{2,132},{3,133},{4,134},{5,135},{6,128},{7,129},{8... | collective-permute-start | bytes 61448 | tf_op jit(solution)/shard_map/ppermute | solution.py:407
  129.8 10.3 %collective-permute-start.18 = (bf16[80,128]{1,0:T(8,128)(2,1)}, bf16[80,128]{1,0:T(8,128)(2,1)S(1)}, u32[]{:S(2)}, u32[]{:S(2)}) collective-permute-start(bf16[80,128]{1,0:T(8,128)(2,1)} %get-tuple-element.50), channel_id=1, source_target_pairs={{0,131},{1,132},{2,133},{3,134},{4,135},{5,128},{6,129},{7,130},{8... | collective-permute-start | bytes 61448 | tf_op jit(solution)/shard_map/ppermute | solution.py:407
  131.6 8.5 %collective-permute-start.19 = (bf16[80,128]{1,0:T(8,128)(2,1)}, bf16[80,128]{1,0:T(8,128)(2,1)S(1)}, u32[]{:S(2)}, u32[]{:S(2)}) collective-permute-start(bf16[80,128]{1,0:T(8,128)(2,1)} %get-tuple-element.50), channel_id=1, source_target_pairs={{0,132},{1,133},{2,134},{3,135},{4,128},{5,129},{6,130},{7,131},{8... | collective-permute-start | bytes 61448 | tf_op jit(solution)/shard_map/ppermute | solution.py:407
  144.2 37.1 %all-to-all-start.2 = ((bf16[16,528,128]{2,1,0:T(8,128)(2,1)}), bf16[16,528,128]{2,1,0:T(8,128)(2,1)}, u32[]{:S(2)}, u32[]{:S(2)}) async-start(bf16[16,528,128]{2,1,0:T(8,128)(2,1)} %copy-done.3), calls=%async_computation.2 | async-start | bytes 4325376 | tf_op jit(solution)/shard_map/all_to_all | solution.py:392
  (46 other events, 191.9 us)

commit v3 on v2

v3 whole, which is shorter than its diff:
```python
import math

import jax
import jax.numpy as jnp
import numpy as np
from jax import lax
from jax.experimental import pallas as pl
from jax.experimental.pallas import tpu as pltpu
from jax.sharding import PartitionSpec as P

NROT = 36
TAU = 1.0
GROUP = 32
STACK = 4
DEPTH = 2 * STACK
CLASSES = GROUP * STACK
LANES = 128
ROWS = 128
SHELLS = ROWS // 2
TAIL = 16
BAND = STACK * ROWS + TAIL
SLAB = ROWS + TAIL
BATCH = 8
HIGH = lax.Precision.HIGHEST
F32 = jnp.float32
BF16 = jnp.bfloat16

HBM = pl.BlockSpec(memory_space=pltpu.HBM)
VMEM = pl.BlockSpec(memory_space=pltpu.VMEM)


def rotation_steps():
    turns = np.arange(NROT)
    offset = turns * LANES // NROT
    fraction = ((turns * LANES) % NROT).astype(np.float32) / np.float32(NROT)
    keep = (np.float32(1.0) - fraction).astype(BF16).astype(np.float32)
    carry = fraction.astype(BF16).astype(np.float32)
    return offset, keep, carry


def lag_matrix():
    offset, keep, carry = rotation_steps()
    out = np.zeros((LANES, LANES), np.float32)
    for r in range(NROT):
        out[offset[r] % LANES, r] += keep[r]
        out[(offset[r] + 1) % LANES, r] += carry[r]
    return out


def fill_steps(offsets, parts):
    offset, keep, carry = rotation_steps()
    for r in range(NROT):
        offsets[r] = jnp.int32(int(offset[r]))
        parts[0, r] = jnp.float32(float(keep[r]))
        parts[1, r] = jnp.float32(float(carry[r]))


def contract(left, right, dims):
    return lax.dot_general(left, right, (dims, ((), ())), precision=HIGH, preferred_element_type=F32)


def weights_by_shell(group_row, table):
    groups, count = table.shape[1], group_row.shape[1]
    pick = (lax.broadcasted_iota(jnp.int32, (groups, count), 0) == group_row).astype(F32)
    return contract(table, pick, ((1,), (0,)))


def split_pair(value):
    high = value.astype(BF16).astype(F32)
    return jnp.concatenate([high, value - high], axis=1)


def join_pair(pair):
    return pair[:, : LANES // 2] + pair[:, LANES // 2 :]


def align(image, turn, offsets, parts):
    first = pltpu.roll(image, offsets[turn], 1)
    second = pltpu.roll(first, 1, 1)
    return parts[0, turn] * first + parts[1, turn] * second


def keep_columns(by_shell, columns):
    for b in range(columns.shape[0]):
        columns[b, :, :BATCH] = by_shell[:, b * BATCH : (b + 1) * BATCH]


def slot_of(c):
    return (c // DEPTH) * 2 + c % 2, (c // 2) % STACK


def begin(assign, rotation, group, table, images, places, sems):
    classes, turns, assign_row, group_row, local, rows = places
    copies = [
        pltpu.make_async_copy(images, rows, sems.at[0]),
        pltpu.make_async_copy(group, group_row, sems.at[1]),
        pltpu.make_async_copy(table, local, sems.at[2]),
        pltpu.make_async_copy(assign, assign_row, sems.at[3]),
        pltpu.make_async_copy(assign, classes, sems.at[4]),
        pltpu.make_async_copy(rotation, turns, sems.at[5]),
    ]
    for copy in copies:
        copy.start()
    return copies


def place_shapes(count, groups):
    return [
        pltpu.SMEM((1, count), jnp.int32),
        pltpu.SMEM((1, count), jnp.int32),
        pltpu.VMEM((1, count), jnp.int32),
        pltpu.VMEM((1, count), jnp.int32),
        pltpu.VMEM((SHELLS, groups), F32),
        pltpu.VMEM((count, ROWS, LANES), BF16),
        pltpu.SMEM((NROT,), jnp.int32),
        pltpu.SMEM((2, NROT), F32),
        pltpu.VMEM((count // BATCH, SHELLS, LANES), F32),
        pltpu.SemaphoreType.DMA((6,)),
    ]


def scale_rows(column, value):
    return jnp.concatenate([column * value[:SHELLS], column * value[SHELLS:]], axis=0)


def sums_kernel(assign, rotation, group, table, images, out, *scratch):
    places, (offsets, parts, columns, sems) = scratch[:6], scratch[6:10]
    classes, turns, assign_row, group_row, local, rows = places
    count = rows.shape[0]
    copies = begin(assign, rotation, group, table, images, places, sems)
    fill_steps(offsets, parts)
    for d in range(GROUP):
        out[d, : STACK * ROWS, :] = jnp.zeros((STACK * ROWS, LANES), BF16)
    for copy in copies:
        copy.wait()
    by_shell = weights_by_shell(group_row[...], local[...])
    keep_columns(by_shell, columns)
    n = lax.broadcasted_iota(jnp.int32, (CLASSES, count), 0)
    d, s = n // STACK, n % STACK
    member = ((d // 2) * DEPTH + s * 2 + d % 2 == assign_row[...]).astype(F32)
    pair = split_pair(contract(member, jnp.transpose(by_shell * by_shell), ((1,), (0,))))
    blank = jnp.zeros((TAIL - STACK, LANES), F32)
    for d in range(GROUP):
        tile = jnp.concatenate([pair[d * STACK : (d + 1) * STACK], blank], axis=0)
        out[d, STACK * ROWS :, :] = tile.astype(BF16)

    def batch(b, _):
        weights = columns[b]
        for j in range(BATCH):
            i = b * BATCH + j
            d, s = slot_of(classes[0, i])
            turned = align(rows[i].astype(F32), turns[0, i], offsets, parts)
            at = pl.ds(pl.multiple_of(s * ROWS, ROWS), ROWS)
            held = out[d, at, :].astype(F32)
            out[d, at, :] = (held + scale_rows(weights[:, j : j + 1], turned)).astype(BF16)
        return 0

    lax.fori_loop(0, count // BATCH, batch, 0)


def class_sums(assign, rotation, group, table, images):
    return pl.pallas_call(
        sums_kernel,
        out_shape=jax.ShapeDtypeStruct((GROUP, BAND, LANES), BF16),
        in_specs=[HBM] * 5,
        out_specs=VMEM,
        scratch_shapes=place_shapes(images.shape[0], table.shape[1]),
        compiler_params=pltpu.CompilerParams(vmem_limit_bytes=24 << 20),
        name="class_sums",
    )(assign, rotation, group, table, images)


def place_along_z():
    return lax.axis_index("cls") // 2 % STACK


def group_kernel(bands, *outs):
    here = place_along_z()
    tail = jnp.sum(bands[:, STACK * ROWS :, :].astype(F32), axis=0)
    tail = split_pair(join_pair(tail))
    for j in range(STACK):
        s = (here + j) % STACK
        for half in range(2):
            at = pl.ds(pl.multiple_of(s * ROWS + half * SHELLS, SHELLS), SHELLS)
            total = bands[0, at, :].astype(F32)
            for d in range(1, GROUP):
                total = total + bands[d, at, :].astype(F32)
            outs[j][half * SHELLS : (half + 1) * SHELLS, :] = total.astype(BF16)
        pick = lax.broadcasted_iota(jnp.int32, tail.shape, 0) == s
        row = jnp.sum(jnp.where(pick, tail, 0.0), axis=0, keepdims=True)
        outs[j][ROWS:, :] = jnp.broadcast_to(row, (TAIL, LANES)).astype(BF16)


def group_sums(bands):
    return pl.pallas_call(
        group_kernel,
        out_shape=[jax.ShapeDtypeStruct((SLAB, LANES), BF16)] * STACK,
        in_specs=[VMEM],
        out_specs=[VMEM] * STACK,
        compiler_params=pltpu.CompilerParams(vmem_limit_bytes=24 << 20),
        name="group_sums",
    )(bands)


def average_kernel(*refs):
    slabs, (avg, tail) = refs[:STACK], refs[STACK:]
    total = sum(s[...].astype(F32) for s in slabs)
    den = join_pair(total[ROWS:])
    tail[...] = split_pair(den).astype(BF16)
    column = jnp.transpose(jnp.broadcast_to(jnp.concatenate([den[:1], den[:1]], axis=1), (LANES, LANES)))
    avg[...] = (total[:ROWS] / (column + TAU)).astype(BF16)


def class_average(slabs):
    return pl.pallas_call(
        average_kernel,
        out_shape=(jax.ShapeDtypeStruct((ROWS, LANES), BF16), jax.ShapeDtypeStruct((TAIL, LANES), BF16)),
        in_specs=[VMEM] * STACK,
        out_specs=(VMEM, VMEM),
        name="class_average",
    )(*slabs)


def copies_kernel(*refs):
    here = place_along_z()
    slabs, out = refs[:STACK], refs[STACK]
    rank = lax.broadcasted_iota(jnp.int32, (TAIL, LANES), 0)
    tail = jnp.zeros((TAIL, LANES), F32)
    for j in range(STACK):
        s = (here + STACK - j) % STACK
        at = pl.ds(pl.multiple_of(s * ROWS, ROWS), ROWS)
        value = slabs[j][:ROWS, :]
        for d in range(GROUP):
            out[d, at, :] = value
        tail = jnp.where(rank == s, slabs[j][ROWS:, :].astype(F32), tail)
    for d in range(GROUP):
        out[d, STACK * ROWS :, :] = tail.astype(BF16)


def group_copies(slabs):
    return pl.pallas_call(
        copies_kernel,
        out_shape=jax.ShapeDtypeStruct((GROUP, BAND, LANES), BF16),
        in_specs=[VMEM] * STACK,
        out_specs=VMEM,
        compiler_params=pltpu.CompilerParams(vmem_limit_bytes=24 << 20),
        name="group_copies",
    )(*slabs)


def outputs_kernel(assign, rotation, group, table, images, bands, lag_ref, resid, score, lever, *scratch):
    places, (offsets, parts, columns, sems) = scratch[:6], scratch[6:10]
    held, out_sems, dens, lags, powers, energies = scratch[10:16]
    classes, turns, assign_row, group_row, local, rows = places
    count = rows.shape[0]
    copies = begin(assign, rotation, group, table, images, places, sems)
    fill_steps(offsets, parts)
    for copy in copies:
        copy.wait()
    by_shell = weights_by_shell(group_row[...], local[...])
    keep_columns(by_shell, columns)

    def leave(b):
        at = pl.ds(pl.multiple_of(b * BATCH, BATCH), BATCH)
        return pltpu.make_async_copy(held.at[at], resid.at[at], out_sems.at[b])

    def batch(b, _):
        weights = columns[b]
        for j in range(BATCH):
            i = b * BATCH + j
            d, s = slot_of(classes[0, i])
            image = rows[i]
            wide = image.astype(F32)
            turned = align(wide, turns[0, i], offsets, parts)
            avg = bands[d, pl.ds(pl.multiple_of(s * ROWS, ROWS), ROWS), :].astype(F32)
            predicted = scale_rows(weights[:, j : j + 1], avg).astype(BF16)
            back = predicted.astype(F32)
            held[i] = (turned - back).astype(BF16)
            cross = lax.dot_general(image, predicted, (((0,), (0,)), ((), ())), preferred_element_type=F32)
            lag = cross[:8]
            for r in range(8, LANES, 8):
                lag = lag + pltpu.roll(cross[r : r + 8], LANES - r, 1)
            lags[pl.ds(pl.multiple_of(i * 8, 8), 8), :] = lag
            powers[pl.ds(i, 1), :] = jnp.sum(wide * wide, axis=0, keepdims=True)
            energies[pl.ds(i, 1), :] = jnp.sum(back * back, axis=0, keepdims=True)
            tile = bands[d, STACK * ROWS :, :].astype(F32)
            pick = lax.broadcasted_iota(jnp.int32, tile.shape, 0) == s
            dens[pl.ds(i, 1), :] = jnp.sum(jnp.where(pick, tile, 0.0), axis=0, keepdims=True)
        leave(b).start()
        return 0

    lax.fori_loop(0, count // BATCH, batch, 0)
    shift = lags[pl.ds(0, count, stride=8), :]
    for r in range(1, 8):
        shift = shift + pltpu.roll(lags[pl.ds(r, count, stride=8), :], LANES - r, 1)
    raw = contract(lag_ref[...], shift, ((0,), (1,)))
    pixels = ROWS * LANES
    power = jnp.sum(jnp.transpose(powers[...]), axis=0, keepdims=True)
    energy = jnp.sum(jnp.transpose(energies[...]), axis=0, keepdims=True)
    first = jnp.sqrt(power / pixels + 1e-05)
    second = jnp.sqrt(energy / pixels + 1e-05)
    score[...] = (raw / (math.sqrt(pixels) * first * second))[:NROT].astype(BF16)
    den = jnp.transpose(join_pair(dens[...]))
    lever[...] = (jnp.sum(by_shell * by_shell / (den + TAU), axis=0, keepdims=True) / SHELLS).astype(BF16)

    def finish(b, _):
        leave(b).wait()
        return 0

    lax.fori_loop(0, count // BATCH, finish, 0)


def particle_outputs(assign, rotation, group, table, images, bands):
    count = images.shape[0]
    per_particle = pltpu.VMEM((count, LANES), F32)
    return pl.pallas_call(
        outputs_kernel,
        out_shape=(
            jax.ShapeDtypeStruct(images.shape, BF16),
            jax.ShapeDtypeStruct((NROT, count), BF16),
            jax.ShapeDtypeStruct((1, count), BF16),
        ),
        in_specs=[HBM] * 5 + [VMEM] * 2,
        out_specs=(HBM, VMEM, VMEM),
        scratch_shapes=place_shapes(count, table.shape[1])
        + [
            pltpu.VMEM((count, ROWS, LANES), BF16),
            pltpu.SemaphoreType.DMA((count // BATCH,)),
            per_particle,
            pltpu.VMEM((count * 8, LANES), F32),
            per_particle,
            per_particle,
        ],
        compiler_params=pltpu.CompilerParams(vmem_limit_bytes=24 << 20),
        name="particle_outputs",
    )(assign, rotation, group, table, images, bands, jnp.asarray(lag_matrix()))


def exchange(value):
    chips = np.arange(CLASSES).reshape(GROUP // 2, STACK, 2)
    groups = [chips[:, k, :].reshape(-1).tolist() for k in range(STACK)]
    return lax.all_to_all(value, "cls", split_axis=0, concat_axis=0, tiled=True, axis_index_groups=groups)


def upward(chip, steps):
    return chip // DEPTH * DEPTH + (chip + 2 * steps) % DEPTH


def shift(value, steps):
    return lax.ppermute(value, "cls", [(i, upward(i, steps)) for i in range(CLASSES)])


def body(particles, assign, rotation, group, ctf):
    common = [pltpu.with_memory_space_constraint(x, pltpu.HBM) for x in (assign, rotation, group, ctf.T, particles[0])]
    pieces = group_sums(exchange(class_sums(*common)))
    average, tail = class_average([pieces[0]] + [shift(pieces[j], j) for j in range(1, STACK)])
    partner = lax.ppermute(average, "half", [(0, 1), (1, 0)])
    packed = jnp.concatenate([partner, tail], axis=0)
    bands = exchange(group_copies([packed] + [shift(packed, j) for j in range(1, STACK)]))
    residual, scores, leverage = particle_outputs(*common, bands)
    return (average[None, None], residual[None], scores.T[None], leverage)


def solution(mesh):
    in_specs = (
        P("half", "cls", None, None),
        P("half", "cls"),
        P("half", "cls"),
        P("half", "cls"),
        P(),
    )
    out_specs = (
        P("half", "cls", None, None),
        P("half", "cls", None, None),
        P("half", "cls", None),
        P("half", "cls"),
    )
    return jax.shard_map(body, mesh=mesh, in_specs=in_specs, out_specs=out_specs, check_vma=False)
```

time: 195 us -> 171 us (0.88)
  blocking collectives: 0 us -> 116 us
  starting transfers between devices: 89.1 us -> 18.4 us
  waiting for transfers between devices: 49.2 us -> 8.32 us
  Pallas kernels: 42.2 us -> 25 us
  local copies, waits for them, and re-layouts: 12.1 us -> 1.92 us
    all_to_all x0 -> x2, blocking collectives: none -> 116 us  [exchange(): lax.all_to_all(value, 'cls', split_axis=0, concat_axis=0, tiled=True, axi...]
    ppermute x31 -> x7, starting transfers between devices: 63 us -> 18.4 us  [the longest x6 15.2 us: shift(): lax.ppermute(value, 'cls', [(i, upward(i, steps)) for i in range(CLASSES)])]
    all_to_all x4 -> x0, waiting for transfers between devices: 40.1 us -> none  [across(): lax.all_to_all(value, 'cls', split_axis=0, concat_axis=0, tiled=True, axi...]
    all_to_all x4 -> x0, starting transfers between devices: 26.1 us -> none  [across(): lax.all_to_all(value, 'cls', split_axis=0, concat_axis=0, tiled=True, axi...]
    pallas_call x10 -> x5, Pallas kernels: 42.2 us -> 25 us  [the longest x1 15 us: particle_outputs(): pl.pallas_call(outputs_kernel, out_shape=(jax.ShapeDtypeStruct(images.sha...]
    unnamed x70 -> x11, local copies, waits for them, and re-layouts: 12.1 us -> 1.23 us
    ppermute x31 -> x7, waiting for transfers between devices: 9.09 us -> 8.32 us  [the longest x6 7.25 us: shift(): lax.ppermute(value, 'cls', [(i, upward(i, steps)) for i in range(CLASSES)])]
  transfers between devices with their start and end apart: 35 -> 7, of which waited for: 9 -> 4; matrix products, arithmetic and copies ran while one was open for 0% -> 0% of each run, Pallas kernels for 13% -> 0%
where the time goes in v3:
time: 171 us; the launch traced here: 170 us
  blocking collectives  116 us (68%)
  Pallas kernels  25 us (15%)
  starting transfers between devices  18.4 us (11%)
  waiting for transfers between devices  8.32 us (5%)
  local copies, waits for them, and re-layouts  1.92 us (1%)
    all_to_all x2, blocking collectives, exchange(): lax.all_to_all(value, 'cls', split_axis=0, concat_axis=0, tiled=True, axi...  116 us
    ppermute x6, starting transfers between devices, shift(): lax.ppermute(value, 'cls', [(i, upward(i, steps)) for i in range(CLASSES)])  15.2 us
    pallas_call x1, Pallas kernels, particle_outputs(): pl.pallas_call(outputs_kernel, out_shape=(jax.ShapeDtypeStruct(images.sha...  15 us
    ppermute x6, waiting for transfers between devices, shift(): lax.ppermute(value, 'cls', [(i, upward(i, steps)) for i in range(CLASSES)])  7.25 us
    pallas_call x1, Pallas kernels, class_sums(): pl.pallas_call(sums_kernel, out_shape=jax.ShapeDtypeStruct((GROUP, BAND,...  7.12 us
  transfers between devices with their start and end apart: 7, of which 4 were waited for; matrix products, arithmetic and copies ran while one was open for 0% of the time, Pallas kernels for 0%

profile of v3, /device:TPU:1, one launch (start us, length us, event | category | flops | bytes accessed | tf_op | source)
XLA Modules:
  0.0 169.9 jit_solution(16735249414057507051)
XLA Ops:
  0.6 7.1 %class_sums.1 = bf16[32,528,128]{2,1,0:T(8,128)(2,1)S(1)} custom-call(s32[1,64]{1,0:T(1,128)} %assign.3, s32[1,64]{1,0:T(1,128)} %rotation.3, s32[1,64]{1,0:T(1,128)} %group.3, f32[64,256]{1,0:T(8,128)} %bitcast.9, bf16[64,128,128]{2,1,0:T(8,128)(2,1)} %bitcast.7), custom_call_target="tpu_custom_call" | custom-call | tf_op jit(solution)/shard_map/class_sums/pallas_call | solution.py:162
  7.8 61.1 %all_to_all.10.bands = bf16[32,528,128]{2,1,0:T(8,128)(2,1)S(1)} all-to-all(bf16[32,528,128]{2,1,0:T(8,128)(2,1)S(1)} %class_sums.1), channel_id=1, replica_groups={{0,1,8,9,16,17,24,25,32,33,40,41,48,49,56,57,64,65,72,73,80,81,88,89,96..., dimensions={0} | all-to-all | bytes 8650752 | tf_op jit(solution)/shard_map/all_to_all | solution.py:342
  68.9 0.6 group_sums.1
  69.5 0.0 copy-start.1
  69.5 0.6 copy-done.1
  70.1 3.0 %collective-permute-start = (bf16[144,128]{1,0:T(8,128)(2,1)S(1)}, bf16[144,128]{1,0:T(8,128)(2,1)S(1)}, u32[]{:S(2)}, u32[]{:S(2)}) collective-permute-start(bf16[144,128]{1,0:T(8,128)(2,1)S(1)} %get-tuple-element.14), channel_id=1, source_target_pairs={{0,2},{1,3},{2,4},{3,5},{4,6},{5,7},{6,0},{7,1},{8,10},{9,11},{10,... | collective-permute-start | bytes 110600 | tf_op jit(solution)/shard_map/ppermute | solution.py:350
  73.1 4.2 %collective-permute-start.1 = (bf16[144,128]{1,0:T(8,128)(2,1)S(1)}, bf16[144,128]{1,0:T(8,128)(2,1)S(1)}, u32[]{:S(2)}, u32[]{:S(2)}) collective-permute-start(bf16[144,128]{1,0:T(8,128)(2,1)S(1)} %get-tuple-element.15), channel_id=1, source_target_pairs={{0,4},{1,5},{2,6},{3,7},{4,0},{5,1},{6,2},{7,3},{8,12},{9,13},{10,... | collective-permute-start | bytes 110600 | tf_op jit(solution)/shard_map/ppermute | solution.py:350
  77.3 2.4 %collective-permute-start.2 = (bf16[144,128]{1,0:T(8,128)(2,1)S(1)}, bf16[144,128]{1,0:T(8,128)(2,1)S(1)}, u32[]{:S(2)}, u32[]{:S(2)}) collective-permute-start(bf16[144,128]{1,0:T(8,128)(2,1)S(1)} %get-tuple-element.16), channel_id=1, source_target_pairs={{0,6},{1,7},{2,0},{3,1},{4,2},{5,3},{6,4},{7,5},{8,14},{9,15},{10,... | collective-permute-start | bytes 110600 | tf_op jit(solution)/shard_map/ppermute | solution.py:350
  79.7 0.0 collective-permute-done.refs_1_
  79.7 0.1 collective-permute-done.1.refs_2_
  79.8 2.3 %collective-permute-done.2.refs_3_ = bf16[144,128]{1,0:T(8,128)(2,1)S(1)} collective-permute-done((bf16[144,128]{1,0:T(8,128)(2,1)S(1)}, bf16[144,128]{1,0:T(8,128)(2,1)S(1)}, u32[]{:S(2)}, u32[]{:S(2)}) %collective-permute-start.2) | collective-permute-done | bytes 36896 | tf_op jit(solution)/shard_map/ppermute | solution.py:350
  82.1 0.6 copy-done.4
  82.7 1.7 class_average.1
  84.4 3.3 %collective-permute-start.3 = (bf16[128,128]{1,0:T(8,128)(2,1)}, bf16[128,128]{1,0:T(8,128)(2,1)S(1)}, u32[]{:S(2)}, u32[]{:S(2)}) collective-permute-start(bf16[128,128]{1,0:T(8,128)(2,1)} %get-tuple-element.17), channel_id=1, source_target_pairs={{0,128},{128,0},{1,129},{129,1},{2,130},{130,2},{3,131},{131,3},{4... | collective-permute-start | bytes 98312 | tf_op jit(solution)/shard_map/ppermute | solution.py:357
  87.7 1.1 collective-permute-done.3
  88.7 0.7 constant_dynamic-update-slice_fusion.refs_0_
  89.4 3.5 %collective-permute-start.6 = (bf16[144,128]{1,0:T(8,128)(2,1)S(1)}, bf16[144,128]{1,0:T(8,128)(2,1)S(1)}, u32[]{:S(2)}, u32[]{:S(2)}) collective-permute-start(bf16[144,128]{1,0:T(8,128)(2,1)S(1)} %constant_dynamic-update-slice_fusion.refs_0_), channel_id=1, source_target_pairs={{0,6},{1,7},{2,0},{3,1},{4,2},{5,3},{6,4},{7,5},{8,14},{9,15},{10,... | collective-permute-start | bytes 110600 | tf_op jit(solution)/shard_map/ppermute | solution.py:350
  92.9 1.2 collective-permute-start.5
  94.1 0.9 collective-permute-start.4
  95.0 4.8 %collective-permute-done.5.refs_2_ = bf16[144,128]{1,0:T(8,128)(2,1)S(1)} collective-permute-done((bf16[144,128]{1,0:T(8,128)(2,1)S(1)}, bf16[144,128]{1,0:T(8,128)(2,1)S(1)}, u32[]{:S(2)}, u32[]{:S(2)}) %collective-permute-start.5) | collective-permute-done | bytes 36896 | tf_op jit(solution)/shard_map/ppermute | solution.py:350
  99.9 0.6 group_copies.1
  100.4 0.0 copy-start
  100.4 54.4 %all_to_all.11.bands = bf16[32,528,128]{2,1,0:T(8,128)(2,1)S(1)} all-to-all(bf16[32,528,128]{2,1,0:T(8,128)(2,1)S(1)} %group_copies.1), channel_id=1, replica_groups={{0,1,8,9,16,17,24,25,32,33,40,41,48,49,56,57,64,65,72,73,80,81,88,89,96..., dimensions={0} | all-to-all | bytes 8650752 | tf_op jit(solution)/shard_map/all_to_all | solution.py:342
  154.8 15.0 %particle_outputs.1 = (bf16[64,128,128]{2,1,0:T(8,128)(2,1)}, bf16[36,64]{1,0:T(8,128)(2,1)}, bf16[1,64]{1,0:T(2,128)(2,1)}) custom-call(s32[1,64]{1,0:T(1,128)} %assign.3, s32[1,64]{1,0:T(1,128)} %rotation.3, s32[1,64]{1,0:T(1,128)} %group.3, f32[64,256]{1,0:T(8,128)} %bitcast.10, bf16[64,128,128]{2,1,0:T(8,128)(2,1)} %bitcast.8, ...), custom_call_target="tpu_custom_call" | custom-call | tf_op jit(solution)/shard_map/particle_outputs/pallas_call | solution.py:316
  (9 shorter events, 0.0 us)
Async XLA Ops:
  69.5 0.6 copy-start.1
  70.1 9.6 %collective-permute-start = (bf16[144,128]{1,0:T(8,128)(2,1)S(1)}, bf16[144,128]{1,0:T(8,128)(2,1)S(1)}, u32[]{:S(2)}, u32[]{:S(2)}) collective-permute-start(bf16[144,128]{1,0:T(8,128)(2,1)S(1)} %get-tuple-element.14), channel_id=1, source_target_pairs={{0,2},{1,3},{2,4},{3,5},{4,6},{5,7},{6,0},{7,1},{8,10},{9,11},{10,... | collective-permute-start | bytes 110600 | tf_op jit(solution)/shard_map/ppermute | solution.py:350
  73.1 6.7 %collective-permute-start.1 = (bf16[144,128]{1,0:T(8,128)(2,1)S(1)}, bf16[144,128]{1,0:T(8,128)(2,1)S(1)}, u32[]{:S(2)}, u32[]{:S(2)}) collective-permute-start(bf16[144,128]{1,0:T(8,128)(2,1)S(1)} %get-tuple-element.15), channel_id=1, source_target_pairs={{0,4},{1,5},{2,6},{3,7},{4,0},{5,1},{6,2},{7,3},{8,12},{9,13},{10,... | collective-permute-start | bytes 110600 | tf_op jit(solution)/shard_map/ppermute | solution.py:350
  77.3 4.8 %collective-permute-start.2 = (bf16[144,128]{1,0:T(8,128)(2,1)S(1)}, bf16[144,128]{1,0:T(8,128)(2,1)S(1)}, u32[]{:S(2)}, u32[]{:S(2)}) collective-permute-start(bf16[144,128]{1,0:T(8,128)(2,1)S(1)} %get-tuple-element.16), channel_id=1, source_target_pairs={{0,6},{1,7},{2,0},{3,1},{4,2},{5,3},{6,4},{7,5},{8,14},{9,15},{10,... | collective-permute-start | bytes 110600 | tf_op jit(solution)/shard_map/ppermute | solution.py:350
  79.7 2.4 %copy-start.2 = (bf16[144,128]{1,0:T(8,128)(2,1)}, bf16[144,128]{1,0:T(8,128)(2,1)S(1)}, u32[]{:S(2)}) copy-start(bf16[144,128]{1,0:T(8,128)(2,1)S(1)} %collective-permute-done.refs_1_) | copy-start | bytes 110596
  79.8 2.3 %copy-start.3 = (bf16[144,128]{1,0:T(8,128)(2,1)}, bf16[144,128]{1,0:T(8,128)(2,1)S(1)}, u32[]{:S(2)}) copy-start(bf16[144,128]{1,0:T(8,128)(2,1)S(1)} %collective-permute-done.1.refs_2_) | copy-start | bytes 110596
  82.1 0.6 copy-start.4
  84.4 4.3 %collective-permute-start.3 = (bf16[128,128]{1,0:T(8,128)(2,1)}, bf16[128,128]{1,0:T(8,128)(2,1)S(1)}, u32[]{:S(2)}, u32[]{:S(2)}) collective-permute-start(bf16[128,128]{1,0:T(8,128)(2,1)} %get-tuple-element.17), channel_id=1, source_target_pairs={{0,128},{128,0},{1,129},{129,1},{2,130},{130,2},{3,131},{131,3},{4... | collective-permute-start | bytes 98312 | tf_op jit(solution)/shard_map/ppermute | solution.py:357
  89.4 5.6 %collective-permute-start.6 = (bf16[144,128]{1,0:T(8,128)(2,1)S(1)}, bf16[144,128]{1,0:T(8,128)(2,1)S(1)}, u32[]{:S(2)}, u32[]{:S(2)}) collective-permute-start(bf16[144,128]{1,0:T(8,128)(2,1)S(1)} %constant_dynamic-update-slice_fusion.refs_0_), channel_id=1, source_target_pairs={{0,6},{1,7},{2,0},{3,1},{4,2},{5,3},{6,4},{7,5},{8,14},{9,15},{10,... | collective-permute-start | bytes 110600 | tf_op jit(solution)/shard_map/ppermute | solution.py:350
  92.9 6.9 %collective-permute-start.5 = (bf16[144,128]{1,0:T(8,128)(2,1)S(1)}, bf16[144,128]{1,0:T(8,128)(2,1)S(1)}, u32[]{:S(2)}, u32[]{:S(2)}) collective-permute-start(bf16[144,128]{1,0:T(8,128)(2,1)S(1)} %constant_dynamic-update-slice_fusion.refs_0_), channel_id=1, source_target_pairs={{0,4},{1,5},{2,6},{3,7},{4,0},{5,1},{6,2},{7,3},{8,12},{9,13},{10,... | collective-permute-start | bytes 110600 | tf_op jit(solution)/shard_map/ppermute | solution.py:350
  94.1 5.8 %collective-permute-start.4 = (bf16[144,128]{1,0:T(8,128)(2,1)S(1)}, bf16[144,128]{1,0:T(8,128)(2,1)S(1)}, u32[]{:S(2)}, u32[]{:S(2)}) collective-permute-start(bf16[144,128]{1,0:T(8,128)(2,1)S(1)} %constant_dynamic-update-slice_fusion.refs_0_), channel_id=1, source_target_pairs={{0,2},{1,3},{2,4},{3,5},{4,6},{5,7},{6,0},{7,1},{8,10},{9,11},{10,... | collective-permute-start | bytes 110600 | tf_op jit(solution)/shard_map/ppermute | solution.py:350
  100.4 54.4 %copy-start = (f32[128,128]{1,0:T(8,128)S(1)}, f32[128,128]{1,0:T(8,128)}, u32[]{:S(2)}) copy-start(f32[128,128]{1,0:T(8,128)} %constant.2.clone.lag_ref) | copy-start | bytes 196612

commit v4 on v3

--- a/solution.py
+++ b/solution.py
@@ -27,6 +27,7 @@
 
 HBM = pl.BlockSpec(memory_space=pltpu.HBM)
 VMEM = pl.BlockSpec(memory_space=pltpu.VMEM)
+SMEM = pl.BlockSpec(memory_space=pltpu.SMEM)
 
 
 def rotation_steps():
@@ -47,12 +48,14 @@
     return out
 
 
-def fill_steps(offsets, parts):
+def rotation_matrices():
     offset, keep, carry = rotation_steps()
+    out = np.zeros((NROT, LANES, LANES), np.float32)
+    t = np.arange(LANES)
     for r in range(NROT):
-        offsets[r] = jnp.int32(int(offset[r]))
-        parts[0, r] = jnp.float32(float(keep[r]))
-        parts[1, r] = jnp.float32(float(carry[r]))
+        out[r, (t - offset[r]) % LANES, t] += keep[r]
+        out[r, (t - offset[r] - 1) % LANES, t] += carry[r]
+    return out.astype(BF16)
 
 
 def contract(left, right, dims):
@@ -74,10 +77,8 @@
     return pair[:, : LANES // 2] + pair[:, LANES // 2 :]
 
 
-def align(image, turn, offsets, parts):
-    first = pltpu.roll(image, offsets[turn], 1)
-    second = pltpu.roll(first, 1, 1)
-    return parts[0, turn] * first + parts[1, turn] * second
+def align(image, turn, rots):
+    return jnp.dot(image, rots[turn], preferred_element_type=F32)
 
 
 def keep_columns(by_shell, columns):
@@ -89,49 +90,28 @@
     return (c // DEPTH) * 2 + c % 2, (c // 2) % STACK
 
 
-def begin(assign, rotation, group, table, images, places, sems):
-    classes, turns, assign_row, group_row, local, rows = places
-    copies = [
-        pltpu.make_async_copy(images, rows, sems.at[0]),
-        pltpu.make_async_copy(group, group_row, sems.at[1]),
-        pltpu.make_async_copy(table, local, sems.at[2]),
-        pltpu.make_async_copy(assign, assign_row, sems.at[3]),
-        pltpu.make_async_copy(assign, classes, sems.at[4]),
-        pltpu.make_async_copy(rotation, turns, sems.at[5]),
+def scale_rows(column, value):
+    return jnp.concatenate([column * value[:SHELLS], column * value[SHELLS:]], axis=0)
+
+
+def sums_kernel(assign, rotation, group, table, images, rotations, out, *scratch):
+    classes, turns, assign_row, group_row, local, rows, rots, columns, sems = scratch
+    count = rows.shape[0]
+    moves = [
+        (images, rows),
+        (rotations, rots),
+        (table, local),
+        (group, group_row),
+        (assign, assign_row),
+        (assign, classes),
+        (rotation, turns),
     ]
+    copies = [pltpu.make_async_copy(source, target, sems.at[n]) for n, (source, target) in enumerate(moves)]
     for copy in copies:
         copy.start()
-    return copies
-
-
-def place_shapes(count, groups):
-    return [
-        pltpu.SMEM((1, count), jnp.int32),
-        pltpu.SMEM((1, count), jnp.int32),
-        pltpu.VMEM((1, count), jnp.int32),
-        pltpu.VMEM((1, count), jnp.int32),
-        pltpu.VMEM((SHELLS, groups), F32),
-        pltpu.VMEM((count, ROWS, LANES), BF16),
-        pltpu.SMEM((NROT,), jnp.int32),
-        pltpu.SMEM((2, NROT), F32),
-        pltpu.VMEM((count // BATCH, SHELLS, LANES), F32),
-        pltpu.SemaphoreType.DMA((6,)),
-    ]
-
-
-def scale_rows(column, value):
-    return jnp.concatenate([column * value[:SHELLS], column * value[SHELLS:]], axis=0)
-
-
-def sums_kernel(assign, rotation, group, table, images, out, *scratch):
-    places, (offsets, parts, columns, sems) = scratch[:6], scratch[6:10]
-    classes, turns, assign_row, group_row, local, rows = places
-    count = rows.shape[0]
-    copies = begin(assign, rotation, group, table, images, places, sems)
-    fill_steps(offsets, parts)
     for d in range(GROUP):
         out[d, : STACK * ROWS, :] = jnp.zeros((STACK * ROWS, LANES), BF16)
-    for copy in copies:
+    for copy in copies[2:]:
         copy.wait()
     by_shell = weights_by_shell(group_row[...], local[...])
     keep_columns(by_shell, columns)
@@ -144,12 +124,15 @@
         tile = jnp.concatenate([pair[d * STACK : (d + 1) * STACK], blank], axis=0)
         out[d, STACK * ROWS :, :] = tile.astype(BF16)
 
+    for copy in copies[:2]:
+        copy.wait()
+
     def batch(b, _):
         weights = columns[b]
         for j in range(BATCH):
             i = b * BATCH + j
             d, s = slot_of(classes[0, i])
-            turned = align(rows[i].astype(F32), turns[0, i], offsets, parts)
+            turned = align(rows[i], turns[0, i], rots)
             at = pl.ds(pl.multiple_of(s * ROWS, ROWS), ROWS)
             held = out[d, at, :].astype(F32)
             out[d, at, :] = (held + scale_rows(weights[:, j : j + 1], turned)).astype(BF16)
@@ -158,16 +141,27 @@
     lax.fori_loop(0, count // BATCH, batch, 0)
 
 
-def class_sums(assign, rotation, group, table, images):
+def class_sums(assign, rotation, group, table, images, rotations):
+    count, groups = images.shape[0], table.shape[1]
     return pl.pallas_call(
         sums_kernel,
         out_shape=jax.ShapeDtypeStruct((GROUP, BAND, LANES), BF16),
-        in_specs=[HBM] * 5,
+        in_specs=[HBM] * 6,
         out_specs=VMEM,
-        scratch_shapes=place_shapes(images.shape[0], table.shape[1]),
+        scratch_shapes=[
+            pltpu.SMEM((1, count), jnp.int32),
+            pltpu.SMEM((1, count), jnp.int32),
+            pltpu.VMEM((1, count), jnp.int32),
+            pltpu.VMEM((1, count), jnp.int32),
+            pltpu.VMEM((SHELLS, groups), F32),
+            pltpu.VMEM((count, ROWS, LANES), BF16),
+            pltpu.VMEM((NROT, LANES, LANES), BF16),
+            pltpu.VMEM((count // BATCH, SHELLS, LANES), F32),
+            pltpu.SemaphoreType.DMA((7,)),
+        ],
         compiler_params=pltpu.CompilerParams(vmem_limit_bytes=24 << 20),
         name="class_sums",
-    )(assign, rotation, group, table, images)
+    )(assign, rotation, group, table, images, rotations)
 
 
 def place_along_z():
@@ -186,9 +180,7 @@
             for d in range(1, GROUP):
                 total = total + bands[d, at, :].astype(F32)
             outs[j][half * SHELLS : (half + 1) * SHELLS, :] = total.astype(BF16)
-        pick = lax.broadcasted_iota(jnp.int32, tail.shape, 0) == s
-        row = jnp.sum(jnp.where(pick, tail, 0.0), axis=0, keepdims=True)
-        outs[j][ROWS:, :] = jnp.broadcast_to(row, (TAIL, LANES)).astype(BF16)
+        outs[j][ROWS:, :] = tail.astype(BF16)
 
 
 def group_sums(bands):
@@ -207,7 +199,9 @@
     total = sum(s[...].astype(F32) for s in slabs)
     den = join_pair(total[ROWS:])
     tail[...] = split_pair(den).astype(BF16)
-    column = jnp.transpose(jnp.broadcast_to(jnp.concatenate([den[:1], den[:1]], axis=1), (LANES, LANES)))
+    here = lax.broadcasted_iota(jnp.int32, den.shape, 0) == place_along_z()
+    den = jnp.sum(jnp.where(here, den, 0.0), axis=0, keepdims=True)
+    column = jnp.transpose(jnp.broadcast_to(jnp.concatenate([den, den], axis=1), (LANES, LANES)))
     avg[...] = (total[:ROWS] / (column + TAU)).astype(BF16)
 
 
@@ -217,47 +211,40 @@
         out_shape=(jax.ShapeDtypeStruct((ROWS, LANES), BF16), jax.ShapeDtypeStruct((TAIL, LANES), BF16)),
         in_specs=[VMEM] * STACK,
         out_specs=(VMEM, VMEM),
+        compiler_params=pltpu.CompilerParams(vmem_limit_bytes=4 << 20),
         name="class_average",
     )(*slabs)
 
 
-def copies_kernel(*refs):
+def copies_kernel(tail, *refs):
+    slabs, out = refs[:STACK], refs[STACK]
     here = place_along_z()
-    slabs, out = refs[:STACK], refs[STACK]
-    rank = lax.broadcasted_iota(jnp.int32, (TAIL, LANES), 0)
-    tail = jnp.zeros((TAIL, LANES), F32)
     for j in range(STACK):
         s = (here + STACK - j) % STACK
         at = pl.ds(pl.multiple_of(s * ROWS, ROWS), ROWS)
-        value = slabs[j][:ROWS, :]
+        value = slabs[j][...]
         for d in range(GROUP):
             out[d, at, :] = value
-        tail = jnp.where(rank == s, slabs[j][ROWS:, :].astype(F32), tail)
+    value = tail[...]
     for d in range(GROUP):
-        out[d, STACK * ROWS :, :] = tail.astype(BF16)
-
-
-def group_copies(slabs):
+        out[d, STACK * ROWS :, :] = value
+
+
+def group_copies(tail, slabs):
     return pl.pallas_call(
         copies_kernel,
         out_shape=jax.ShapeDtypeStruct((GROUP, BAND, LANES), BF16),
-        in_specs=[VMEM] * STACK,
+        in_specs=[VMEM] * (STACK + 1),
         out_specs=VMEM,
         compiler_params=pltpu.CompilerParams(vmem_limit_bytes=24 << 20),
         name="group_copies",
-    )(*slabs)
-
-
-def outputs_kernel(assign, rotation, group, table, images, bands, lag_ref, resid, score, lever, *scratch):
-    places, (offsets, parts, columns, sems) = scratch[:6], scratch[6:10]
-    held, out_sems, dens, lags, powers, energies = scratch[10:16]
-    classes, turns, assign_row, group_row, local, rows = places
+    )(tail, *slabs)
+
+
+def outputs_kernel(classes, turns, group_row, table, rows, rots, bands, lag_ref, resid, score, lever, *scratch):
+    columns, held, out_sems, dens, lags, powers, energies = scratch
     count = rows.shape[0]
-    copies = begin(assign, rotation, group, table, images, places, sems)
-    fill_steps(offsets, parts)
-    for copy in copies:
-        copy.wait()
-    by_shell = weights_by_shell(group_row[...], local[...])
+    by_shell = weights_by_shell(group_row[...], table[...])
     keep_columns(by_shell, columns)
 
     def leave(b):
@@ -271,7 +258,7 @@
             d, s = slot_of(classes[0, i])
             image = rows[i]
             wide = image.astype(F32)
-            turned = align(wide, turns[0, i], offsets, parts)
+            turned = align(image, turns[0, i], rots)
             avg = bands[d, pl.ds(pl.multiple_of(s * ROWS, ROWS), ROWS), :].astype(F32)
             predicted = scale_rows(weights[:, j : j + 1], avg).astype(BF16)
             back = predicted.astype(F32)
@@ -310,7 +297,7 @@
     lax.fori_loop(0, count // BATCH, finish, 0)
 
 
-def particle_outputs(assign, rotation, group, table, images, bands):
+def particle_outputs(assign, rotation, group, table, images, rotations, bands):
     count = images.shape[0]
     per_particle = pltpu.VMEM((count, LANES), F32)
     return pl.pallas_call(
@@ -320,10 +307,10 @@
             jax.ShapeDtypeStruct((NROT, count), BF16),
             jax.ShapeDtypeStruct((1, count), BF16),
         ),
-        in_specs=[HBM] * 5 + [VMEM] * 2,
+        in_specs=[SMEM] * 2 + [VMEM] * 6,
         out_specs=(HBM, VMEM, VMEM),
-        scratch_shapes=place_shapes(count, table.shape[1])
-        + [
+        scratch_shapes=[
+            pltpu.VMEM((count // BATCH, SHELLS, LANES), F32),
             pltpu.VMEM((count, ROWS, LANES), BF16),
             pltpu.SemaphoreType.DMA((count // BATCH,)),
             per_particle,
@@ -333,7 +320,7 @@
         ],
         compiler_params=pltpu.CompilerParams(vmem_limit_bytes=24 << 20),
         name="particle_outputs",
-    )(assign, rotation, group, table, images, bands, jnp.asarray(lag_matrix()))
+    )(assign, rotation, group, table, images, rotations, bands, jnp.asarray(lag_matrix()))
 
 
 def exchange(value):
@@ -350,14 +337,18 @@
     return lax.ppermute(value, "cls", [(i, upward(i, steps)) for i in range(CLASSES)])
 
 
+def cross(value, steps):
+    pairs = [(h * CLASSES + i, (1 - h) * CLASSES + upward(i, steps)) for h in range(2) for i in range(CLASSES)]
+    return lax.ppermute(value, ("half", "cls"), pairs)
+
+
 def body(particles, assign, rotation, group, ctf):
-    common = [pltpu.with_memory_space_constraint(x, pltpu.HBM) for x in (assign, rotation, group, ctf.T, particles[0])]
-    pieces = group_sums(exchange(class_sums(*common)))
+    operands = (assign, rotation, group, ctf.T, particles[0], jnp.asarray(rotation_matrices()))
+    pinned = [pltpu.with_memory_space_constraint(x, pltpu.HBM) for x in operands]
+    pieces = group_sums(exchange(class_sums(*pinned)))
     average, tail = class_average([pieces[0]] + [shift(pieces[j], j) for j in range(1, STACK)])
-    partner = lax.ppermute(average, "half", [(0, 1), (1, 0)])
-    packed = jnp.concatenate([partner, tail], axis=0)
-    bands = exchange(group_copies([packed] + [shift(packed, j) for j in range(1, STACK)]))
-    residual, scores, leverage = particle_outputs(*common, bands)
+    bands = exchange(group_copies(tail, [cross(average, j) for j in range(STACK)]))
+    residual, scores, leverage = particle_outputs(*operands, bands)
     return (average[None, None], residual[None], scores.T[None], leverage)
 
 

time: 171 us -> 161 us (0.942)
  Pallas kernels: 25 us -> 13.1 us
  blocking collectives: 116 us -> 120 us
  local copies, waits for them, and re-layouts: 1.92 us -> 0.05 us
    pallas_call x1, Pallas kernels: 15 us -> 6.61 us  [particle_outputs(): pl.pallas_call(outputs_kernel, out_shape=(jax.ShapeDtypeStruct(images.sha...]
    ppermute x1 -> x4, starting transfers between devices: 3.25 us -> 9.39 us  [cross(): return lax.ppermute(value, ('half', 'cls'), pairs)]
    ppermute x6 -> x3, starting transfers between devices: 15.2 us -> 9.67 us  [shift(): lax.ppermute(value, 'cls', [(i, upward(i, steps)) for i in range(CLASSES)])]
    ppermute x6 -> x3, waiting for transfers between devices: 7.25 us -> 2.12 us  [shift(): lax.ppermute(value, 'cls', [(i, upward(i, steps)) for i in range(CLASSES)])]
    all_to_all x2, blocking collectives: 116 us -> 120 us  [exchange(): lax.all_to_all(value, 'cls', split_axis=0, concat_axis=0, tiled=True, axi...]
    ppermute x1 -> x4, waiting for transfers between devices: 1.07 us -> 5.18 us  [cross(): return lax.ppermute(value, ('half', 'cls'), pairs)]
    pallas_call x1, Pallas kernels: 7.12 us -> 4.45 us  [class_sums(): pl.pallas_call(sums_kernel, out_shape=jax.ShapeDtypeStruct((GROUP, BAND,...]
  transfers between devices with their start and end apart: 7 -> 7, of which waited for: 4 -> 3; matrix products, arithmetic and copies ran while one was open for 0% -> 0% of each run, Pallas kernels for 0% -> 0%
where the time goes in v4:
time: 161 us
  blocking collectives  120 us (75%)
  starting transfers between devices  19.1 us (12%)
  Pallas kernels  13.1 us (8%)
  waiting for transfers between devices  7.3 us (5%)
    all_to_all x2, blocking collectives, exchange(): lax.all_to_all(value, 'cls', split_axis=0, concat_axis=0, tiled=True, axi...  120 us
    ppermute x3, starting transfers between devices, shift(): lax.ppermute(value, 'cls', [(i, upward(i, steps)) for i in range(CLASSES)])  9.67 us
    ppermute x4, starting transfers between devices, cross(): return lax.ppermute(value, ('half', 'cls'), pairs)  9.39 us
    pallas_call x1, Pallas kernels, particle_outputs(): pl.pallas_call(outputs_kernel, out_shape=(jax.ShapeDtypeStruct(images.sha...  6.61 us
    ppermute x4, waiting for transfers between devices, cross(): return lax.ppermute(value, ('half', 'cls'), pairs)  5.18 us
    pallas_call x1, Pallas kernels, class_sums(): pl.pallas_call(sums_kernel, out_shape=jax.ShapeDtypeStruct((GROUP, BAND,...  4.45 us
  transfers between devices with their start and end apart: 7, of which 3 were waited for; matrix products, arithmetic and copies ran while one was open for 0% of the time, Pallas kernels for 0%

profile of v4, /device:TPU:1, one launch (start us, length us, event | category | flops | bytes accessed | tf_op | source)
XLA Modules:
  0.0 160.6 jit_solution(11354513586056575123)
XLA Ops:
  0.6 4.5 %class_sums.1 = bf16[32,528,128]{2,1,0:T(8,128)(2,1)S(1)} custom-call(s32[1,64]{1,0:T(1,128)} %classes.1, s32[1,64]{1,0:T(1,128)} %turns.1, s32[1,64]{1,0:T(1,128)} %group_row.1, f32[64,256]{1,0:T(8,128)} %bitcast.9, bf16[64,128,128]{2,1,0:T(8,128)(2,1)} %bitcast.7, bf16[36,128,128]{2,1,0:T(8,128)(2,1)} %constant.4.clone.rotations.rots), custom_call_target="tpu_custom_call" | custom-call | tf_op jit(solution)/shard_map/class_sums/pallas_call | solution.py:146
  5.1 61.1 %all_to_all.10.bands = bf16[32,528,128]{2,1,0:T(8,128)(2,1)S(1)} all-to-all(bf16[32,528,128]{2,1,0:T(8,128)(2,1)S(1)} %class_sums.1), channel_id=1, replica_groups={{0,1,8,9,16,17,24,25,32,33,40,41,48,49,56,57,64,65,72,73,80,81,88,89,96..., dimensions={0} | all-to-all | bytes 8650752 | tf_op jit(solution)/shard_map/all_to_all | solution.py:329
  66.2 0.6 group_sums.1
  66.8 3.1 %collective-permute-start = (bf16[144,128]{1,0:T(8,128)(2,1)S(1)}, bf16[144,128]{1,0:T(8,128)(2,1)S(1)}, u32[]{:S(2)}, u32[]{:S(2)}) collective-permute-start(bf16[144,128]{1,0:T(8,128)(2,1)S(1)} %get-tuple-element.14), channel_id=1, source_target_pairs={{0,2},{1,3},{2,4},{3,5},{4,6},{5,7},{6,0},{7,1},{8,10},{9,11},{10,... | collective-permute-start | bytes 110600 | tf_op jit(solution)/shard_map/ppermute | solution.py:337
  69.9 4.2 %collective-permute-start.1 = (bf16[144,128]{1,0:T(8,128)(2,1)S(1)}, bf16[144,128]{1,0:T(8,128)(2,1)S(1)}, u32[]{:S(2)}, u32[]{:S(2)}) collective-permute-start(bf16[144,128]{1,0:T(8,128)(2,1)S(1)} %get-tuple-element.15), channel_id=1, source_target_pairs={{0,4},{1,5},{2,6},{3,7},{4,0},{5,1},{6,2},{7,3},{8,12},{9,13},{10,... | collective-permute-start | bytes 110600 | tf_op jit(solution)/shard_map/ppermute | solution.py:337
  74.1 2.4 %collective-permute-start.2 = (bf16[144,128]{1,0:T(8,128)(2,1)S(1)}, bf16[144,128]{1,0:T(8,128)(2,1)S(1)}, u32[]{:S(2)}, u32[]{:S(2)}) collective-permute-start(bf16[144,128]{1,0:T(8,128)(2,1)S(1)} %get-tuple-element.16), channel_id=1, source_target_pairs={{0,6},{1,7},{2,0},{3,1},{4,2},{5,3},{6,4},{7,5},{8,14},{9,15},{10,... | collective-permute-start | bytes 110600 | tf_op jit(solution)/shard_map/ppermute | solution.py:337
  76.5 0.1 collective-permute-done.1.refs_2_
  76.6 2.0 %collective-permute-done.2.refs_3_ = bf16[144,128]{1,0:T(8,128)(2,1)S(1)} collective-permute-done((bf16[144,128]{1,0:T(8,128)(2,1)S(1)}, bf16[144,128]{1,0:T(8,128)(2,1)S(1)}, u32[]{:S(2)}, u32[]{:S(2)}) %collective-permute-start.2) | collective-permute-done | bytes 36896 | tf_op jit(solution)/shard_map/ppermute | solution.py:337
  78.6 0.9 class_average.1
  79.5 6.9 %collective-permute-start.6 = (bf16[128,128]{1,0:T(8,128)(2,1)}, bf16[128,128]{1,0:T(8,128)(2,1)S(1)}, u32[]{:S(2)}, u32[]{:S(2)}) collective-permute-start(bf16[128,128]{1,0:T(8,128)(2,1)} %get-tuple-element.17), channel_id=1, source_target_pairs={{0,134},{1,135},{2,128},{3,129},{4,130},{5,131},{6,132},{7,133},{8... | collective-permute-start | bytes 98312 | tf_op jit(solution)/shard_map/ppermute | solution.py:342
  86.4 1.4 collective-permute-start.4
  87.8 1.1 collective-permute-start.3
  88.9 5.2 %collective-permute-done.5.refs_2_ = bf16[128,128]{1,0:T(8,128)(2,1)S(1)} collective-permute-done((bf16[128,128]{1,0:T(8,128)(2,1)}, bf16[128,128]{1,0:T(8,128)(2,1)S(1)}, u32[]{:S(2)}, u32[]{:S(2)}) %collective-permute-start.5) | collective-permute-done | bytes 32800 | tf_op jit(solution)/shard_map/ppermute | solution.py:342
  94.1 0.0 collective-permute-done.4.refs_1_
  94.1 0.6 group_copies.1
  94.6 0.0 copy-start
  94.7 0.0 copy-start.1
  94.7 0.0 copy-start.2
  94.7 0.0 copy-start.3
  94.7 0.0 copy-start.4
  94.7 0.0 copy-start.5
  94.7 0.0 copy-start.6
  94.7 59.2 %all_to_all.11.bands = bf16[32,528,128]{2,1,0:T(8,128)(2,1)S(1)} all-to-all(bf16[32,528,128]{2,1,0:T(8,128)(2,1)S(1)} %group_copies.1), channel_id=1, replica_groups={{0,1,8,9,16,17,24,25,32,33,40,41,48,49,56,57,64,65,72,73,80,81,88,89,96..., dimensions={0} | all-to-all | bytes 8650752 | tf_op jit(solution)/shard_map/all_to_all | solution.py:329
  154.0 6.6 %particle_outputs.1 = (bf16[64,128,128]{2,1,0:T(8,128)(2,1)}, bf16[36,64]{1,0:T(8,128)(2,1)}, bf16[1,64]{1,0:T(2,128)(2,1)}) custom-call(s32[1,64]{1,0:T(1,128)S(1)} %copy-done.4, s32[1,64]{1,0:T(1,128)S(1)} %copy-done.5, s32[1,64]{1,0:T(1,128)S(1)} %copy-done.6, f32[64,256]{1,0:T(8,128)S(1)} %bitcast.10, bf16[64,128,128]{2,1,0:T(8,128)(2,1)S(1)} %bitcast.8, ...), custom_call_target="tpu_custom_call" | custom-call | tf_op jit(solution)/shard_map/particle_outputs/pallas_call | solution.py:303
  (11 shorter events, 0.0 us)
Async XLA Ops:
  66.8 9.7 %collective-permute-start = (bf16[144,128]{1,0:T(8,128)(2,1)S(1)}, bf16[144,128]{1,0:T(8,128)(2,1)S(1)}, u32[]{:S(2)}, u32[]{:S(2)}) collective-permute-start(bf16[144,128]{1,0:T(8,128)(2,1)S(1)} %get-tuple-element.14), channel_id=1, source_target_pairs={{0,2},{1,3},{2,4},{3,5},{4,6},{5,7},{6,0},{7,1},{8,10},{9,11},{10,... | collective-permute-start | bytes 110600 | tf_op jit(solution)/shard_map/ppermute | solution.py:337
  69.9 6.7 %collective-permute-start.1 = (bf16[144,128]{1,0:T(8,128)(2,1)S(1)}, bf16[144,128]{1,0:T(8,128)(2,1)S(1)}, u32[]{:S(2)}, u32[]{:S(2)}) collective-permute-start(bf16[144,128]{1,0:T(8,128)(2,1)S(1)} %get-tuple-element.15), channel_id=1, source_target_pairs={{0,4},{1,5},{2,6},{3,7},{4,0},{5,1},{6,2},{7,3},{8,12},{9,13},{10,... | collective-permute-start | bytes 110600 | tf_op jit(solution)/shard_map/ppermute | solution.py:337
  74.1 4.5 %collective-permute-start.2 = (bf16[144,128]{1,0:T(8,128)(2,1)S(1)}, bf16[144,128]{1,0:T(8,128)(2,1)S(1)}, u32[]{:S(2)}, u32[]{:S(2)}) collective-permute-start(bf16[144,128]{1,0:T(8,128)(2,1)S(1)} %get-tuple-element.16), channel_id=1, source_target_pairs={{0,6},{1,7},{2,0},{3,1},{4,2},{5,3},{6,4},{7,5},{8,14},{9,15},{10,... | collective-permute-start | bytes 110600 | tf_op jit(solution)/shard_map/ppermute | solution.py:337
  79.5 9.4 %collective-permute-start.6 = (bf16[128,128]{1,0:T(8,128)(2,1)}, bf16[128,128]{1,0:T(8,128)(2,1)S(1)}, u32[]{:S(2)}, u32[]{:S(2)}) collective-permute-start(bf16[128,128]{1,0:T(8,128)(2,1)} %get-tuple-element.17), channel_id=1, source_target_pairs={{0,134},{1,135},{2,128},{3,129},{4,130},{5,131},{6,132},{7,133},{8... | collective-permute-start | bytes 98312 | tf_op jit(solution)/shard_map/ppermute | solution.py:342
  86.4 7.7 %collective-permute-start.5 = (bf16[128,128]{1,0:T(8,128)(2,1)}, bf16[128,128]{1,0:T(8,128)(2,1)S(1)}, u32[]{:S(2)}, u32[]{:S(2)}) collective-permute-start(bf16[128,128]{1,0:T(8,128)(2,1)} %get-tuple-element.17), channel_id=1, source_target_pairs={{0,132},{1,133},{2,134},{3,135},{4,128},{5,129},{6,130},{7,131},{8... | collective-permute-start | bytes 98312 | tf_op jit(solution)/shard_map/ppermute | solution.py:342
  86.4 7.7 %collective-permute-start.4 = (bf16[128,128]{1,0:T(8,128)(2,1)}, bf16[128,128]{1,0:T(8,128)(2,1)S(1)}, u32[]{:S(2)}, u32[]{:S(2)}) collective-permute-start(bf16[128,128]{1,0:T(8,128)(2,1)} %get-tuple-element.17), channel_id=1, source_target_pairs={{0,130},{1,131},{2,132},{3,133},{4,134},{5,135},{6,128},{7,129},{8... | collective-permute-start | bytes 98312 | tf_op jit(solution)/shard_map/ppermute | solution.py:342
  87.8 6.3 %collective-permute-start.3 = (bf16[128,128]{1,0:T(8,128)(2,1)}, bf16[128,128]{1,0:T(8,128)(2,1)S(1)}, u32[]{:S(2)}, u32[]{:S(2)}) collective-permute-start(bf16[128,128]{1,0:T(8,128)(2,1)} %get-tuple-element.17), channel_id=1, source_target_pairs={{0,128},{1,129},{2,130},{3,131},{4,132},{5,133},{6,134},{7,135},{8... | collective-permute-start | bytes 98312 | tf_op jit(solution)/shard_map/ppermute | solution.py:342
  94.6 59.3 %copy-start = (bf16[1,64,128,128]{3,2,1,0:T(8,128)(2,1)S(1)}, bf16[1,64,128,128]{3,2,1,0:T(8,128)(2,1)}, u32[]{:S(2)}) copy-start(bf16[1,64,128,128]{3,2,1,0:T(8,128)(2,1)} %param.7) | copy-start | bytes 6291460
  94.7 59.3 %copy-start.1 = (bf16[36,128,128]{2,1,0:T(8,128)(2,1)S(1)}, bf16[36,128,128]{2,1,0:T(8,128)(2,1)}, u32[]{:S(2)}) copy-start(bf16[36,128,128]{2,1,0:T(8,128)(2,1)} %constant.4.clone.rotations.rots) | copy-start | bytes 3538948
  94.7 59.3 %copy-start.2 = (f32[256,64]{0,1:T(8,128)S(1)}, f32[256,64]{0,1:T(8,128)}, u32[]{:S(2)}) copy-start(f32[256,64]{0,1:T(8,128)} %param.11) | copy-start | bytes 196612
  94.7 59.3 %copy-start.3 = (f32[128,128]{1,0:T(8,128)S(1)}, f32[128,128]{1,0:T(8,128)}, u32[]{:S(2)}) copy-start(f32[128,128]{1,0:T(8,128)} %constant.5.clone.lag_ref) | copy-start | bytes 196612
  94.7 59.3 %copy-start.4 = (s32[1,64]{1,0:T(1,128)S(1)}, s32[1,64]{1,0:T(1,128)}, u32[]{:S(2)}) copy-start(s32[1,64]{1,0:T(1,128)} %classes.1) | copy-start | bytes 772
  94.7 59.3 %copy-start.5 = (s32[1,64]{1,0:T(1,128)S(1)}, s32[1,64]{1,0:T(1,128)}, u32[]{:S(2)}) copy-start(s32[1,64]{1,0:T(1,128)} %turns.1) | copy-start | bytes 772
  94.7 59.3 %copy-start.6 = (s32[1,64]{1,0:T(1,128)S(1)}, s32[1,64]{1,0:T(1,128)}, u32[]{:S(2)}) copy-start(s32[1,64]{1,0:T(1,128)} %group_row.1) | copy-start | bytes 772

commit v5 on v4

--- a/solution.py
+++ b/solution.py
@@ -19,7 +19,6 @@
 SHELLS = ROWS // 2
 TAIL = 16
 BAND = STACK * ROWS + TAIL
-SLAB = ROWS + TAIL
 BATCH = 8
 HIGH = lax.Precision.HIGHEST
 F32 = jnp.float32
@@ -168,77 +167,92 @@
     return lax.axis_index("cls") // 2 % STACK
 
 
-def group_kernel(bands, *outs):
-    here = place_along_z()
+def store_band(out, total):
+    out[: STACK * ROWS, :] = total[: STACK * ROWS].astype(BF16)
+    out[STACK * ROWS :, :] = split_pair(join_pair(total[STACK * ROWS :])).astype(BF16)
+
+
+def group_kernel(bands, out):
+    for at in range(0, STACK * ROWS, SHELLS):
+        total = bands[0, at : at + SHELLS, :].astype(F32)
+        for d in range(1, GROUP):
+            total = total + bands[d, at : at + SHELLS, :].astype(F32)
+        out[at : at + SHELLS, :] = total.astype(BF16)
     tail = jnp.sum(bands[:, STACK * ROWS :, :].astype(F32), axis=0)
-    tail = split_pair(join_pair(tail))
-    for j in range(STACK):
-        s = (here + j) % STACK
-        for half in range(2):
-            at = pl.ds(pl.multiple_of(s * ROWS + half * SHELLS, SHELLS), SHELLS)
-            total = bands[0, at, :].astype(F32)
-            for d in range(1, GROUP):
-                total = total + bands[d, at, :].astype(F32)
-            outs[j][half * SHELLS : (half + 1) * SHELLS, :] = total.astype(BF16)
-        outs[j][ROWS:, :] = tail.astype(BF16)
+    out[STACK * ROWS :, :] = split_pair(join_pair(tail)).astype(BF16)
 
 
 def group_sums(bands):
     return pl.pallas_call(
         group_kernel,
-        out_shape=[jax.ShapeDtypeStruct((SLAB, LANES), BF16)] * STACK,
+        out_shape=jax.ShapeDtypeStruct((BAND, LANES), BF16),
         in_specs=[VMEM],
-        out_specs=[VMEM] * STACK,
+        out_specs=VMEM,
         compiler_params=pltpu.CompilerParams(vmem_limit_bytes=24 << 20),
         name="group_sums",
     )(bands)
 
 
-def average_kernel(*refs):
-    slabs, (avg, tail) = refs[:STACK], refs[STACK:]
-    total = sum(s[...].astype(F32) for s in slabs)
-    den = join_pair(total[ROWS:])
+def pair_kernel(mine, theirs, out):
+    store_band(out, mine[...].astype(F32) + theirs[...].astype(F32))
+
+
+def pair_sums(mine, theirs):
+    return pl.pallas_call(
+        pair_kernel,
+        out_shape=jax.ShapeDtypeStruct((BAND, LANES), BF16),
+        in_specs=[VMEM] * 2,
+        out_specs=VMEM,
+        compiler_params=pltpu.CompilerParams(vmem_limit_bytes=4 << 20),
+        name="pair_sums",
+    )(mine, theirs)
+
+
+def average_kernel(mine, theirs, stack, own, tail):
+    total = mine[...].astype(F32) + theirs[...].astype(F32)
+    den = join_pair(total[STACK * ROWS :])
     tail[...] = split_pair(den).astype(BF16)
-    here = lax.broadcasted_iota(jnp.int32, den.shape, 0) == place_along_z()
-    den = jnp.sum(jnp.where(here, den, 0.0), axis=0, keepdims=True)
-    column = jnp.transpose(jnp.broadcast_to(jnp.concatenate([den, den], axis=1), (LANES, LANES)))
-    avg[...] = (total[:ROWS] / (column + TAU)).astype(BF16)
-
-
-def class_average(slabs):
+    for s in range(STACK):
+        row = den[s : s + 1]
+        column = jnp.transpose(jnp.broadcast_to(jnp.concatenate([row, row], axis=1), (LANES, LANES)))
+        stack[s * ROWS : (s + 1) * ROWS, :] = (total[s * ROWS : (s + 1) * ROWS] / (column + TAU)).astype(BF16)
+    own[...] = stack[pl.ds(pl.multiple_of(place_along_z() * ROWS, ROWS), ROWS), :]
+
+
+def class_averages(mine, theirs):
     return pl.pallas_call(
         average_kernel,
-        out_shape=(jax.ShapeDtypeStruct((ROWS, LANES), BF16), jax.ShapeDtypeStruct((TAIL, LANES), BF16)),
-        in_specs=[VMEM] * STACK,
-        out_specs=(VMEM, VMEM),
+        out_shape=(
+            jax.ShapeDtypeStruct((STACK * ROWS, LANES), BF16),
+            jax.ShapeDtypeStruct((ROWS, LANES), BF16),
+            jax.ShapeDtypeStruct((TAIL, LANES), BF16),
+        ),
+        in_specs=[VMEM] * 2,
+        out_specs=(VMEM, VMEM, VMEM),
         compiler_params=pltpu.CompilerParams(vmem_limit_bytes=4 << 20),
-        name="class_average",
-    )(*slabs)
-
-
-def copies_kernel(tail, *refs):
-    slabs, out = refs[:STACK], refs[STACK]
-    here = place_along_z()
-    for j in range(STACK):
-        s = (here + STACK - j) % STACK
-        at = pl.ds(pl.multiple_of(s * ROWS, ROWS), ROWS)
-        value = slabs[j][...]
+        name="class_averages",
+    )(mine, theirs)
+
+
+def copies_kernel(stack, tail, out):
+    for at in range(0, STACK * ROWS, SHELLS):
+        value = stack[at : at + SHELLS, :]
         for d in range(GROUP):
-            out[d, at, :] = value
+            out[d, at : at + SHELLS, :] = value
     value = tail[...]
     for d in range(GROUP):
         out[d, STACK * ROWS :, :] = value
 
 
-def group_copies(tail, slabs):
+def group_copies(stack, tail):
     return pl.pallas_call(
         copies_kernel,
         out_shape=jax.ShapeDtypeStruct((GROUP, BAND, LANES), BF16),
-        in_specs=[VMEM] * (STACK + 1),
+        in_specs=[VMEM] * 2,
         out_specs=VMEM,
         compiler_params=pltpu.CompilerParams(vmem_limit_bytes=24 << 20),
         name="group_copies",
-    )(tail, *slabs)
+    )(stack, tail)
 
 
 def outputs_kernel(classes, turns, group_row, table, rows, rots, bands, lag_ref, resid, score, lever, *scratch):
@@ -329,25 +343,23 @@
     return lax.all_to_all(value, "cls", split_axis=0, concat_axis=0, tiled=True, axis_index_groups=groups)
 
 
-def upward(chip, steps):
-    return chip // DEPTH * DEPTH + (chip + 2 * steps) % DEPTH
-
-
-def shift(value, steps):
-    return lax.ppermute(value, "cls", [(i, upward(i, steps)) for i in range(CLASSES)])
-
-
-def cross(value, steps):
-    pairs = [(h * CLASSES + i, (1 - h) * CLASSES + upward(i, steps)) for h in range(2) for i in range(CLASSES)]
-    return lax.ppermute(value, ("half", "cls"), pairs)
+def swap_along_z(value, odd):
+    def partner(chip):
+        place = chip // 2 % STACK
+        other = (place + (1 if place % 2 == odd else STACK - 1)) % STACK
+        return chip + 2 * (other - place)
+
+    return lax.ppermute(value, "cls", [(i, partner(i)) for i in range(CLASSES)])
 
 
 def body(particles, assign, rotation, group, ctf):
     operands = (assign, rotation, group, ctf.T, particles[0], jnp.asarray(rotation_matrices()))
     pinned = [pltpu.with_memory_space_constraint(x, pltpu.HBM) for x in operands]
-    pieces = group_sums(exchange(class_sums(*pinned)))
-    average, tail = class_average([pieces[0]] + [shift(pieces[j], j) for j in range(1, STACK)])
-    bands = exchange(group_copies(tail, [cross(average, j) for j in range(STACK)]))
+    band = group_sums(exchange(class_sums(*pinned)))
+    band = pair_sums(band, swap_along_z(band, 0))
+    stack, average, tail = class_averages(band, swap_along_z(band, 1))
+    stack = lax.ppermute(stack, "half", [(0, 1), (1, 0)])
+    bands = exchange(group_copies(stack, tail))
     residual, scores, leverage = particle_outputs(*operands, bands)
     return (average[None, None], residual[None], scores.T[None], leverage)
 

time: 161 us -> 154 us (0.957)
  starting transfers between devices: 19.1 us -> 9.06 us
  waiting for transfers between devices: 7.3 us -> 11 us
    ppermute x7 -> x3, starting transfers between devices: 19.1 us -> 9.06 us  [the longest x2 5.22 us: swap_along_z(): return lax.ppermute(value, 'cls', [(i, partner(i)) for i in range(CLASSES)])]
    ppermute x7 -> x3, waiting for transfers between devices: 7.3 us -> 11 us  [the longest x2 10 us: swap_along_z(): return lax.ppermute(value, 'cls', [(i, partner(i)) for i in range(CLASSES)])]
  transfers between devices with their start and end apart: 7 -> 3, of which waited for: 3 -> 3; matrix products, arithmetic and copies ran while one was open for 0% -> 0% of each run, Pallas kernels for 0% -> 0%
where the time goes in v5:
time: 154 us
  blocking collectives  120 us (78%)
  Pallas kernels  13.3 us (9%)
  waiting for transfers between devices  11 us (7%)
  starting transfers between devices  9.06 us (6%)
    all_to_all x2, blocking collectives, exchange(): lax.all_to_all(value, 'cls', split_axis=0, concat_axis=0, tiled=True, axi...  120 us
    ppermute x2, waiting for transfers between devices, swap_along_z(): return lax.ppermute(value, 'cls', [(i, partner(i)) for i in range(CLASSES)])  10 us
    pallas_call x1, Pallas kernels, particle_outputs(): pl.pallas_call(outputs_kernel, out_shape=(jax.ShapeDtypeStruct(images.sha...  6.6 us
    ppermute x2, starting transfers between devices, swap_along_z(): return lax.ppermute(value, 'cls', [(i, partner(i)) for i in range(CLASSES)])  5.22 us
    pallas_call x1, Pallas kernels, class_sums(): pl.pallas_call(sums_kernel, out_shape=jax.ShapeDtypeStruct((GROUP, BAND,...  4.45 us
    ppermute x1, starting transfers between devices, body(): stack = lax.ppermute(stack, 'half', [(0, 1), (1, 0)])  3.83 us
  transfers between devices with their start and end apart: 3, of which 3 were waited for; matrix products, arithmetic and copies ran while one was open for 0% of the time, Pallas kernels for 0%

profile of v5, /device:TPU:1, one launch (start us, length us, event | category | flops | bytes accessed | tf_op | source)
XLA Modules:
  0.0 153.7 jit_solution(6154829420123804911)
XLA Ops:
  0.6 4.5 %class_sums.1 = bf16[32,528,128]{2,1,0:T(8,128)(2,1)S(1)} custom-call(s32[1,64]{1,0:T(1,128)} %classes.1, s32[1,64]{1,0:T(1,128)} %turns.1, s32[1,64]{1,0:T(1,128)} %group_row.1, f32[64,256]{1,0:T(8,128)} %bitcast.9, bf16[64,128,128]{2,1,0:T(8,128)(2,1)} %bitcast.7, bf16[36,128,128]{2,1,0:T(8,128)(2,1)} %constant.4.clone.rotations.rots), custom_call_target="tpu_custom_call" | custom-call | tf_op jit(solution)/shard_map/class_sums/pallas_call | solution.py:145
  5.1 61.1 %all_to_all.10.bands = bf16[32,528,128]{2,1,0:T(8,128)(2,1)S(1)} all-to-all(bf16[32,528,128]{2,1,0:T(8,128)(2,1)S(1)} %class_sums.1), channel_id=1, replica_groups={{0,1,8,9,16,17,24,25,32,33,40,41,48,49,56,57,64,65,72,73,80,81,88,89,96..., dimensions={0} | all-to-all | bytes 8650752 | tf_op jit(solution)/shard_map/all_to_all | solution.py:343
  66.2 0.6 group_sums.1.mine
  66.8 3.1 %collective-permute-start = (bf16[528,128]{1,0:T(8,128)(2,1)S(1)}, bf16[528,128]{1,0:T(8,128)(2,1)S(1)}, u32[]{:S(2)}, u32[]{:S(2)}) collective-permute-start(bf16[528,128]{1,0:T(8,128)(2,1)S(1)} %group_sums.1.mine), channel_id=1, source_target_pairs={{0,2},{1,3},{2,0},{3,1},{4,6},{5,7},{6,4},{7,5},{8,10},{9,11},{10,... | collective-permute-start | bytes 405512 | tf_op jit(solution)/shard_map/ppermute | solution.py:352
  69.9 6.1 %collective-permute-done.theirs = bf16[528,128]{1,0:T(8,128)(2,1)S(1)} collective-permute-done((bf16[528,128]{1,0:T(8,128)(2,1)S(1)}, bf16[528,128]{1,0:T(8,128)(2,1)S(1)}, u32[]{:S(2)}, u32[]{:S(2)}) %collective-permute-start) | collective-permute-done | bytes 135200 | tf_op jit(solution)/shard_map/ppermute | solution.py:352
  76.0 0.2 pair_sums.1.mine
  76.2 2.1 %collective-permute-start.1 = (bf16[528,128]{1,0:T(8,128)(2,1)S(1)}, bf16[528,128]{1,0:T(8,128)(2,1)S(1)}, u32[]{:S(2)}, u32[]{:S(2)}) collective-permute-start(bf16[528,128]{1,0:T(8,128)(2,1)S(1)} %pair_sums.1.mine), channel_id=1, source_target_pairs={{0,6},{1,7},{2,4},{3,5},{4,2},{5,3},{6,0},{7,1},{8,14},{9,15},{10,... | collective-permute-start | bytes 405512 | tf_op jit(solution)/shard_map/ppermute | solution.py:352
  78.3 3.9 %collective-permute-done.1.theirs = bf16[528,128]{1,0:T(8,128)(2,1)S(1)} collective-permute-done((bf16[528,128]{1,0:T(8,128)(2,1)S(1)}, bf16[528,128]{1,0:T(8,128)(2,1)S(1)}, u32[]{:S(2)}, u32[]{:S(2)}) %collective-permute-start.1) | collective-permute-done | bytes 135200 | tf_op jit(solution)/shard_map/ppermute | solution.py:352
  82.3 0.9 class_averages.1
  83.2 3.8 %collective-permute-start.2 = (bf16[512,128]{1,0:T(8,128)(2,1)S(1)}, bf16[512,128]{1,0:T(8,128)(2,1)S(1)}, u32[]{:S(2)}, u32[]{:S(2)}) collective-permute-start(bf16[512,128]{1,0:T(8,128)(2,1)S(1)} %get-tuple-element.11), channel_id=1, source_target_pairs={{0,128},{128,0},{1,129},{129,1},{2,130},{130,2},{3,131},{131,3},{4... | collective-permute-start | bytes 393224 | tf_op jit(solution)/shard_map/ppermute | solution.py:361
  87.0 1.0 collective-permute-done.2.stack
  88.0 0.6 group_copies.1
  88.5 0.0 copy-start
  88.6 0.0 copy-start.1
  88.6 0.0 copy-start.2
  88.6 0.0 copy-start.3
  88.6 0.0 copy-start.4
  88.6 0.0 copy-start.5
  88.6 0.0 copy-start.6
  88.6 58.4 %all_to_all.11.bands = bf16[32,528,128]{2,1,0:T(8,128)(2,1)S(1)} all-to-all(bf16[32,528,128]{2,1,0:T(8,128)(2,1)S(1)} %group_copies.1), channel_id=1, replica_groups={{0,1,8,9,16,17,24,25,32,33,40,41,48,49,56,57,64,65,72,73,80,81,88,89,96..., dimensions={0} | all-to-all | bytes 8650752 | tf_op jit(solution)/shard_map/all_to_all | solution.py:343
  147.0 0.0 copy-done
  147.0 0.0 copy-done.1
  147.0 0.0 copy-done.2
  147.1 6.6 %particle_outputs.1 = (bf16[64,128,128]{2,1,0:T(8,128)(2,1)}, bf16[36,64]{1,0:T(8,128)(2,1)}, bf16[1,64]{1,0:T(2,128)(2,1)}) custom-call(s32[1,64]{1,0:T(1,128)S(1)} %copy-done.4, s32[1,64]{1,0:T(1,128)S(1)} %copy-done.5, s32[1,64]{1,0:T(1,128)S(1)} %copy-done.6, f32[64,256]{1,0:T(8,128)S(1)} %bitcast.10, bf16[64,128,128]{2,1,0:T(8,128)(2,1)S(1)} %bitcast.8, ...), custom_call_target="tpu_custom_call" | custom-call | tf_op jit(solution)/shard_map/particle_outputs/pallas_call | solution.py:317
  (4 shorter events, 0.0 us)
Async XLA Ops:
  66.8 9.2 %collective-permute-start = (bf16[528,128]{1,0:T(8,128)(2,1)S(1)}, bf16[528,128]{1,0:T(8,128)(2,1)S(1)}, u32[]{:S(2)}, u32[]{:S(2)}) collective-permute-start(bf16[528,128]{1,0:T(8,128)(2,1)S(1)} %group_sums.1.mine), channel_id=1, source_target_pairs={{0,2},{1,3},{2,0},{3,1},{4,6},{5,7},{6,4},{7,5},{8,10},{9,11},{10,... | collective-permute-start | bytes 405512 | tf_op jit(solution)/shard_map/ppermute | solution.py:352
  76.2 6.1 %collective-permute-start.1 = (bf16[528,128]{1,0:T(8,128)(2,1)S(1)}, bf16[528,128]{1,0:T(8,128)(2,1)S(1)}, u32[]{:S(2)}, u32[]{:S(2)}) collective-permute-start(bf16[528,128]{1,0:T(8,128)(2,1)S(1)} %pair_sums.1.mine), channel_id=1, source_target_pairs={{0,6},{1,7},{2,4},{3,5},{4,2},{5,3},{6,0},{7,1},{8,14},{9,15},{10,... | collective-permute-start | bytes 405512 | tf_op jit(solution)/shard_map/ppermute | solution.py:352
  83.2 4.8 %collective-permute-start.2 = (bf16[512,128]{1,0:T(8,128)(2,1)S(1)}, bf16[512,128]{1,0:T(8,128)(2,1)S(1)}, u32[]{:S(2)}, u32[]{:S(2)}) collective-permute-start(bf16[512,128]{1,0:T(8,128)(2,1)S(1)} %get-tuple-element.11), channel_id=1, source_target_pairs={{0,128},{128,0},{1,129},{129,1},{2,130},{130,2},{3,131},{131,3},{4... | collective-permute-start | bytes 393224 | tf_op jit(solution)/shard_map/ppermute | solution.py:361
  88.5 58.5 %copy-start = (bf16[1,64,128,128]{3,2,1,0:T(8,128)(2,1)S(1)}, bf16[1,64,128,128]{3,2,1,0:T(8,128)(2,1)}, u32[]{:S(2)}) copy-start(bf16[1,64,128,128]{3,2,1,0:T(8,128)(2,1)} %param.7) | copy-start | bytes 6291460
  88.6 58.5 %copy-start.1 = (bf16[36,128,128]{2,1,0:T(8,128)(2,1)S(1)}, bf16[36,128,128]{2,1,0:T(8,128)(2,1)}, u32[]{:S(2)}) copy-start(bf16[36,128,128]{2,1,0:T(8,128)(2,1)} %constant.4.clone.rotations.rots) | copy-start | bytes 3538948
  88.6 58.5 %copy-start.2 = (f32[256,64]{0,1:T(8,128)S(1)}, f32[256,64]{0,1:T(8,128)}, u32[]{:S(2)}) copy-start(f32[256,64]{0,1:T(8,128)} %param.11) | copy-start | bytes 196612
  88.6 58.5 %copy-start.3 = (f32[128,128]{1,0:T(8,128)S(1)}, f32[128,128]{1,0:T(8,128)}, u32[]{:S(2)}) copy-start(f32[128,128]{1,0:T(8,128)} %constant.5.clone.lag_ref) | copy-start | bytes 196612
  88.6 58.5 %copy-start.4 = (s32[1,64]{1,0:T(1,128)S(1)}, s32[1,64]{1,0:T(1,128)}, u32[]{:S(2)}) copy-start(s32[1,64]{1,0:T(1,128)} %classes.1) | copy-start | bytes 772
  88.6 58.5 %copy-start.5 = (s32[1,64]{1,0:T(1,128)S(1)}, s32[1,64]{1,0:T(1,128)}, u32[]{:S(2)}) copy-start(s32[1,64]{1,0:T(1,128)} %turns.1) | copy-start | bytes 772
  88.6 58.5 %copy-start.6 = (s32[1,64]{1,0:T(1,128)S(1)}, s32[1,64]{1,0:T(1,128)}, u32[]{:S(2)}) copy-start(s32[1,64]{1,0:T(1,128)} %group_row.1) | copy-start | bytes 772

commit v6 on v5

--- a/solution.py
+++ b/solution.py
@@ -86,7 +86,7 @@
 
 
 def slot_of(c):
-    return (c // DEPTH) * 2 + c % 2, (c // 2) % STACK
+    return (c % 2) * (GROUP // 2) + c // DEPTH, (c // 2) % STACK
 
 
 def scale_rows(column, value):
@@ -116,7 +116,7 @@
     keep_columns(by_shell, columns)
     n = lax.broadcasted_iota(jnp.int32, (CLASSES, count), 0)
     d, s = n // STACK, n % STACK
-    member = ((d // 2) * DEPTH + s * 2 + d % 2 == assign_row[...]).astype(F32)
+    member = (d % (GROUP // 2) * DEPTH + s * 2 + d // (GROUP // 2) == assign_row[...]).astype(F32)
     pair = split_pair(contract(member, jnp.transpose(by_shell * by_shell), ((1,), (0,))))
     blank = jnp.zeros((TAIL - STACK, LANES), F32)
     for d in range(GROUP):
@@ -339,7 +339,7 @@
 
 def exchange(value):
     chips = np.arange(CLASSES).reshape(GROUP // 2, STACK, 2)
-    groups = [chips[:, k, :].reshape(-1).tolist() for k in range(STACK)]
+    groups = [chips[:, k, :].T.reshape(-1).tolist() for k in range(STACK)]
     return lax.all_to_all(value, "cls", split_axis=0, concat_axis=0, tiled=True, axis_index_groups=groups)
 
 

time: 154 us -> 153 us (level)
  blocking collectives: 120 us -> 118 us
where the time goes in v6:
time: 153 us
  blocking collectives  118 us (77%)
  Pallas kernels  13.3 us (9%)
  waiting for transfers between devices  12.1 us (8%)
  starting transfers between devices  8.15 us (5%)
    all_to_all x2, blocking collectives, exchange(): lax.all_to_all(value, 'cls', split_axis=0, concat_axis=0, tiled=True, axi...  118 us
    ppermute x2, waiting for transfers between devices, swap_along_z(): return lax.ppermute(value, 'cls', [(i, partner(i)) for i in range(CLASSES)])  11.1 us
    pallas_call x1, Pallas kernels, particle_outputs(): pl.pallas_call(outputs_kernel, out_shape=(jax.ShapeDtypeStruct(images.sha...  6.6 us
    pallas_call x1, Pallas kernels, class_sums(): pl.pallas_call(sums_kernel, out_shape=jax.ShapeDtypeStruct((GROUP, BAND,...  4.46 us
    ppermute x1, starting transfers between devices, body(): stack = lax.ppermute(stack, 'half', [(0, 1), (1, 0)])  4.08 us
    ppermute x2, starting transfers between devices, swap_along_z(): return lax.ppermute(value, 'cls', [(i, partner(i)) for i in range(CLASSES)])  4.07 us
  transfers between devices with their start and end apart: 3, of which 3 were waited for; matrix products, arithmetic and copies ran while one was open for 0% of the time, Pallas kernels for 0%

profile of v6, /device:TPU:1, one launch (start us, length us, event | category | flops | bytes accessed | tf_op | source)
XLA Modules:
  0.0 152.7 jit_solution(7069399475393200524)
XLA Ops:
  0.6 4.5 %class_sums.1 = bf16[32,528,128]{2,1,0:T(8,128)(2,1)S(1)} custom-call(s32[1,64]{1,0:T(1,128)} %classes.1, s32[1,64]{1,0:T(1,128)} %turns.1, s32[1,64]{1,0:T(1,128)} %group_row.1, f32[64,256]{1,0:T(8,128)} %bitcast.9, bf16[64,128,128]{2,1,0:T(8,128)(2,1)} %bitcast.7, bf16[36,128,128]{2,1,0:T(8,128)(2,1)} %constant.4.clone.rotations.rots), custom_call_target="tpu_custom_call" | custom-call | tf_op jit(solution)/shard_map/class_sums/pallas_call | solution.py:145
  5.1 60.6 %all_to_all.10.bands = bf16[32,528,128]{2,1,0:T(8,128)(2,1)S(1)} all-to-all(bf16[32,528,128]{2,1,0:T(8,128)(2,1)S(1)} %class_sums.1), channel_id=1, replica_groups={{0,8,16,24,32,40,48,56,64,72,80,88,96,104,112,120,1,9,17,25,33,41,49,57..., dimensions={0} | all-to-all | bytes 8650752 | tf_op jit(solution)/shard_map/all_to_all | solution.py:343
  65.7 0.6 group_sums.1.mine
  66.3 3.1 %collective-permute-start = (bf16[528,128]{1,0:T(8,128)(2,1)S(1)}, bf16[528,128]{1,0:T(8,128)(2,1)S(1)}, u32[]{:S(2)}, u32[]{:S(2)}) collective-permute-start(bf16[528,128]{1,0:T(8,128)(2,1)S(1)} %group_sums.1.mine), channel_id=1, source_target_pairs={{0,2},{1,3},{2,0},{3,1},{4,6},{5,7},{6,4},{7,5},{8,10},{9,11},{10,... | collective-permute-start | bytes 405512 | tf_op jit(solution)/shard_map/ppermute | solution.py:352
  69.4 6.0 %collective-permute-done.theirs = bf16[528,128]{1,0:T(8,128)(2,1)S(1)} collective-permute-done((bf16[528,128]{1,0:T(8,128)(2,1)S(1)}, bf16[528,128]{1,0:T(8,128)(2,1)S(1)}, u32[]{:S(2)}, u32[]{:S(2)}) %collective-permute-start) | collective-permute-done | bytes 135200 | tf_op jit(solution)/shard_map/ppermute | solution.py:352
  75.4 0.2 pair_sums.1.mine
  75.6 1.0 collective-permute-start.1
  76.6 5.1 %collective-permute-done.1.theirs = bf16[528,128]{1,0:T(8,128)(2,1)S(1)} collective-permute-done((bf16[528,128]{1,0:T(8,128)(2,1)S(1)}, bf16[528,128]{1,0:T(8,128)(2,1)S(1)}, u32[]{:S(2)}, u32[]{:S(2)}) %collective-permute-start.1) | collective-permute-done | bytes 135200 | tf_op jit(solution)/shard_map/ppermute | solution.py:352
  81.7 0.9 class_averages.1
  82.6 4.1 %collective-permute-start.2 = (bf16[512,128]{1,0:T(8,128)(2,1)S(1)}, bf16[512,128]{1,0:T(8,128)(2,1)S(1)}, u32[]{:S(2)}, u32[]{:S(2)}) collective-permute-start(bf16[512,128]{1,0:T(8,128)(2,1)S(1)} %get-tuple-element.11), channel_id=1, source_target_pairs={{0,128},{128,0},{1,129},{129,1},{2,130},{130,2},{3,131},{131,3},{4... | collective-permute-start | bytes 393224 | tf_op jit(solution)/shard_map/ppermute | solution.py:361
  86.7 1.0 collective-permute-done.2.stack
  87.7 0.6 group_copies.1
  88.2 0.0 copy-start
  88.2 0.0 copy-start.1
  88.2 0.0 copy-start.2
  88.3 0.0 copy-start.3
  88.3 0.0 copy-start.4
  88.3 0.0 copy-start.5
  88.3 0.0 copy-start.6
  88.3 57.7 %all_to_all.11.bands = bf16[32,528,128]{2,1,0:T(8,128)(2,1)S(1)} all-to-all(bf16[32,528,128]{2,1,0:T(8,128)(2,1)S(1)} %group_copies.1), channel_id=1, replica_groups={{0,8,16,24,32,40,48,56,64,72,80,88,96,104,112,120,1,9,17,25,33,41,49,57..., dimensions={0} | all-to-all | bytes 8650752 | tf_op jit(solution)/shard_map/all_to_all | solution.py:343
  146.0 0.0 copy-done.2
  146.0 0.0 copy-done.3
  146.1 0.0 copy-done.4
  146.1 6.6 %particle_outputs.1 = (bf16[64,128,128]{2,1,0:T(8,128)(2,1)}, bf16[36,64]{1,0:T(8,128)(2,1)}, bf16[1,64]{1,0:T(2,128)(2,1)}) custom-call(s32[1,64]{1,0:T(1,128)S(1)} %copy-done.4, s32[1,64]{1,0:T(1,128)S(1)} %copy-done.5, s32[1,64]{1,0:T(1,128)S(1)} %copy-done.6, f32[64,256]{1,0:T(8,128)S(1)} %bitcast.10, bf16[64,128,128]{2,1,0:T(8,128)(2,1)S(1)} %bitcast.8, ...), custom_call_target="tpu_custom_call" | custom-call | tf_op jit(solution)/shard_map/particle_outputs/pallas_call | solution.py:317
  (4 shorter events, 0.0 us)
Async XLA Ops:
  66.3 9.1 %collective-permute-start = (bf16[528,128]{1,0:T(8,128)(2,1)S(1)}, bf16[528,128]{1,0:T(8,128)(2,1)S(1)}, u32[]{:S(2)}, u32[]{:S(2)}) collective-permute-start(bf16[528,128]{1,0:T(8,128)(2,1)S(1)} %group_sums.1.mine), channel_id=1, source_target_pairs={{0,2},{1,3},{2,0},{3,1},{4,6},{5,7},{6,4},{7,5},{8,10},{9,11},{10,... | collective-permute-start | bytes 405512 | tf_op jit(solution)/shard_map/ppermute | solution.py:352
  75.6 6.1 %collective-permute-start.1 = (bf16[528,128]{1,0:T(8,128)(2,1)S(1)}, bf16[528,128]{1,0:T(8,128)(2,1)S(1)}, u32[]{:S(2)}, u32[]{:S(2)}) collective-permute-start(bf16[528,128]{1,0:T(8,128)(2,1)S(1)} %pair_sums.1.mine), channel_id=1, source_target_pairs={{0,6},{1,7},{2,4},{3,5},{4,2},{5,3},{6,0},{7,1},{8,14},{9,15},{10,... | collective-permute-start | bytes 405512 | tf_op jit(solution)/shard_map/ppermute | solution.py:352
  82.6 5.1 %collective-permute-start.2 = (bf16[512,128]{1,0:T(8,128)(2,1)S(1)}, bf16[512,128]{1,0:T(8,128)(2,1)S(1)}, u32[]{:S(2)}, u32[]{:S(2)}) collective-permute-start(bf16[512,128]{1,0:T(8,128)(2,1)S(1)} %get-tuple-element.11), channel_id=1, source_target_pairs={{0,128},{128,0},{1,129},{129,1},{2,130},{130,2},{3,131},{131,3},{4... | collective-permute-start | bytes 393224 | tf_op jit(solution)/shard_map/ppermute | solution.py:361
  88.2 57.8 %copy-start = (bf16[1,64,128,128]{3,2,1,0:T(8,128)(2,1)S(1)}, bf16[1,64,128,128]{3,2,1,0:T(8,128)(2,1)}, u32[]{:S(2)}) copy-start(bf16[1,64,128,128]{3,2,1,0:T(8,128)(2,1)} %param.7) | copy-start | bytes 6291460
  88.2 57.8 %copy-start.1 = (bf16[36,128,128]{2,1,0:T(8,128)(2,1)S(1)}, bf16[36,128,128]{2,1,0:T(8,128)(2,1)}, u32[]{:S(2)}) copy-start(bf16[36,128,128]{2,1,0:T(8,128)(2,1)} %constant.4.clone.rotations.rots) | copy-start | bytes 3538948
  88.2 57.8 %copy-start.2 = (f32[256,64]{0,1:T(8,128)S(1)}, f32[256,64]{0,1:T(8,128)}, u32[]{:S(2)}) copy-start(f32[256,64]{0,1:T(8,128)} %param.11) | copy-start | bytes 196612
  88.3 57.8 %copy-start.3 = (f32[128,128]{1,0:T(8,128)S(1)}, f32[128,128]{1,0:T(8,128)}, u32[]{:S(2)}) copy-start(f32[128,128]{1,0:T(8,128)} %constant.5.clone.lag_ref) | copy-start | bytes 196612
  88.3 57.8 %copy-start.4 = (s32[1,64]{1,0:T(1,128)S(1)}, s32[1,64]{1,0:T(1,128)}, u32[]{:S(2)}) copy-start(s32[1,64]{1,0:T(1,128)} %classes.1) | copy-start | bytes 772
  88.3 57.8 %copy-start.5 = (s32[1,64]{1,0:T(1,128)S(1)}, s32[1,64]{1,0:T(1,128)}, u32[]{:S(2)}) copy-start(s32[1,64]{1,0:T(1,128)} %turns.1) | copy-start | bytes 772
  88.3 57.8 %copy-start.6 = (s32[1,64]{1,0:T(1,128)S(1)}, s32[1,64]{1,0:T(1,128)}, u32[]{:S(2)}) copy-start(s32[1,64]{1,0:T(1,128)} %group_row.1) | copy-start | bytes 772

commit v7 on v6

--- a/solution.py
+++ b/solution.py
@@ -17,7 +17,7 @@
 LANES = 128
 ROWS = 128
 SHELLS = ROWS // 2
-TAIL = 16
+TAIL = 8
 BAND = STACK * ROWS + TAIL
 BATCH = 8
 HIGH = lax.Precision.HIGHEST
@@ -82,7 +82,8 @@
 
 def keep_columns(by_shell, columns):
     for b in range(columns.shape[0]):
-        columns[b, :, :BATCH] = by_shell[:, b * BATCH : (b + 1) * BATCH]
+        part = by_shell[:, b * BATCH : (b + 1) * BATCH]
+        columns[b] = jnp.concatenate([part, jnp.zeros((SHELLS, LANES - BATCH), F32)], axis=1)
 
 
 def slot_of(c):
@@ -93,8 +94,8 @@
     return jnp.concatenate([column * value[:SHELLS], column * value[SHELLS:]], axis=0)
 
 
-def sums_kernel(assign, rotation, group, table, images, rotations, out, *scratch):
-    classes, turns, assign_row, group_row, local, rows, rots, columns, sems = scratch
+def sums_kernel(assign, rotation, group, table, images, rotations, out, columns, weights_out, *scratch):
+    classes, turns, assign_row, group_row, local, rows, rots, sems = scratch
     count = rows.shape[0]
     moves = [
         (images, rows),
@@ -113,6 +114,7 @@
     for copy in copies[2:]:
         copy.wait()
     by_shell = weights_by_shell(group_row[...], local[...])
+    weights_out[...] = by_shell
     keep_columns(by_shell, columns)
     n = lax.broadcasted_iota(jnp.int32, (CLASSES, count), 0)
     d, s = n // STACK, n % STACK
@@ -144,9 +146,13 @@
     count, groups = images.shape[0], table.shape[1]
     return pl.pallas_call(
         sums_kernel,
-        out_shape=jax.ShapeDtypeStruct((GROUP, BAND, LANES), BF16),
+        out_shape=(
+            jax.ShapeDtypeStruct((GROUP, BAND, LANES), BF16),
+            jax.ShapeDtypeStruct((count // BATCH, SHELLS, LANES), F32),
+            jax.ShapeDtypeStruct((SHELLS, count), F32),
+        ),
         in_specs=[HBM] * 6,
-        out_specs=VMEM,
+        out_specs=(VMEM, VMEM, VMEM),
         scratch_shapes=[
             pltpu.SMEM((1, count), jnp.int32),
             pltpu.SMEM((1, count), jnp.int32),
@@ -155,7 +161,6 @@
             pltpu.VMEM((SHELLS, groups), F32),
             pltpu.VMEM((count, ROWS, LANES), BF16),
             pltpu.VMEM((NROT, LANES, LANES), BF16),
-            pltpu.VMEM((count // BATCH, SHELLS, LANES), F32),
             pltpu.SemaphoreType.DMA((7,)),
         ],
         compiler_params=pltpu.CompilerParams(vmem_limit_bytes=24 << 20),
@@ -255,11 +260,10 @@
     )(stack, tail)
 
 
-def outputs_kernel(classes, turns, group_row, table, rows, rots, bands, lag_ref, resid, score, lever, *scratch):
-    columns, held, out_sems, dens, lags, powers, energies = scratch
+def outputs_kernel(classes, turns, columns, weights_in, rows, rots, bands, lag_ref, resid, score, lever, *scratch):
+    held, out_sems, dens, lags, powers, energies = scratch
     count = rows.shape[0]
-    by_shell = weights_by_shell(group_row[...], table[...])
-    keep_columns(by_shell, columns)
+    by_shell = weights_in[...]
 
     def leave(b):
         at = pl.ds(pl.multiple_of(b * BATCH, BATCH), BATCH)
@@ -311,7 +315,7 @@
     lax.fori_loop(0, count // BATCH, finish, 0)
 
 
-def particle_outputs(assign, rotation, group, table, images, rotations, bands):
+def particle_outputs(assign, rotation, columns, weights, images, rotations, bands):
     count = images.shape[0]
     per_particle = pltpu.VMEM((count, LANES), F32)
     return pl.pallas_call(
@@ -324,7 +328,6 @@
         in_specs=[SMEM] * 2 + [VMEM] * 6,
         out_specs=(HBM, VMEM, VMEM),
         scratch_shapes=[
-            pltpu.VMEM((count // BATCH, SHELLS, LANES), F32),
             pltpu.VMEM((count, ROWS, LANES), BF16),
             pltpu.SemaphoreType.DMA((count // BATCH,)),
             per_particle,
@@ -334,7 +337,7 @@
         ],
         compiler_params=pltpu.CompilerParams(vmem_limit_bytes=24 << 20),
         name="particle_outputs",
-    )(assign, rotation, group, table, images, rotations, bands, jnp.asarray(lag_matrix()))
+    )(assign, rotation, columns, weights, images, rotations, bands, jnp.asarray(lag_matrix()))
 
 
 def exchange(value):
@@ -353,14 +356,16 @@
 
 
 def body(particles, assign, rotation, group, ctf):
-    operands = (assign, rotation, group, ctf.T, particles[0], jnp.asarray(rotation_matrices()))
+    images, rotations = particles[0], jnp.asarray(rotation_matrices())
+    operands = (assign, rotation, group, ctf.T, images, rotations)
     pinned = [pltpu.with_memory_space_constraint(x, pltpu.HBM) for x in operands]
-    band = group_sums(exchange(class_sums(*pinned)))
+    bands, columns, weights = class_sums(*pinned)
+    band = group_sums(exchange(bands))
     band = pair_sums(band, swap_along_z(band, 0))
     stack, average, tail = class_averages(band, swap_along_z(band, 1))
     stack = lax.ppermute(stack, "half", [(0, 1), (1, 0)])
     bands = exchange(group_copies(stack, tail))
-    residual, scores, leverage = particle_outputs(*operands, bands)
+    residual, scores, leverage = particle_outputs(assign, rotation, columns, weights, images, rotations, bands)
     return (average[None, None], residual[None], scores.T[None], leverage)
 
 

time: 153 us -> 151 us (0.987)
    ppermute x1, starting transfers between devices: 4.08 us -> 2.53 us  [body(): stack = lax.ppermute(stack, 'half', [(0, 1), (1, 0)])]
where the time goes in v7:
time: 151 us
  blocking collectives  119 us (79%)
  Pallas kernels  12.9 us (9%)
  waiting for transfers between devices  11.8 us (8%)
  starting transfers between devices  6.75 us (4%)
    all_to_all x2, blocking collectives, exchange(): lax.all_to_all(value, 'cls', split_axis=0, concat_axis=0, tiled=True, axi...  119 us
    ppermute x2, waiting for transfers between devices, swap_along_z(): return lax.ppermute(value, 'cls', [(i, partner(i)) for i in range(CLASSES)])  10.8 us
    pallas_call x1, Pallas kernels, particle_outputs(): pl.pallas_call(outputs_kernel, out_shape=(jax.ShapeDtypeStruct(images.sha...  6.22 us
    pallas_call x1, Pallas kernels, class_sums(): pl.pallas_call(sums_kernel, out_shape=(jax.ShapeDtypeStruct((GROUP, BAND,...  4.45 us
    ppermute x2, starting transfers between devices, swap_along_z(): return lax.ppermute(value, 'cls', [(i, partner(i)) for i in range(CLASSES)])  4.23 us
  transfers between devices with their start and end apart: 3, of which 3 were waited for; matrix products, arithmetic and copies ran while one was open for 0% of the time, Pallas kernels for 0%

profile of v7, /device:TPU:1, one launch (start us, length us, event | category | flops | bytes accessed | tf_op | source)
XLA Modules:
  0.0 150.8 jit_solution(17746138996839911980)
XLA Ops:
  0.6 4.4 %class_sums.1 = (bf16[32,520,128]{2,1,0:T(8,128)(2,1)S(1)}, f32[8,64,128]{2,1,0:T(8,128)S(1)}, f32[64,64]{1,0:T(8,128)S(1)}) custom-call(s32[1,64]{1,0:T(1,128)} %classes.1, s32[1,64]{1,0:T(1,128)} %turns.1, s32[1,64]{1,0:T(1,128)} %group.1, f32[64,256]{1,0:T(8,128)} %bitcast.9, bf16[64,128,128]{2,1,0:T(8,128)(2,1)} %bitcast.7, ...), custom_call_target="tpu_custom_call" | custom-call | tf_op jit(solution)/shard_map/class_sums/pallas_call | solution.py:147
  5.1 60.1 %all_to_all.10.bands = bf16[32,520,128]{2,1,0:T(8,128)(2,1)S(1)} all-to-all(bf16[32,520,128]{2,1,0:T(8,128)(2,1)S(1)} %get-tuple-element.13), channel_id=1, replica_groups={{0,8,16,24,32,40,48,56,64,72,80,88,96,104,112,120,1,9,17,25,33,41,49,57..., dimensions={0} | all-to-all | bytes 8519680 | tf_op jit(solution)/shard_map/all_to_all | solution.py:346
  65.1 0.6 group_sums.1.mine
  65.7 3.1 %collective-permute-start = (bf16[520,128]{1,0:T(8,128)(2,1)S(1)}, bf16[520,128]{1,0:T(8,128)(2,1)S(1)}, u32[]{:S(2)}, u32[]{:S(2)}) collective-permute-start(bf16[520,128]{1,0:T(8,128)(2,1)S(1)} %group_sums.1.mine), channel_id=1, source_target_pairs={{0,2},{1,3},{2,0},{3,1},{4,6},{5,7},{6,4},{7,5},{8,10},{9,11},{10,... | collective-permute-start | bytes 399368 | tf_op jit(solution)/shard_map/ppermute | solution.py:355
  68.8 5.9 %collective-permute-done.theirs = bf16[520,128]{1,0:T(8,128)(2,1)S(1)} collective-permute-done((bf16[520,128]{1,0:T(8,128)(2,1)S(1)}, bf16[520,128]{1,0:T(8,128)(2,1)S(1)}, u32[]{:S(2)}, u32[]{:S(2)}) %collective-permute-start) | collective-permute-done | bytes 133152 | tf_op jit(solution)/shard_map/ppermute | solution.py:355
  74.7 0.1 pair_sums.1.mine
  74.8 1.2 collective-permute-start.1
  76.0 5.0 %collective-permute-done.1.theirs = bf16[520,128]{1,0:T(8,128)(2,1)S(1)} collective-permute-done((bf16[520,128]{1,0:T(8,128)(2,1)S(1)}, bf16[520,128]{1,0:T(8,128)(2,1)S(1)}, u32[]{:S(2)}, u32[]{:S(2)}) %collective-permute-start.1) | collective-permute-done | bytes 133152 | tf_op jit(solution)/shard_map/ppermute | solution.py:355
  81.0 0.9 class_averages.1
  81.9 2.5 %collective-permute-start.2 = (bf16[512,128]{1,0:T(8,128)(2,1)S(1)}, bf16[512,128]{1,0:T(8,128)(2,1)S(1)}, u32[]{:S(2)}, u32[]{:S(2)}) collective-permute-start(bf16[512,128]{1,0:T(8,128)(2,1)S(1)} %get-tuple-element.17), channel_id=1, source_target_pairs={{0,128},{128,0},{1,129},{129,1},{2,130},{130,2},{3,131},{131,3},{4... | collective-permute-start | bytes 393224 | tf_op jit(solution)/shard_map/ppermute | solution.py:366
  84.4 1.0 collective-permute-done.2.stack
  85.4 0.5 group_copies.1
  85.9 0.0 copy-start
  85.9 0.0 copy-start.1
  85.9 0.0 copy-start.2
  86.0 0.0 copy-start.3
  86.0 0.0 copy-start.4
  86.0 58.5 %all_to_all.11.bands = bf16[32,520,128]{2,1,0:T(8,128)(2,1)S(1)} all-to-all(bf16[32,520,128]{2,1,0:T(8,128)(2,1)S(1)} %group_copies.1), channel_id=1, replica_groups={{0,8,16,24,32,40,48,56,64,72,80,88,96,104,112,120,1,9,17,25,33,41,49,57..., dimensions={0} | all-to-all | bytes 8519680 | tf_op jit(solution)/shard_map/all_to_all | solution.py:346
  144.5 0.0 copy-done
  144.5 0.0 copy-done.1
  144.5 0.0 copy-done.2
  144.5 0.0 copy-done.3
  144.5 0.0 copy-done.4
  144.5 6.2 %particle_outputs.1 = (bf16[64,128,128]{2,1,0:T(8,128)(2,1)}, bf16[36,64]{1,0:T(8,128)(2,1)}, bf16[1,64]{1,0:T(2,128)(2,1)}) custom-call(s32[1,64]{1,0:T(1,128)S(1)} %copy-done.3, s32[1,64]{1,0:T(1,128)S(1)} %copy-done.4, f32[8,64,128]{2,1,0:T(8,128)S(1)} %get-tuple-element.15.columns, f32[64,64]{1,0:T(8,128)S(1)} %get-tuple-element.16.weights_in, ...), custom_call_target="tpu_custom_call" | custom-call | tf_op jit(solution)/shard_map/particle_outputs/pallas_call | solution.py:321
Async XLA Ops:
  65.7 8.9 %collective-permute-start = (bf16[520,128]{1,0:T(8,128)(2,1)S(1)}, bf16[520,128]{1,0:T(8,128)(2,1)S(1)}, u32[]{:S(2)}, u32[]{:S(2)}) collective-permute-start(bf16[520,128]{1,0:T(8,128)(2,1)S(1)} %group_sums.1.mine), channel_id=1, source_target_pairs={{0,2},{1,3},{2,0},{3,1},{4,6},{5,7},{6,4},{7,5},{8,10},{9,11},{10,... | collective-permute-start | bytes 399368 | tf_op jit(solution)/shard_map/ppermute | solution.py:355
  74.8 6.1 %collective-permute-start.1 = (bf16[520,128]{1,0:T(8,128)(2,1)S(1)}, bf16[520,128]{1,0:T(8,128)(2,1)S(1)}, u32[]{:S(2)}, u32[]{:S(2)}) collective-permute-start(bf16[520,128]{1,0:T(8,128)(2,1)S(1)} %pair_sums.1.mine), channel_id=1, source_target_pairs={{0,6},{1,7},{2,4},{3,5},{4,2},{5,3},{6,0},{7,1},{8,14},{9,15},{10,... | collective-permute-start | bytes 399368 | tf_op jit(solution)/shard_map/ppermute | solution.py:355
  81.9 3.5 %collective-permute-start.2 = (bf16[512,128]{1,0:T(8,128)(2,1)S(1)}, bf16[512,128]{1,0:T(8,128)(2,1)S(1)}, u32[]{:S(2)}, u32[]{:S(2)}) collective-permute-start(bf16[512,128]{1,0:T(8,128)(2,1)S(1)} %get-tuple-element.17), channel_id=1, source_target_pairs={{0,128},{128,0},{1,129},{129,1},{2,130},{130,2},{3,131},{131,3},{4... | collective-permute-start | bytes 393224 | tf_op jit(solution)/shard_map/ppermute | solution.py:366
  85.9 58.6 %copy-start = (bf16[1,64,128,128]{3,2,1,0:T(8,128)(2,1)S(1)}, bf16[1,64,128,128]{3,2,1,0:T(8,128)(2,1)}, u32[]{:S(2)}) copy-start(bf16[1,64,128,128]{3,2,1,0:T(8,128)(2,1)} %param.7) | copy-start | bytes 6291460
  85.9 58.6 %copy-start.1 = (bf16[36,128,128]{2,1,0:T(8,128)(2,1)S(1)}, bf16[36,128,128]{2,1,0:T(8,128)(2,1)}, u32[]{:S(2)}) copy-start(bf16[36,128,128]{2,1,0:T(8,128)(2,1)} %constant.4.clone.rotations.rots) | copy-start | bytes 3538948
  85.9 58.6 %copy-start.2 = (f32[128,128]{1,0:T(8,128)S(1)}, f32[128,128]{1,0:T(8,128)}, u32[]{:S(2)}) copy-start(f32[128,128]{1,0:T(8,128)} %constant.5.clone.lag_ref) | copy-start | bytes 196612
  86.0 58.6 %copy-start.3 = (s32[1,64]{1,0:T(1,128)S(1)}, s32[1,64]{1,0:T(1,128)}, u32[]{:S(2)}) copy-start(s32[1,64]{1,0:T(1,128)} %classes.1) | copy-start | bytes 772
  86.0 58.6 %copy-start.4 = (s32[1,64]{1,0:T(1,128)S(1)}, s32[1,64]{1,0:T(1,128)}, u32[]{:S(2)}) copy-start(s32[1,64]{1,0:T(1,128)} %turns.1) | copy-start | bytes 772

commit v8 on v7

--- a/solution.py
+++ b/solution.py
@@ -94,8 +94,8 @@
     return jnp.concatenate([column * value[:SHELLS], column * value[SHELLS:]], axis=0)
 
 
-def sums_kernel(assign, rotation, group, table, images, rotations, out, columns, weights_out, *scratch):
-    classes, turns, assign_row, group_row, local, rows, rots, sems = scratch
+def sums_kernel(assign, rotation, group, table, images, rotations, out, spread, weights_out, *scratch):
+    classes, turns, assign_row, group_row, local, rows, rots, columns, sems = scratch
     count = rows.shape[0]
     moves = [
         (images, rows),
@@ -135,8 +135,10 @@
             d, s = slot_of(classes[0, i])
             turned = align(rows[i], turns[0, i], rots)
             at = pl.ds(pl.multiple_of(s * ROWS, ROWS), ROWS)
+            wide = jnp.broadcast_to(weights[:, j : j + 1], (SHELLS, LANES))
+            spread[i] = wide
             held = out[d, at, :].astype(F32)
-            out[d, at, :] = (held + scale_rows(weights[:, j : j + 1], turned)).astype(BF16)
+            out[d, at, :] = (held + scale_rows(wide, turned)).astype(BF16)
         return 0
 
     lax.fori_loop(0, count // BATCH, batch, 0)
@@ -148,7 +150,7 @@
         sums_kernel,
         out_shape=(
             jax.ShapeDtypeStruct((GROUP, BAND, LANES), BF16),
-            jax.ShapeDtypeStruct((count // BATCH, SHELLS, LANES), F32),
+            jax.ShapeDtypeStruct((count, SHELLS, LANES), F32),
             jax.ShapeDtypeStruct((SHELLS, count), F32),
         ),
         in_specs=[HBM] * 6,
@@ -161,6 +163,7 @@
             pltpu.VMEM((SHELLS, groups), F32),
             pltpu.VMEM((count, ROWS, LANES), BF16),
             pltpu.VMEM((NROT, LANES, LANES), BF16),
+            pltpu.VMEM((count // BATCH, SHELLS, LANES), F32),
             pltpu.SemaphoreType.DMA((7,)),
         ],
         compiler_params=pltpu.CompilerParams(vmem_limit_bytes=24 << 20),
@@ -260,7 +263,16 @@
     )(stack, tail)
 
 
-def outputs_kernel(classes, turns, columns, weights_in, rows, rots, bands, lag_ref, resid, score, lever, *scratch):
+def eight_rows(value):
+    return jnp.sum(value.reshape(value.shape[0] // 8, 8, LANES), axis=0)
+
+
+def fold_rows(ref):
+    count = ref.shape[0] // 8
+    return sum(ref[pl.ds(r, count, stride=8), :] for r in range(8))
+
+
+def outputs_kernel(classes, turns, spread, weights_in, rows, rots, bands, lag_ref, resid, score, lever, *scratch):
     held, out_sems, dens, lags, powers, energies = scratch
     count = rows.shape[0]
     by_shell = weights_in[...]
@@ -270,7 +282,6 @@
         return pltpu.make_async_copy(held.at[at], resid.at[at], out_sems.at[b])
 
     def batch(b, _):
-        weights = columns[b]
         for j in range(BATCH):
             i = b * BATCH + j
             d, s = slot_of(classes[0, i])
@@ -278,19 +289,20 @@
             wide = image.astype(F32)
             turned = align(image, turns[0, i], rots)
             avg = bands[d, pl.ds(pl.multiple_of(s * ROWS, ROWS), ROWS), :].astype(F32)
-            predicted = scale_rows(weights[:, j : j + 1], avg).astype(BF16)
+            predicted = scale_rows(spread[i], avg).astype(BF16)
             back = predicted.astype(F32)
             held[i] = (turned - back).astype(BF16)
             cross = lax.dot_general(image, predicted, (((0,), (0,)), ((), ())), preferred_element_type=F32)
             lag = cross[:8]
             for r in range(8, LANES, 8):
                 lag = lag + pltpu.roll(cross[r : r + 8], LANES - r, 1)
-            lags[pl.ds(pl.multiple_of(i * 8, 8), 8), :] = lag
-            powers[pl.ds(i, 1), :] = jnp.sum(wide * wide, axis=0, keepdims=True)
-            energies[pl.ds(i, 1), :] = jnp.sum(back * back, axis=0, keepdims=True)
+            at = pl.ds(pl.multiple_of(i * 8, 8), 8)
+            lags[at, :] = lag
+            powers[at, :] = eight_rows(wide * wide)
+            energies[at, :] = eight_rows(back * back)
             tile = bands[d, STACK * ROWS :, :].astype(F32)
             pick = lax.broadcasted_iota(jnp.int32, tile.shape, 0) == s
-            dens[pl.ds(i, 1), :] = jnp.sum(jnp.where(pick, tile, 0.0), axis=0, keepdims=True)
+            dens[at, :] = jnp.where(pick, tile, 0.0)
         leave(b).start()
         return 0
 
@@ -300,12 +312,12 @@
         shift = shift + pltpu.roll(lags[pl.ds(r, count, stride=8), :], LANES - r, 1)
     raw = contract(lag_ref[...], shift, ((0,), (1,)))
     pixels = ROWS * LANES
-    power = jnp.sum(jnp.transpose(powers[...]), axis=0, keepdims=True)
-    energy = jnp.sum(jnp.transpose(energies[...]), axis=0, keepdims=True)
+    power = jnp.sum(jnp.transpose(fold_rows(powers)), axis=0, keepdims=True)
+    energy = jnp.sum(jnp.transpose(fold_rows(energies)), axis=0, keepdims=True)
     first = jnp.sqrt(power / pixels + 1e-05)
     second = jnp.sqrt(energy / pixels + 1e-05)
     score[...] = (raw / (math.sqrt(pixels) * first * second))[:NROT].astype(BF16)
-    den = jnp.transpose(join_pair(dens[...]))
+    den = jnp.transpose(join_pair(fold_rows(dens)))
     lever[...] = (jnp.sum(by_shell * by_shell / (den + TAU), axis=0, keepdims=True) / SHELLS).astype(BF16)
 
     def finish(b, _):
@@ -315,9 +327,9 @@
     lax.fori_loop(0, count // BATCH, finish, 0)
 
 
-def particle_outputs(assign, rotation, columns, weights, images, rotations, bands):
+def particle_outputs(assign, rotation, spread, weights, images, rotations, bands):
     count = images.shape[0]
-    per_particle = pltpu.VMEM((count, LANES), F32)
+    per_particle = pltpu.VMEM((count * 8, LANES), F32)
     return pl.pallas_call(
         outputs_kernel,
         out_shape=(
@@ -331,13 +343,13 @@
             pltpu.VMEM((count, ROWS, LANES), BF16),
             pltpu.SemaphoreType.DMA((count // BATCH,)),
             per_particle,
-            pltpu.VMEM((count * 8, LANES), F32),
+            per_particle,
             per_particle,
             per_particle,
         ],
         compiler_params=pltpu.CompilerParams(vmem_limit_bytes=24 << 20),
         name="particle_outputs",
-    )(assign, rotation, columns, weights, images, rotations, bands, jnp.asarray(lag_matrix()))
+    )(assign, rotation, spread, weights, images, rotations, bands, jnp.asarray(lag_matrix()))
 
 
 def exchange(value):
@@ -359,13 +371,13 @@
     images, rotations = particles[0], jnp.asarray(rotation_matrices())
     operands = (assign, rotation, group, ctf.T, images, rotations)
     pinned = [pltpu.with_memory_space_constraint(x, pltpu.HBM) for x in operands]
-    bands, columns, weights = class_sums(*pinned)
+    bands, spread, weights = class_sums(*pinned)
     band = group_sums(exchange(bands))
     band = pair_sums(band, swap_along_z(band, 0))
     stack, average, tail = class_averages(band, swap_along_z(band, 1))
     stack = lax.ppermute(stack, "half", [(0, 1), (1, 0)])
     bands = exchange(group_copies(stack, tail))
-    residual, scores, leverage = particle_outputs(assign, rotation, columns, weights, images, rotations, bands)
+    residual, scores, leverage = particle_outputs(assign, rotation, spread, weights, images, rotations, bands)
     return (average[None, None], residual[None], scores.T[None], leverage)
 
 

time: 151 us -> 150 us (level)
  no operation moved by 1% of the time
where the time goes in v8:
time: 150 us
  blocking collectives  119 us (79%)
  waiting for transfers between devices  11.8 us (8%)
  Pallas kernels  11.7 us (8%)
  starting transfers between devices  6.75 us (4%)
    all_to_all x2, blocking collectives, exchange(): lax.all_to_all(value, 'cls', split_axis=0, concat_axis=0, tiled=True, axi...  119 us
    ppermute x2, waiting for transfers between devices, swap_along_z(): return lax.ppermute(value, 'cls', [(i, partner(i)) for i in range(CLASSES)])  10.8 us
    pallas_call x1, Pallas kernels, particle_outputs(): pl.pallas_call(outputs_kernel, out_shape=(jax.ShapeDtypeStruct(images.sha...  5.08 us
    pallas_call x1, Pallas kernels, class_sums(): pl.pallas_call(sums_kernel, out_shape=(jax.ShapeDtypeStruct((GROUP, BAND,...  4.47 us
    ppermute x2, starting transfers between devices, swap_along_z(): return lax.ppermute(value, 'cls', [(i, partner(i)) for i in range(CLASSES)])  4.23 us
  transfers between devices with their start and end apart: 3, of which 3 were waited for; matrix products, arithmetic and copies ran while one was open for 0% of the time, Pallas kernels for 0%

profile of v8, /device:TPU:1, one launch (start us, length us, event | category | flops | bytes accessed | tf_op | source)
XLA Modules:
  0.0 149.6 jit_solution(5090923611318028589)
XLA Ops:
  0.6 4.5 %class_sums.1 = (bf16[32,520,128]{2,1,0:T(8,128)(2,1)S(1)}, f32[64,64,128]{2,1,0:T(8,128)S(1)}, f32[64,64]{1,0:T(8,128)S(1)}) custom-call(s32[1,64]{1,0:T(1,128)} %classes.1, s32[1,64]{1,0:T(1,128)} %turns.1, s32[1,64]{1,0:T(1,128)} %group.1, f32[64,256]{1,0:T(8,128)} %bitcast.9, bf16[64,128,128]{2,1,0:T(8,128)(2,1)} %bitcast.7, ...), custom_call_target="tpu_custom_call" | custom-call | tf_op jit(solution)/shard_map/class_sums/pallas_call | solution.py:149
  5.1 60.1 %all_to_all.10.bands = bf16[32,520,128]{2,1,0:T(8,128)(2,1)S(1)} all-to-all(bf16[32,520,128]{2,1,0:T(8,128)(2,1)S(1)} %get-tuple-element.13), channel_id=1, replica_groups={{0,8,16,24,32,40,48,56,64,72,80,88,96,104,112,120,1,9,17,25,33,41,49,57..., dimensions={0} | all-to-all | bytes 8519680 | tf_op jit(solution)/shard_map/all_to_all | solution.py:358
  65.2 0.6 group_sums.1.mine
  65.8 3.1 %collective-permute-start = (bf16[520,128]{1,0:T(8,128)(2,1)S(1)}, bf16[520,128]{1,0:T(8,128)(2,1)S(1)}, u32[]{:S(2)}, u32[]{:S(2)}) collective-permute-start(bf16[520,128]{1,0:T(8,128)(2,1)S(1)} %group_sums.1.mine), channel_id=1, source_target_pairs={{0,2},{1,3},{2,0},{3,1},{4,6},{5,7},{6,4},{7,5},{8,10},{9,11},{10,... | collective-permute-start | bytes 399368 | tf_op jit(solution)/shard_map/ppermute | solution.py:367
  68.8 5.9 %collective-permute-done.theirs = bf16[520,128]{1,0:T(8,128)(2,1)S(1)} collective-permute-done((bf16[520,128]{1,0:T(8,128)(2,1)S(1)}, bf16[520,128]{1,0:T(8,128)(2,1)S(1)}, u32[]{:S(2)}, u32[]{:S(2)}) %collective-permute-start) | collective-permute-done | bytes 133152 | tf_op jit(solution)/shard_map/ppermute | solution.py:367
  74.7 0.1 pair_sums.1.mine
  74.9 1.1 collective-permute-start.1
  76.0 5.0 %collective-permute-done.1.theirs = bf16[520,128]{1,0:T(8,128)(2,1)S(1)} collective-permute-done((bf16[520,128]{1,0:T(8,128)(2,1)S(1)}, bf16[520,128]{1,0:T(8,128)(2,1)S(1)}, u32[]{:S(2)}, u32[]{:S(2)}) %collective-permute-start.1) | collective-permute-done | bytes 133152 | tf_op jit(solution)/shard_map/ppermute | solution.py:367
  81.0 0.9 class_averages.1
  81.9 2.5 %collective-permute-start.2 = (bf16[512,128]{1,0:T(8,128)(2,1)S(1)}, bf16[512,128]{1,0:T(8,128)(2,1)S(1)}, u32[]{:S(2)}, u32[]{:S(2)}) collective-permute-start(bf16[512,128]{1,0:T(8,128)(2,1)S(1)} %get-tuple-element.17), channel_id=1, source_target_pairs={{0,128},{128,0},{1,129},{129,1},{2,130},{130,2},{3,131},{131,3},{4... | collective-permute-start | bytes 393224 | tf_op jit(solution)/shard_map/ppermute | solution.py:378
  84.4 1.0 collective-permute-done.2.stack
  85.4 0.5 group_copies.1
  85.9 0.0 copy-start
  85.9 0.0 copy-start.1
  86.0 0.0 copy-start.2
  86.0 0.0 copy-start.3
  86.0 0.0 copy-start.4
  86.0 58.5 %all_to_all.11.bands = bf16[32,520,128]{2,1,0:T(8,128)(2,1)S(1)} all-to-all(bf16[32,520,128]{2,1,0:T(8,128)(2,1)S(1)} %group_copies.1), channel_id=1, replica_groups={{0,8,16,24,32,40,48,56,64,72,80,88,96,104,112,120,1,9,17,25,33,41,49,57..., dimensions={0} | all-to-all | bytes 8519680 | tf_op jit(solution)/shard_map/all_to_all | solution.py:358
  144.5 0.0 copy-done
  144.5 0.0 copy-done.1
  144.5 0.0 copy-done.2
  144.5 0.0 copy-done.3
  144.5 0.0 copy-done.4
  144.6 5.1 %particle_outputs.1 = (bf16[64,128,128]{2,1,0:T(8,128)(2,1)}, bf16[36,64]{1,0:T(8,128)(2,1)}, bf16[1,64]{1,0:T(2,128)(2,1)}) custom-call(s32[1,64]{1,0:T(1,128)S(1)} %copy-done.3, s32[1,64]{1,0:T(1,128)S(1)} %copy-done.4, f32[64,64,128]{2,1,0:T(8,128)S(1)} %get-tuple-element.15.spread, f32[64,64]{1,0:T(8,128)S(1)} %get-tuple-element.16.weights_in, ...), custom_call_target="tpu_custom_call" | custom-call | tf_op jit(solution)/shard_map/particle_outputs/pallas_call | solution.py:333
Async XLA Ops:
  65.8 9.0 %collective-permute-start = (bf16[520,128]{1,0:T(8,128)(2,1)S(1)}, bf16[520,128]{1,0:T(8,128)(2,1)S(1)}, u32[]{:S(2)}, u32[]{:S(2)}) collective-permute-start(bf16[520,128]{1,0:T(8,128)(2,1)S(1)} %group_sums.1.mine), channel_id=1, source_target_pairs={{0,2},{1,3},{2,0},{3,1},{4,6},{5,7},{6,4},{7,5},{8,10},{9,11},{10,... | collective-permute-start | bytes 399368 | tf_op jit(solution)/shard_map/ppermute | solution.py:367
  74.9 6.1 %collective-permute-start.1 = (bf16[520,128]{1,0:T(8,128)(2,1)S(1)}, bf16[520,128]{1,0:T(8,128)(2,1)S(1)}, u32[]{:S(2)}, u32[]{:S(2)}) collective-permute-start(bf16[520,128]{1,0:T(8,128)(2,1)S(1)} %pair_sums.1.mine), channel_id=1, source_target_pairs={{0,6},{1,7},{2,4},{3,5},{4,2},{5,3},{6,0},{7,1},{8,14},{9,15},{10,... | collective-permute-start | bytes 399368 | tf_op jit(solution)/shard_map/ppermute | solution.py:367
  81.9 3.5 %collective-permute-start.2 = (bf16[512,128]{1,0:T(8,128)(2,1)S(1)}, bf16[512,128]{1,0:T(8,128)(2,1)S(1)}, u32[]{:S(2)}, u32[]{:S(2)}) collective-permute-start(bf16[512,128]{1,0:T(8,128)(2,1)S(1)} %get-tuple-element.17), channel_id=1, source_target_pairs={{0,128},{128,0},{1,129},{129,1},{2,130},{130,2},{3,131},{131,3},{4... | collective-permute-start | bytes 393224 | tf_op jit(solution)/shard_map/ppermute | solution.py:378
  85.9 58.6 %copy-start = (bf16[1,64,128,128]{3,2,1,0:T(8,128)(2,1)S(1)}, bf16[1,64,128,128]{3,2,1,0:T(8,128)(2,1)}, u32[]{:S(2)}) copy-start(bf16[1,64,128,128]{3,2,1,0:T(8,128)(2,1)} %param.7) | copy-start | bytes 6291460
  85.9 58.6 %copy-start.1 = (bf16[36,128,128]{2,1,0:T(8,128)(2,1)S(1)}, bf16[36,128,128]{2,1,0:T(8,128)(2,1)}, u32[]{:S(2)}) copy-start(bf16[36,128,128]{2,1,0:T(8,128)(2,1)} %constant.4.clone.rotations.rots) | copy-start | bytes 3538948
  86.0 58.6 %copy-start.2 = (f32[128,128]{1,0:T(8,128)S(1)}, f32[128,128]{1,0:T(8,128)}, u32[]{:S(2)}) copy-start(f32[128,128]{1,0:T(8,128)} %constant.5.clone.lag_ref) | copy-start | bytes 196612
  86.0 58.6 %copy-start.3 = (s32[1,64]{1,0:T(1,128)S(1)}, s32[1,64]{1,0:T(1,128)}, u32[]{:S(2)}) copy-start(s32[1,64]{1,0:T(1,128)} %classes.1) | copy-start | bytes 772
  86.0 58.6 %copy-start.4 = (s32[1,64]{1,0:T(1,128)S(1)}, s32[1,64]{1,0:T(1,128)}, u32[]{:S(2)}) copy-start(s32[1,64]{1,0:T(1,128)} %turns.1) | copy-start | bytes 772

commit v9 on v8

--- a/solution.py
+++ b/solution.py
@@ -373,8 +373,8 @@
     pinned = [pltpu.with_memory_space_constraint(x, pltpu.HBM) for x in operands]
     bands, spread, weights = class_sums(*pinned)
     band = group_sums(exchange(bands))
-    band = pair_sums(band, swap_along_z(band, 0))
-    stack, average, tail = class_averages(band, swap_along_z(band, 1))
+    band = pair_sums(band, swap_along_z(band, 1))
+    stack, average, tail = class_averages(band, swap_along_z(band, 0))
     stack = lax.ppermute(stack, "half", [(0, 1), (1, 0)])
     bands = exchange(group_copies(stack, tail))
     residual, scores, leverage = particle_outputs(assign, rotation, spread, weights, images, rotations, bands)

time: 150 us -> 149 us (level)
  starting transfers between devices: 6.75 us -> 14.1 us
  waiting for transfers between devices: 11.8 us -> 6.73 us
  blocking collectives: 119 us -> 116 us
    ppermute x2, waiting for transfers between devices: 10.8 us -> 5.74 us  [swap_along_z(): return lax.ppermute(value, 'cls', [(i, partner(i)) for i in range(CLASSES)])]
    ppermute x2, starting transfers between devices: 4.23 us -> 8.97 us  [swap_along_z(): return lax.ppermute(value, 'cls', [(i, partner(i)) for i in range(CLASSES)])]
    all_to_all x2, blocking collectives: 119 us -> 116 us  [exchange(): lax.all_to_all(value, 'cls', split_axis=0, concat_axis=0, tiled=True, axi...]
    ppermute x1, starting transfers between devices: 2.53 us -> 5.17 us  [body(): stack = lax.ppermute(stack, 'half', [(0, 1), (1, 0)])]
where the time goes in v9:
time: 149 us
  blocking collectives  116 us (78%)
  starting transfers between devices  14.1 us (9%)
  Pallas kernels  11.7 us (8%)
  waiting for transfers between devices  6.73 us (5%)
    all_to_all x2, blocking collectives, exchange(): lax.all_to_all(value, 'cls', split_axis=0, concat_axis=0, tiled=True, axi...  116 us
    ppermute x2, starting transfers between devices, swap_along_z(): return lax.ppermute(value, 'cls', [(i, partner(i)) for i in range(CLASSES)])  8.97 us
    ppermute x2, waiting for transfers between devices, swap_along_z(): return lax.ppermute(value, 'cls', [(i, partner(i)) for i in range(CLASSES)])  5.74 us
    ppermute x1, starting transfers between devices, body(): stack = lax.ppermute(stack, 'half', [(0, 1), (1, 0)])  5.17 us
    pallas_call x1, Pallas kernels, particle_outputs(): pl.pallas_call(outputs_kernel, out_shape=(jax.ShapeDtypeStruct(images.sha...  5.08 us
    pallas_call x1, Pallas kernels, class_sums(): pl.pallas_call(sums_kernel, out_shape=(jax.ShapeDtypeStruct((GROUP, BAND,...  4.47 us
  transfers between devices with their start and end apart: 3, of which 3 were waited for; matrix products, arithmetic and copies ran while one was open for 0% of the time, Pallas kernels for 0%

profile of v9, /device:TPU:1, one launch (start us, length us, event | category | flops | bytes accessed | tf_op | source)
XLA Modules:
  0.0 148.9 jit_solution(3102878115168721961)
XLA Ops:
  0.6 4.5 %class_sums.1 = (bf16[32,520,128]{2,1,0:T(8,128)(2,1)S(1)}, f32[64,64,128]{2,1,0:T(8,128)S(1)}, f32[64,64]{1,0:T(8,128)S(1)}) custom-call(s32[1,64]{1,0:T(1,128)} %classes.1, s32[1,64]{1,0:T(1,128)} %turns.1, s32[1,64]{1,0:T(1,128)} %group.1, f32[64,256]{1,0:T(8,128)} %bitcast.9, bf16[64,128,128]{2,1,0:T(8,128)(2,1)} %bitcast.7, ...), custom_call_target="tpu_custom_call" | custom-call | tf_op jit(solution)/shard_map/class_sums/pallas_call | solution.py:149
  5.1 60.1 %all_to_all.10.bands = bf16[32,520,128]{2,1,0:T(8,128)(2,1)S(1)} all-to-all(bf16[32,520,128]{2,1,0:T(8,128)(2,1)S(1)} %get-tuple-element.13), channel_id=1, replica_groups={{0,8,16,24,32,40,48,56,64,72,80,88,96,104,112,120,1,9,17,25,33,41,49,57..., dimensions={0} | all-to-all | bytes 8519680 | tf_op jit(solution)/shard_map/all_to_all | solution.py:358
  65.2 0.6 group_sums.1.mine
  65.8 5.2 %collective-permute-start = (bf16[520,128]{1,0:T(8,128)(2,1)S(1)}, bf16[520,128]{1,0:T(8,128)(2,1)S(1)}, u32[]{:S(2)}, u32[]{:S(2)}) collective-permute-start(bf16[520,128]{1,0:T(8,128)(2,1)S(1)} %group_sums.1.mine), channel_id=1, source_target_pairs={{0,6},{1,7},{2,4},{3,5},{4,2},{5,3},{6,0},{7,1},{8,14},{9,15},{10,... | collective-permute-start | bytes 399368 | tf_op jit(solution)/shard_map/ppermute | solution.py:367
  71.0 3.4 %collective-permute-done.theirs = bf16[520,128]{1,0:T(8,128)(2,1)S(1)} collective-permute-done((bf16[520,128]{1,0:T(8,128)(2,1)S(1)}, bf16[520,128]{1,0:T(8,128)(2,1)S(1)}, u32[]{:S(2)}, u32[]{:S(2)}) %collective-permute-start) | collective-permute-done | bytes 133152 | tf_op jit(solution)/shard_map/ppermute | solution.py:367
  74.3 0.1 pair_sums.1.mine
  74.5 3.8 %collective-permute-start.1 = (bf16[520,128]{1,0:T(8,128)(2,1)S(1)}, bf16[520,128]{1,0:T(8,128)(2,1)S(1)}, u32[]{:S(2)}, u32[]{:S(2)}) collective-permute-start(bf16[520,128]{1,0:T(8,128)(2,1)S(1)} %pair_sums.1.mine), channel_id=1, source_target_pairs={{0,2},{1,3},{2,0},{3,1},{4,6},{5,7},{6,4},{7,5},{8,10},{9,11},{10,... | collective-permute-start | bytes 399368 | tf_op jit(solution)/shard_map/ppermute | solution.py:367
  78.2 2.4 %collective-permute-done.1.theirs = bf16[520,128]{1,0:T(8,128)(2,1)S(1)} collective-permute-done((bf16[520,128]{1,0:T(8,128)(2,1)S(1)}, bf16[520,128]{1,0:T(8,128)(2,1)S(1)}, u32[]{:S(2)}, u32[]{:S(2)}) %collective-permute-start.1) | collective-permute-done | bytes 133152 | tf_op jit(solution)/shard_map/ppermute | solution.py:367
  80.6 0.9 class_averages.1
  81.5 5.2 %collective-permute-start.2 = (bf16[512,128]{1,0:T(8,128)(2,1)S(1)}, bf16[512,128]{1,0:T(8,128)(2,1)S(1)}, u32[]{:S(2)}, u32[]{:S(2)}) collective-permute-start(bf16[512,128]{1,0:T(8,128)(2,1)S(1)} %get-tuple-element.17), channel_id=1, source_target_pairs={{0,128},{128,0},{1,129},{129,1},{2,130},{130,2},{3,131},{131,3},{4... | collective-permute-start | bytes 393224 | tf_op jit(solution)/shard_map/ppermute | solution.py:378
  86.7 1.0 collective-permute-done.2.stack
  87.7 0.5 group_copies.1
  88.2 0.0 copy-start
  88.2 0.0 copy-start.1
  88.3 0.0 copy-start.2
  88.3 0.0 copy-start.3
  88.3 0.0 copy-start.4
  88.3 55.5 %all_to_all.11.bands = bf16[32,520,128]{2,1,0:T(8,128)(2,1)S(1)} all-to-all(bf16[32,520,128]{2,1,0:T(8,128)(2,1)S(1)} %group_copies.1), channel_id=1, replica_groups={{0,8,16,24,32,40,48,56,64,72,80,88,96,104,112,120,1,9,17,25,33,41,49,57..., dimensions={0} | all-to-all | bytes 8519680 | tf_op jit(solution)/shard_map/all_to_all | solution.py:358
  143.8 0.0 copy-done
  143.8 0.0 copy-done.1
  143.8 0.0 copy-done.2
  143.8 0.0 copy-done.3
  143.8 0.0 copy-done.4
  143.8 5.1 %particle_outputs.1 = (bf16[64,128,128]{2,1,0:T(8,128)(2,1)}, bf16[36,64]{1,0:T(8,128)(2,1)}, bf16[1,64]{1,0:T(2,128)(2,1)}) custom-call(s32[1,64]{1,0:T(1,128)S(1)} %copy-done.3, s32[1,64]{1,0:T(1,128)S(1)} %copy-done.4, f32[64,64,128]{2,1,0:T(8,128)S(1)} %get-tuple-element.15.spread, f32[64,64]{1,0:T(8,128)S(1)} %get-tuple-element.16.weights_in, ...), custom_call_target="tpu_custom_call" | custom-call | tf_op jit(solution)/shard_map/particle_outputs/pallas_call | solution.py:333
Async XLA Ops:
  65.8 8.6 %collective-permute-start = (bf16[520,128]{1,0:T(8,128)(2,1)S(1)}, bf16[520,128]{1,0:T(8,128)(2,1)S(1)}, u32[]{:S(2)}, u32[]{:S(2)}) collective-permute-start(bf16[520,128]{1,0:T(8,128)(2,1)S(1)} %group_sums.1.mine), channel_id=1, source_target_pairs={{0,6},{1,7},{2,4},{3,5},{4,2},{5,3},{6,0},{7,1},{8,14},{9,15},{10,... | collective-permute-start | bytes 399368 | tf_op jit(solution)/shard_map/ppermute | solution.py:367
  74.5 6.1 %collective-permute-start.1 = (bf16[520,128]{1,0:T(8,128)(2,1)S(1)}, bf16[520,128]{1,0:T(8,128)(2,1)S(1)}, u32[]{:S(2)}, u32[]{:S(2)}) collective-permute-start(bf16[520,128]{1,0:T(8,128)(2,1)S(1)} %pair_sums.1.mine), channel_id=1, source_target_pairs={{0,2},{1,3},{2,0},{3,1},{4,6},{5,7},{6,4},{7,5},{8,10},{9,11},{10,... | collective-permute-start | bytes 399368 | tf_op jit(solution)/shard_map/ppermute | solution.py:367
  81.5 6.2 %collective-permute-start.2 = (bf16[512,128]{1,0:T(8,128)(2,1)S(1)}, bf16[512,128]{1,0:T(8,128)(2,1)S(1)}, u32[]{:S(2)}, u32[]{:S(2)}) collective-permute-start(bf16[512,128]{1,0:T(8,128)(2,1)S(1)} %get-tuple-element.17), channel_id=1, source_target_pairs={{0,128},{128,0},{1,129},{129,1},{2,130},{130,2},{3,131},{131,3},{4... | collective-permute-start | bytes 393224 | tf_op jit(solution)/shard_map/ppermute | solution.py:378
  88.2 55.5 %copy-start = (bf16[1,64,128,128]{3,2,1,0:T(8,128)(2,1)S(1)}, bf16[1,64,128,128]{3,2,1,0:T(8,128)(2,1)}, u32[]{:S(2)}) copy-start(bf16[1,64,128,128]{3,2,1,0:T(8,128)(2,1)} %param.7) | copy-start | bytes 6291460
  88.2 55.5 %copy-start.1 = (bf16[36,128,128]{2,1,0:T(8,128)(2,1)S(1)}, bf16[36,128,128]{2,1,0:T(8,128)(2,1)}, u32[]{:S(2)}) copy-start(bf16[36,128,128]{2,1,0:T(8,128)(2,1)} %constant.4.clone.rotations.rots) | copy-start | bytes 3538948
  88.3 55.5 %copy-start.2 = (f32[128,128]{1,0:T(8,128)S(1)}, f32[128,128]{1,0:T(8,128)}, u32[]{:S(2)}) copy-start(f32[128,128]{1,0:T(8,128)} %constant.5.clone.lag_ref) | copy-start | bytes 196612
  88.3 55.5 %copy-start.3 = (s32[1,64]{1,0:T(1,128)S(1)}, s32[1,64]{1,0:T(1,128)}, u32[]{:S(2)}) copy-start(s32[1,64]{1,0:T(1,128)} %classes.1) | copy-start | bytes 772
  88.3 55.5 %copy-start.4 = (s32[1,64]{1,0:T(1,128)S(1)}, s32[1,64]{1,0:T(1,128)}, u32[]{:S(2)}) copy-start(s32[1,64]{1,0:T(1,128)} %turns.1) | copy-start | bytes 772
